TPU v7x, 256 devices: a whole 4x4x8 slice. The times are simulated.
256 devices in a mesh: pop: 32 (over x, y, core), site: 8 (over z).
Axes of the slice: x: 4, y: 4, z: 8, core: 2. Of those that a mesh axis runs over, the one named last changes fastest.
Arguments:
- profile: bfloat16 [32768, 96], P(('pop', 'site')), may hold values from 0 to 1
- panel: bfloat16 [32768, 128], P(('pop', 'site')), may hold values from -6 to 6
- visit_person: int32 [131072], P(('pop', 'site')), may hold values from 0 to 127
- visit_owner: int32 [131072], P(('pop', 'site')), may hold values from 0 to 31, as said below
- visit_row: int32 [131072], P(('pop', 'site')), may hold values from 0 to 1023, as said below
- visit_start: int32 [131072], P(('pop', 'site')), may hold values from 0 to 95
- visit_length: int32 [131072], P(('pop', 'site')), may hold values from 2 to 48
- tile_loc: int32 [2048], P(('pop', 'site')), may hold values from 0 to 7
Outputs:
- exposure: bfloat16 [32768, 128], P(('pop', 'site'))
Inputs may be any that keep to these rules, and one draw needn't show every extreme that they name: `visit_owner`: all devices with one site index send the same number of visits to a given owner index; at most 24 visits of one device go to one owner index, and in every draw some owner index receives exactly 24 from every device of a site index. `visit_row`: among the visits that reach one owner device the rows are distinct; in each tile the rows that are used come first and the rest are empty.
All inputs are finite; a program needn't handle non-finite values.
Results may differ from a plain program's by a relative error of at most 0.013.
Values may be sent and summed in bfloat16 or wider, within the bound.
No kernel may reach another device: no remote copies, remote signals or barrier semaphores. Data moves between devices by JAX's collectives and lax.ppermute only.
A program may use at most 64 MiB of HBM per device.

v0:
```python
import math

import jax
import jax.numpy as jnp
from jax import lax
from jax.sharding import PartitionSpec as P


def pair_terms(own_weights, own_places, running, pieces):
    far_weights, far_panel, far_places = pieces
    piece_tiles = far_weights.shape[0]
    group_size = math.gcd(piece_tiles, 8)
    group_count = piece_tiles // group_size
    grouped = (
        far_weights.reshape((group_count, group_size) + far_weights.shape[1:]),
        far_panel.reshape((group_count, group_size) + far_panel.shape[1:]),
        far_places.reshape(group_count, group_size),
    )

    def one_group(carried, item):
        group_weights, group_panel, group_places = item
        same_place = (own_places[:, None] == group_places[None, :]).astype(jnp.bfloat16)
        masked_far = group_weights[None, :, :, :] * same_place[:, :, None, None]
        copresence = jnp.einsum(
            "ars,abqs->abrq", own_weights, masked_far, preferred_element_type=jnp.float32
        )
        high_part = copresence.astype(jnp.bfloat16)
        low_part = (copresence - high_part.astype(jnp.float32)).astype(jnp.bfloat16)
        added = jnp.einsum(
            "abrq,bqc->arc", high_part, group_panel, preferred_element_type=jnp.float32
        )
        added = added + jnp.einsum(
            "abrq,bqc->arc", low_part, group_panel, preferred_element_type=jnp.float32
        )
        return (carried + added, None)

    result_sum, unused = lax.scan(one_group, running, grouped)
    return result_sum


def per_device(
    profile, panel, visit_person, visit_owner, visit_row, visit_start, visit_length, tile_loc
):
    pop_count = lax.axis_size("pop")
    visit_count = visit_person.shape[0]
    person_count, slot_count = profile.shape
    panel_width = panel.shape[1]
    capacity = visit_count // pop_count * 3 // 2
    tile_count = tile_loc.shape[0]
    row_count = tile_count * 128
    slot_ids = jnp.arange(slot_count, dtype=jnp.int32)
    finish = jnp.minimum(visit_start + visit_length, slot_count)
    inside = (slot_ids[None, :] >= visit_start[:, None]) & (slot_ids[None, :] < finish[:, None])
    weights = jnp.where(inside, profile[visit_person], jnp.zeros((), jnp.bfloat16))
    visit_panel = panel[visit_person]
    owner_hot = (visit_owner[:, None] == jnp.arange(pop_count, dtype=jnp.int32)[None, :]).astype(
        jnp.int32
    )
    position = jnp.sum((jnp.cumsum(owner_hot, axis=0) - 1) * owner_hot, axis=1)
    send_index = visit_owner * capacity + position
    send_weights = (
        jnp.zeros((pop_count * capacity, slot_count), jnp.bfloat16)
        .at[send_index]
        .set(weights)
        .reshape(pop_count, capacity, slot_count)
    )
    send_panel = (
        jnp.zeros((pop_count * capacity, panel_width), jnp.bfloat16)
        .at[send_index]
        .set(visit_panel)
        .reshape(pop_count, capacity, panel_width)
    )
    send_rows = (
        jnp.full((pop_count * capacity,), row_count, jnp.int32)
        .at[send_index]
        .set(visit_row)
        .reshape(pop_count, capacity)
    )
    got_weights, got_panel, got_rows = (
        lax.all_to_all(send_weights, "pop", split_axis=0, concat_axis=0, tiled=True),
        lax.all_to_all(send_panel, "pop", split_axis=0, concat_axis=0, tiled=True),
        lax.all_to_all(send_rows, "pop", split_axis=0, concat_axis=0, tiled=True),
    )
    target = got_rows.reshape(-1)
    tile_weights = (
        jnp.zeros((row_count, slot_count), jnp.bfloat16)
        .at[target]
        .set(got_weights.reshape(-1, slot_count), mode="drop")
        .reshape(tile_count, 128, slot_count)
    )
    tile_panel = (
        jnp.zeros((row_count, panel_width), jnp.bfloat16)
        .at[target]
        .set(got_panel.reshape(-1, panel_width), mode="drop")
        .reshape(tile_count, 128, panel_width)
    )
    initial = jnp.zeros((tile_count, 128, panel_width), jnp.float32)
    summed_rows = pair_terms(
        tile_weights,
        tile_loc,
        initial,
        (
            lax.all_gather(tile_weights, "site", axis=0, tiled=True),
            lax.all_gather(tile_panel, "site", axis=0, tiled=True),
            lax.all_gather(tile_loc, "site", axis=0, tiled=True),
        ),
    )
    row_result = (summed_rows / slot_count).astype(jnp.bfloat16).reshape(row_count, panel_width)
    sent_back = row_result[jnp.minimum(got_rows, row_count - 1)]
    returned = lax.all_to_all(sent_back, "pop", split_axis=0, concat_axis=0, tiled=True)
    own_results = returned.reshape(pop_count * capacity, panel_width)[send_index]
    person_hot = (
        jnp.arange(person_count, dtype=jnp.int32)[:, None] == visit_person[None, :]
    ).astype(jnp.bfloat16)
    return jnp.dot(person_hot, own_results, preferred_element_type=jnp.float32).astype(jnp.bfloat16)


def solution(mesh):
    placed = (
        P(("pop", "site"), None),
        P(("pop", "site"), None),
        P(("pop", "site")),
        P(("pop", "site")),
        P(("pop", "site")),
        P(("pop", "site")),
        P(("pop", "site")),
        P(("pop", "site")),
    )
    return jax.shard_map(
        per_device, mesh=mesh, in_specs=placed, out_specs=P(("pop", "site"), None), check_vma=False
    )
```

profile of v0, /device:TPU:1, one launch (start us, length us, event | category | flops | bytes accessed | tf_op | source)
XLA Modules:
  0.0 205.3 jit_solution(10561987336551839992)
XLA Ops:
  10.2 2.6 %scatter_custom_fusion = s32[768]{0:T(1024)S(1)} fusion(s32[512]{0:T(512)S(1)} %get-tuple-element.104, s32[512]{0:T(512)} %param.14, s32[]{:T(128)} %constant.8.clone.1), kind=kCustom, calls=%fused_computation.71 | custom fusion | bytes 3584 | tf_op jit(solution)/shard_map/scatter | solution.py:76
  13.5 8.6 %all-to-all-start = ((s32[32,1,24]{2,1,0:T(1,128)}), s32[32,1,24]{2,1,0:T(1,128)S(1)}, u32[]{:S(2)}, u32[]{:S(2)}) async-start(s32[32,1,24]{2,1,0:T(1,128)} %bitcast.2), calls=%async_computation | async-start | bytes 32768 | tf_op jit(solution)/shard_map/all_to_all | solution.py:82
  23.6 3.9 %scatter_custom_fusion.1 = bf16[768,96]{1,0:T(8,128)(2,1)} fusion(s32[512]{0:T(512)S(1)} %get-tuple-element.104, s32[512]{0:T(512)S(1)} %get-tuple-element.105, s32[512]{0:T(512)} %param.15, bf16[]{:T(256)} %constant.19.clone.1, bf16[128,96]{1,0:T(8,128)(2,1)S(1)} %copy.29, s32[1024]{0:T(1024)S(1)} %pad_clamp_fusion.2), kind=kCustom, calls=%fused_computation.40 | custom fusion | flops 196608 | bytes 189440 | tf_op jit(solution)/shard_map/scatter | solution.py:64
  28.9 6.0 %all-to-all-start.1 = ((bf16[32,24,96]{2,1,0:T(8,128)(2,1)}), bf16[32,24,96]{2,1,0:T(8,128)(2,1)S(1)}, u32[]{:S(2)}, u32[]{:S(2)}) async-start(bf16[32,24,96]{2,1,0:T(8,128)(2,1)} %bitcast.3), calls=%async_computation.1 | async-start | bytes 393216 | tf_op jit(solution)/shard_map/all_to_all | solution.py:80
  36.3 7.0 %all-to-all-done.1 = bf16[32,24,96]{2,1,0:T(8,128)(2,1)S(1)} async-done(((bf16[32,24,96]{2,1,0:T(8,128)(2,1)}), bf16[32,24,96]{2,1,0:T(8,128)(2,1)S(1)}, u32[]{:S(2)}, u32[]{:S(2)}) %all-to-all-start.1) | async-done | bytes 147488 | tf_op jit(solution)/shard_map/all_to_all | solution.py:80
  43.2 4.3 %scatter_custom_fusion.2 = bf16[1024,96]{1,0:T(8,128)(2,1)S(1)} fusion(s32[768]{0:T(1024)S(1)} %fusion.39, bf16[768,96]{1,0:T(8,128)(2,1)S(1)} %bitcast.114, bf16[]{:T(256)} %constant.19.clone.1), kind=kCustom, calls=%fused_computation.47 | custom fusion | bytes 196610 | tf_op jit(solution)/shard_map/scatter | solution.py:88
  48.5 3.0 %scatter_custom_fusion.3 = bf16[768,128]{1,0:T(8,128)(2,1)S(1)} fusion(s32[512]{0:T(512)S(1)} %get-tuple-element.104, bf16[128,128]{1,0:T(8,128)(2,1)S(1)} %copy-done, s32[1024]{0:T(1024)S(1)} %pad_clamp_fusion.2, bf16[]{:T(256)} %constant.19.clone.1), kind=kCustom, calls=%fused_computation.41 | custom fusion | bytes 196610 | tf_op jit(solution)/shard_map/scatter | solution.py:70
  51.5 11.9 %all_to_all.24 = bf16[32,24,128]{2,1,0:T(8,128)(2,1)S(1)} all-to-all(bf16[32,24,128]{2,1,0:T(8,128)(2,1)S(1)} %bitcast.112), channel_id=1, replica_groups=mesh['pop'=32,'site'=8] {'pop'}, dimensions={0} | all-to-all | bytes 393216 | tf_op jit(solution)/shard_map/all_to_all | solution.py:81
  63.4 4.9 %scatter_custom_fusion.4 = bf16[1024,128]{1,0:T(8,128)(2,1)} fusion(s32[768]{0:T(1024)S(1)} %fusion.39, bf16[768,128]{1,0:T(8,128)(2,1)S(1)} %bitcast.115, bf16[]{:T(256)} %constant.19.clone.1), kind=kCustom, calls=%fused_computation.43 | custom fusion | bytes 262146 | tf_op jit(solution)/shard_map/scatter | solution.py:94
  69.9 13.6 %all-reduce = s32[64]{0:T(128)S(1)} all-reduce(s32[64]{0:T(128)S(1)} %dynamic-update-slice), channel_id=1, replica_groups=mesh['pop'=32,'site'=8] {'site'}, use_global_device_ids=true, to_apply=%add | all-reduce | flops 64 | bytes 512
  83.9 3.5 %all-gather.3.cloned.1.call-done = bf16[64,128,96]{1,0,2:T(8,128)(2,1)} async-done(((bf16[8,128,96]{1,0,2:T(8,128)(2,1)}), bf16[64,128,96]{1,0,2:T(8,128)(2,1)}) %all-gather.3.cloned.1.call-update) | async-done | bytes 1572880 | tf_op jit(solution)/shard_map/all_gather | solution.py:103
  87.3 42.4 %all-gather.5.cloned.1.call-done = bf16[64,128,128]{2,1,0:T(8,128)(2,1)} async-done(((bf16[8,128,128]{2,1,0:T(8,128)(2,1)}), bf16[64,128,128]{2,1,0:T(8,128)(2,1)}) %all-gather.5.cloned.1.call-update) | async-done | bytes 2097168 | tf_op jit(solution)/shard_map/all_gather | solution.py:104
  129.7 44.4 %while.11 = (s32[]{:T(128)}, f32[8,128,128]{2,1,0:T(8,128)S(1)}, bf16[8,8,128,96]{2,1,0,3:T(8,128)(2,1)}, s32[8]{0:T(128)S(1)}, s32[8,8]{1,0:T(8,128)S(1)}, /*in...) while((s32[]{:T(128)}, f32[8,128,128]{2,1,0:T(8,128)S(1)}, ...), condition=%wide.region_9.10_spmd.clone, body=%wide.region_8.9_spmd.clone.sunk | while | flops 743571584 | bytes 16384511 | solution.py:37
  133.4 1.9 fusion.68
  139.0 1.9 fusion.68
  144.5 1.9 fusion.68
  150.1 1.9 fusion.68
  155.6 1.9 fusion.68
  161.2 1.9 fusion.68
  166.7 1.9 fusion.68
  172.3 1.9 fusion.68
  174.3 2.5 %gather_fusion = bf16[768,128]{1,0:T(8,128)(2,1)} fusion(bf16[1024,128]{1,0:T(8,128)(2,1)S(1)} %bitcast.106, s32[1024]{0:T(1024)S(1)} %pad_clamp_fusion.1), kind=kCustom, calls=%fused_computation.2 | custom fusion | bytes 396288 | tf_op jit(solution)/shard_map/gather | solution.py:109
  176.8 11.2 %all-to-all-start.3 = ((bf16[32,24,128]{2,1,0:T(8,128)(2,1)}), bf16[32,24,128]{2,1,0:T(8,128)(2,1)S(1)}, u32[]{:S(2)}, u32[]{:S(2)}) async-start(bf16[32,24,128]{2,1,0:T(8,128)(2,1)} %bitcast.14), calls=%async_computation.3 | async-start | bytes 393216 | tf_op jit(solution)/shard_map/all_to_all | solution.py:110
  188.0 8.3 %all-to-all-done.3 = bf16[32,24,128]{2,1,0:T(8,128)(2,1)S(1)} async-done(((bf16[32,24,128]{2,1,0:T(8,128)(2,1)}), bf16[32,24,128]{2,1,0:T(8,128)(2,1)S(1)}, u32[]{:S(2)}, u32[]{:S(2)}) %all-to-all-start.3) | async-done | bytes 196640 | tf_op jit(solution)/shard_map/all_to_all | solution.py:110
  (90 shorter events, 42.2 us)
Async XLA Ops:
  6.5 41.9 %copy-start = (bf16[128,128]{1,0:T(8,128)(2,1)S(1)}, bf16[128,128]{1,0:T(8,128)(2,1)}, u32[]{:S(2)}) copy-start(bf16[128,128]{1,0:T(8,128)(2,1)} %param.11) | copy-start | bytes 98308
  6.5 61.8 %copy-start.3 = (u32[256]{0:T(256)S(1)}, u32[256]{0:T(256)}, u32[]{:S(2)}) copy-start(u32[256]{0:T(256)} %constant.52) | copy-start | bytes 3076
  6.5 63.1 %copy-start.1 = (s32[8]{0:T(128)S(1)}, s32[8]{0:T(128)}, u32[]{:S(2)}) copy-start(s32[8]{0:T(128)} %param.17) | copy-start | bytes 100
  13.5 15.5 %all-to-all-start = ((s32[32,1,24]{2,1,0:T(1,128)}), s32[32,1,24]{2,1,0:T(1,128)S(1)}, u32[]{:S(2)}, u32[]{:S(2)}) async-start(s32[32,1,24]{2,1,0:T(1,128)} %bitcast.2), calls=%async_computation | async-start | bytes 32768 | tf_op jit(solution)/shard_map/all_to_all | solution.py:82
  28.9 14.3 %all-to-all-start.1 = ((bf16[32,24,96]{2,1,0:T(8,128)(2,1)}), bf16[32,24,96]{2,1,0:T(8,128)(2,1)S(1)}, u32[]{:S(2)}, u32[]{:S(2)}) async-start(bf16[32,24,96]{2,1,0:T(8,128)(2,1)} %bitcast.3), calls=%async_computation.1 | async-start | bytes 393216 | tf_op jit(solution)/shard_map/all_to_all | solution.py:80
  34.9 52.4 %all-gather.3.cloned.1.call-start = ((), (), s32[]{:S(2)}) async-start(), calls=%async_computation.4 | async-start | bytes 1769472 | tf_op jit(solution)/shard_map/all_gather | solution.py:103
  48.4 81.3 %all-gather.5.cloned.1.call-start = ((), (), s32[]{:S(2)}) async-start(), calls=%async_computation.5 | async-start | bytes 2359296 | tf_op jit(solution)/shard_map/all_gather | solution.py:104
  174.2 23.5 %copy-start.2 = (s32[512]{0:T(512)S(1)}, s32[512]{0:T(512)}, u32[]{:S(2)}) copy-start(s32[512]{0:T(512)} %param.12) | copy-start | bytes 6148
  176.8 19.6 %all-to-all-start.3 = ((bf16[32,24,128]{2,1,0:T(8,128)(2,1)}), bf16[32,24,128]{2,1,0:T(8,128)(2,1)S(1)}, u32[]{:S(2)}, u32[]{:S(2)}) async-start(bf16[32,24,128]{2,1,0:T(8,128)(2,1)} %bitcast.14), calls=%async_computation.3 | async-start | bytes 393216 | tf_op jit(solution)/shard_map/all_to_all | solution.py:110
Sparse Core Ops, SparseCore 0:
  48.5 38.7 all-gather.2
  89.1 40.5 all-gather.4
where the time goes:
time: 207 us; the launch traced here: 205 us
  waiting for transfers between devices  62.6 us (30%)
  matrix products  36.5 us (18%)
  local copies, waits for them, and re-layouts  30.9 us (15%)
  starting transfers between devices  25.9 us (13%)
  blocking collectives  25.5 us (12%)
  between operations  14.2 us (7%)
  other arithmetic  9.37 us (5%)
    all_gather x1, waiting for transfers between devices, per_device(): lax.all_gather(tile_panel, 'site', axis=0, tiled=True)  42.4 us
    dot_general x8, matrix products, one_group(): jnp.einsum('abrq,bqc->arc', high_part, group_panel, preferred_element_typ...  14.8 us
    unnamed x1, blocking collectives  13.6 us
    dot_general x8, matrix products, one_group(): jnp.einsum('abrq,bqc->arc', low_part, group_panel, preferred_element_type...  13.6 us
    all_to_all x1, blocking collectives, per_device(): lax.all_to_all(send_panel, 'pop', split_axis=0, concat_axis=0, tiled=True)  11.9 us
    all_to_all x1, starting transfers between devices, per_device(): lax.all_to_all(sent_back, 'pop', split_axis=0, concat_axis=0, tiled=True)  11.2 us
    all_to_all x1, starting transfers between devices, per_device(): lax.all_to_all(send_rows, 'pop', split_axis=0, concat_axis=0, tiled=True)  8.59 us
    all_to_all x1, waiting for transfers between devices, per_device(): lax.all_to_all(sent_back, 'pop', split_axis=0, concat_axis=0, tiled=True)  8.32 us
  transfers between devices with their start and end apart: 5, of which 5 were waited for; matrix products, arithmetic and copies ran while one was open for 8% of the time, Pallas kernels for 0%

commit v1 on v0

v1 whole, which is shorter than its diff:
```python
import jax
import jax.numpy as jnp
from jax import lax
from jax.experimental import pallas as pl
from jax.experimental.pallas import tpu as pltpu
from jax.sharding import PartitionSpec as P

BF16 = jnp.bfloat16
F32 = jnp.float32
LOCATIONS = 8
NT = (((1,), (1,)), ((), ()))


def iota(shape, axis):
    return lax.broadcasted_iota(jnp.int32, shape, axis)


def matmul(a, b):
    return jnp.dot(a, b, preferred_element_type=F32)


def matmul_nt(a, b):
    return lax.dot_general(a, b, NT, preferred_element_type=F32)


def as_bf16(mask):
    return jnp.where(mask, 1.0, 0.0).astype(BF16)


def pack_kernel(
    pop_count,
    profile_ref,
    panel_ref,
    person_ref,
    owner_ref,
    row_ref,
    start_ref,
    length_ref,
    send_ref,
    persons_ref,
    wide_ref,
):
    visits = person_ref.shape[1]
    persons, slots = profile_ref.shape
    rows = send_ref.shape[0]
    capacity = rows // pop_count
    owner = owner_ref[...]
    start = start_ref[...]
    finish = jnp.minimum(start + length_ref[...], slots)
    tile = row_ref[...] >> 7
    owner_hot = iota((pop_count, visits), 0) == owner
    earlier = as_bf16(iota((visits, visits), 0) < iota((visits, visits), 1))
    before = matmul(as_bf16(owner_hot), earlier)
    position = jnp.sum(jnp.where(owner_hot, before, 0.0), axis=0, keepdims=True)
    slot = owner * capacity + position.astype(jnp.int32)
    place = as_bf16(iota((rows, visits), 0) == slot)
    person_hot = as_bf16(iota((persons, visits), 0) == person_ref[...])
    line = iota((128, visits), 0)
    facts = jnp.where(line == 0, start, jnp.where(line == 1, finish, jnp.where(line == 2, tile, 0)))
    table = jnp.concatenate([person_hot, facts.astype(F32).astype(BF16)], axis=0)
    placed = matmul_nt(place, table)
    hot = placed[:, :persons].astype(BF16)
    start_at = placed[:, persons : persons + 1]
    finish_at = placed[:, persons + 1 : persons + 2]
    tile_at = placed[:, persons + 2 : persons + 3]
    wide_ref[...] = jnp.zeros_like(wide_ref)
    wide_ref[:, :slots] = profile_ref[...]
    weights = matmul(hot, wide_ref[...])
    lane = iota((rows, 128), 1)
    lane_f = lane.astype(F32)
    inside = (lane_f >= start_at) & (lane_f < finish_at)
    weights = jnp.where(inside, weights, 0.0)
    weights = jnp.where(lane == slots, tile_at, weights)
    send_ref[:, :128] = weights.astype(BF16)
    send_ref[:, 128:] = matmul(hot, panel_ref[...]).astype(BF16)
    persons_ref[...] = matmul_nt(person_hot, place).astype(BF16)


def moment_kernel(slots, tile_loc_ref, got_ref, moment_ref):
    rows = got_ref.shape[0]
    unit = as_bf16(iota((128, 128), 0) == iota((128, 128), 1))
    flipped = matmul_nt(unit, got_ref[:, :128])
    tile = flipped[slots : slots + 1, :].astype(jnp.int32)
    place = jnp.zeros((1, rows), jnp.int32)
    for t in range(tile_loc_ref.shape[0]):
        place = jnp.where(tile == t, tile_loc_ref[t], place)
    weights = flipped[:slots, :]
    masked = [jnp.where(place == l, weights, 0.0).astype(BF16) for l in range(LOCATIONS)]
    moment = matmul(jnp.concatenate(masked, axis=0), got_ref[:, 128:])
    moment_ref[...] = moment.reshape(moment_ref.shape).astype(moment_ref.dtype)


def apply_kernel(slots, tile_loc_ref, got_ref, total_ref, result_ref, high_ref, low_ref):
    rows = got_ref.shape[0]
    tile = got_ref[:, slots : slots + 1].astype(F32).astype(jnp.int32)
    place = jnp.zeros((rows, 1), jnp.int32)
    for t in range(tile_loc_ref.shape[0]):
        place = jnp.where(tile == t, tile_loc_ref[t], place)
    high_ref[...] = jnp.zeros_like(high_ref)
    low_ref[...] = jnp.zeros_like(low_ref)
    for l in range(LOCATIONS):
        total = total_ref[l].astype(F32)
        high = total.astype(BF16)
        high_ref[pl.ds(l * 128, slots), :] = high
        low_ref[pl.ds(l * 128, slots), :] = (total - high.astype(F32)).astype(BF16)
    weights = got_ref[:, :128].astype(F32)
    weights = jnp.where(iota((rows, 128), 1) < slots, weights, 0.0)
    spread = jnp.concatenate(
        [jnp.where(place == l, weights, 0.0).astype(BF16) for l in range(LOCATIONS)], axis=1
    )
    result = matmul(spread, high_ref[...]) + matmul(spread, low_ref[...])
    result_ref[...] = (result / slots).astype(BF16)


def finish_kernel(persons_ref, results_ref, out_ref):
    out_ref[...] = matmul(persons_ref[...], results_ref[...]).astype(BF16)


def vmem(count):
    return [pl.BlockSpec(memory_space=pltpu.VMEM)] * count


def per_device(
    profile, panel, visit_person, visit_owner, visit_row, visit_start, visit_length, tile_loc
):
    pop_count = lax.axis_size("pop")
    visits = visit_person.shape[0]
    persons, slots = profile.shape
    width = panel.shape[1]
    capacity = visits // pop_count * 3 // 2
    rows = pop_count * capacity
    as_row = lambda x: x.reshape(1, visits)
    send, person_rows = pl.pallas_call(
        lambda *refs: pack_kernel(pop_count, *refs),
        out_shape=(
            jax.ShapeDtypeStruct((rows, 128 + width), BF16),
            jax.ShapeDtypeStruct((persons, rows), BF16),
        ),
        in_specs=vmem(7),
        out_specs=tuple(vmem(2)),
        scratch_shapes=[pltpu.VMEM((persons, 128), BF16)],
        name="pack",
    )(
        profile,
        panel,
        as_row(visit_person),
        as_row(visit_owner),
        as_row(visit_row),
        as_row(visit_start),
        as_row(visit_length),
    )
    got = lax.all_to_all(
        send.reshape(pop_count, capacity, 128 + width), "pop", 0, 0, tiled=True
    ).reshape(rows, 128 + width)
    smem = pl.BlockSpec(memory_space=pltpu.SMEM)
    moment = pl.pallas_call(
        lambda *refs: moment_kernel(slots, *refs),
        out_shape=jax.ShapeDtypeStruct((LOCATIONS, slots, width), F32),
        in_specs=[smem] + vmem(1),
        out_specs=vmem(1)[0],
        name="moments",
    )(tile_loc, got)
    total = lax.psum(moment, "site")
    result = pl.pallas_call(
        lambda *refs: apply_kernel(slots, *refs),
        out_shape=jax.ShapeDtypeStruct((rows, width), BF16),
        in_specs=[smem] + vmem(2),
        out_specs=vmem(1)[0],
        scratch_shapes=[pltpu.VMEM((LOCATIONS * 128, width), BF16)] * 2,
        name="apply",
    )(tile_loc, got, total)
    returned = lax.all_to_all(
        result.reshape(pop_count, capacity, width), "pop", 0, 0, tiled=True
    ).reshape(rows, width)
    return pl.pallas_call(
        finish_kernel,
        out_shape=jax.ShapeDtypeStruct((persons, width), BF16),
        in_specs=vmem(2),
        out_specs=vmem(1)[0],
        name="finish",
    )(person_rows, returned)


def solution(mesh):
    both = P(("pop", "site"))
    wide = P(("pop", "site"), None)
    return jax.shard_map(
        per_device,
        mesh=mesh,
        in_specs=(wide, wide, both, both, both, both, both, both),
        out_specs=wide,
        check_vma=False,
    )
```

time: 207 us -> 132 us (0.64)
  matrix products: 36.5 us -> 0 us
  local copies, waits for them, and re-layouts: 30.9 us -> 1.45 us
  starting transfers between devices: 25.9 us -> 0.01 us
  blocking collectives: 25.5 us -> 39.5 us
  Pallas kernels: 0 us -> 10.1 us
  other arithmetic: 9.37 us -> 0 us
  waiting for transfers between devices: 62.6 us -> 67.4 us
    psum x0 -> x1, waiting for transfers between devices: none -> 67.4 us  [per_device(): total = lax.psum(moment, 'site')]
    all_gather x2 -> x0, waiting for transfers between devices: 45.9 us -> none  [the longest x1 42.4 us: per_device(): lax.all_gather(tile_panel, 'site', axis=0, tiled=True)]
    dot_general x25 -> x0, matrix products: 36.5 us -> none  [the longest x8 14.8 us: one_group(): jnp.einsum('abrq,bqc->arc', high_part, group_panel, preferred_element_typ...]
    all_to_all x1 -> x2, blocking collectives: 11.9 us -> 39.5 us  [the longest x1 20.5 us: per_device(): lax.all_to_all(result.reshape(pop_count, capacity, width), 'pop', 0, 0, t...]
    all_to_all x3 -> x0, starting transfers between devices: 25.8 us -> none  [the longest x1 11.2 us: per_device(): lax.all_to_all(sent_back, 'pop', split_axis=0, concat_axis=0, tiled=True)]
    all_to_all x3 -> x0, waiting for transfers between devices: 16.7 us -> none  [the longest x1 8.32 us: per_device(): lax.all_to_all(sent_back, 'pop', split_axis=0, concat_axis=0, tiled=True)]
    scatter x4 -> x0, local copies, waits for them, and re-layouts: 14.8 us -> none  [the longest x1 4.9 us: per_device(): tile_panel = jnp.zeros((row_count, panel_width), jnp.bfloat16).at[target]...]
    unnamed x1 -> x0, blocking collectives: 13.6 us -> none
  transfers between devices with their start and end apart: 5 -> 1, of which waited for: 5 -> 1; matrix products, arithmetic and copies ran while one was open for 8% -> 0% of each run, Pallas kernels for 0% -> 0%
where the time goes in v1:
time: 132 us
  waiting for transfers between devices  67.4 us (51%)
  blocking collectives  39.5 us (30%)
  between operations  13.4 us (10%)
  Pallas kernels  10.1 us (8%)
  local copies, waits for them, and re-layouts  1.45 us (1%)
    psum x1, waiting for transfers between devices, per_device(): total = lax.psum(moment, 'site')  67.4 us
    all_to_all x1, blocking collectives, per_device(): lax.all_to_all(result.reshape(pop_count, capacity, width), 'pop', 0, 0, t...  20.5 us
    all_to_all x1, blocking collectives, per_device(): lax.all_to_all(send.reshape(pop_count, capacity, 128 + width), 'pop', 0,...  19 us
    pallas_call x1, Pallas kernels, per_device(): pl.pallas_call(lambda *refs: apply_kernel(slots, *refs), out_shape=jax.Sh...  3.15 us
    pallas_call x1, Pallas kernels, per_device(): pl.pallas_call(lambda *refs: pack_kernel(pop_count, *refs), out_shape=(ja...  2.74 us
  transfers between devices with their start and end apart: 1, of which 1 were waited for; matrix products, arithmetic and copies ran while one was open for 0% of the time, Pallas kernels for 0%

profile of v1, /device:TPU:1, one launch (start us, length us, event | category | flops | bytes accessed | tf_op | source)
XLA Modules:
  0.0 131.9 jit_solution(1466980662774773303)
XLA Ops:
  6.5 0.0 all-reduce.2.cloned.1.call-start
  6.5 1.5 %copy.9.refs_0_ = bf16[128,96]{1,0:T(8,128)(2,1)} copy(bf16[128,96]{0,1:T(8,128)(2,1)} %param.8) | data formatting | bytes 49152 | tf_op args[0]
  8.0 2.7 %pack.1 = (bf16[768,256]{1,0:T(8,128)(2,1)}, bf16[128,768]{1,0:T(8,128)(2,1)}) custom-call(bf16[128,96]{1,0:T(8,128)(2,1)} %copy.9.refs_0_, bf16[128,128]{1,0:T(8,128)(2,1)} %refs_1_.1, s32[1,512]{1,0:T(1,128)} %bitcast.14, s32[1,512]{1,0:T(1,128)} %bitcast.15, s32[1,512]{1,0:T(1,128)} %bitcast.16, s32[1,512]{1,0:T(1,128)} %bitcast.17, s32[1,512]{1,0:T(1,128)} %bitcast.18), custom_call_target="tpu_custom_call" | custom-call | tf_op jit(solution)/shard_map/pack/pallas_call | solution.py:133
  10.7 19.0 %all_to_all.10 = bf16[32,24,256]{2,1,0:T(8,128)(2,1)} all-to-all(bf16[32,24,256]{2,1,0:T(8,128)(2,1)} %bitcast.13), channel_id=1, replica_groups=mesh['pop'=32,'site'=8] {'pop'}, dimensions={0} | all-to-all | bytes 786432 | tf_op jit(solution)/shard_map/all_to_all | solution.py:152
  29.7 2.4 %moments.1 = f32[8,96,128]{2,1,0:T(8,128)} custom-call(s32[8]{0:T(128)} %refs_0_.4, bf16[768,256]{1,0:T(8,128)(2,1)} %bitcast.9), custom_call_target="tpu_custom_call" | custom-call | tf_op jit(solution)/shard_map/moments/pallas_call | solution.py:156
  32.1 0.0 all-reduce.2.cloned.1.call-update
  32.2 67.4 %all-reduce.2.cloned.1.call-done.refs_2_ = f32[8,96,128]{2,1,0:T(8,128)} async-done(((f32[8,96,128]{2,1,0:T(8,128)}), f32[8,96,128]{2,1,0:T(8,128)}) %all-reduce.2.cloned.1.call-update) | async-done | bytes 393232 | tf_op jit(solution)/shard_map/psum | solution.py:163
  99.6 3.2 %apply.1 = bf16[768,128]{1,0:T(8,128)(2,1)} custom-call(s32[8]{0:T(128)} %refs_0_.4, bf16[768,256]{1,0:T(8,128)(2,1)} %bitcast.10, f32[8,96,128]{2,1,0:T(8,128)} %all-reduce.2.cloned.1.call-done.refs_2_), custom_call_target="tpu_custom_call" | custom-call | tf_op jit(solution)/shard_map/apply/pallas_call | solution.py:164
  102.7 20.5 %all_to_all.11 = bf16[32,24,128]{2,1,0:T(8,128)(2,1)} all-to-all(bf16[32,24,128]{2,1,0:T(8,128)(2,1)} %bitcast.11), channel_id=1, replica_groups=mesh['pop'=32,'site'=8] {'pop'}, dimensions={0} | all-to-all | bytes 393216 | tf_op jit(solution)/shard_map/all_to_all | solution.py:172
  123.2 1.8 %finish.1 = bf16[128,128]{1,0:T(8,128)(2,1)} custom-call(bf16[128,768]{1,0:T(8,128)(2,1)} %get-tuple-element.7.persons_ref, bf16[768,128]{1,0:T(8,128)(2,1)} %bitcast.12), custom_call_target="tpu_custom_call" | custom-call | tf_op jit(solution)/shard_map/finish/pallas_call | solution.py:175
Async XLA Ops:
  6.5 93.0 %all-reduce.2.cloned.1.call-start = ((), (), s32[]{:S(2)}) async-start(), calls=%async_computation.2 | async-start | bytes 786432 | tf_op jit(solution)/shard_map/psum | solution.py:163
Sparse Core Ops, SparseCore 0:
  32.3 67.2 all-reduce.1

commit v2 on v1

--- a/solution.py
+++ b/solution.py
@@ -38,10 +38,9 @@
     length_ref,
     send_ref,
     persons_ref,
-    wide_ref,
 ):
     visits = person_ref.shape[1]
-    persons, slots = profile_ref.shape
+    slots, persons = profile_ref.shape
     rows = send_ref.shape[0]
     capacity = rows // pop_count
     owner = owner_ref[...]
@@ -63,9 +62,8 @@
     start_at = placed[:, persons : persons + 1]
     finish_at = placed[:, persons + 1 : persons + 2]
     tile_at = placed[:, persons + 2 : persons + 3]
-    wide_ref[...] = jnp.zeros_like(wide_ref)
-    wide_ref[:, :slots] = profile_ref[...]
-    weights = matmul(hot, wide_ref[...])
+    no_slots = jnp.zeros((128 - slots, persons), BF16)
+    weights = matmul_nt(hot, jnp.concatenate([profile_ref[...], no_slots], axis=0))
     lane = iota((rows, 128), 1)
     lane_f = lane.astype(F32)
     inside = (lane_f >= start_at) & (lane_f < finish_at)
@@ -90,25 +88,27 @@
     moment_ref[...] = moment.reshape(moment_ref.shape).astype(moment_ref.dtype)
 
 
-def apply_kernel(slots, tile_loc_ref, got_ref, total_ref, result_ref, high_ref, low_ref):
+def sum_kernel(parts_ref, copies_ref):
+    total = jnp.sum(parts_ref[...].astype(F32), axis=0).astype(BF16)
+    for member in range(copies_ref.shape[0]):
+        copies_ref[member] = total
+
+
+def apply_kernel(slots, tile_loc_ref, got_ref, total_ref, result_ref, wide_ref):
     rows = got_ref.shape[0]
     tile = got_ref[:, slots : slots + 1].astype(F32).astype(jnp.int32)
     place = jnp.zeros((rows, 1), jnp.int32)
     for t in range(tile_loc_ref.shape[0]):
         place = jnp.where(tile == t, tile_loc_ref[t], place)
-    high_ref[...] = jnp.zeros_like(high_ref)
-    low_ref[...] = jnp.zeros_like(low_ref)
     for l in range(LOCATIONS):
-        total = total_ref[l].astype(F32)
-        high = total.astype(BF16)
-        high_ref[pl.ds(l * 128, slots), :] = high
-        low_ref[pl.ds(l * 128, slots), :] = (total - high.astype(F32)).astype(BF16)
+        wide_ref[pl.ds(l * 128, slots), :] = total_ref[l]
+        wide_ref[pl.ds(l * 128 + slots, 128 - slots), :] = jnp.zeros((128 - slots, 128), BF16)
     weights = got_ref[:, :128].astype(F32)
     weights = jnp.where(iota((rows, 128), 1) < slots, weights, 0.0)
     spread = jnp.concatenate(
         [jnp.where(place == l, weights, 0.0).astype(BF16) for l in range(LOCATIONS)], axis=1
     )
-    result = matmul(spread, high_ref[...]) + matmul(spread, low_ref[...])
+    result = matmul(spread, wide_ref[...])
     result_ref[...] = (result / slots).astype(BF16)
 
 
@@ -138,10 +138,9 @@
         ),
         in_specs=vmem(7),
         out_specs=tuple(vmem(2)),
-        scratch_shapes=[pltpu.VMEM((persons, 128), BF16)],
         name="pack",
     )(
-        profile,
+        profile.T,
         panel,
         as_row(visit_person),
         as_row(visit_owner),
@@ -155,18 +154,26 @@
     smem = pl.BlockSpec(memory_space=pltpu.SMEM)
     moment = pl.pallas_call(
         lambda *refs: moment_kernel(slots, *refs),
-        out_shape=jax.ShapeDtypeStruct((LOCATIONS, slots, width), F32),
+        out_shape=jax.ShapeDtypeStruct((LOCATIONS, slots, width), BF16),
         in_specs=[smem] + vmem(1),
         out_specs=vmem(1)[0],
         name="moments",
     )(tile_loc, got)
-    total = lax.psum(moment, "site")
+    parts = lax.all_to_all(moment, "site", 0, 0, tiled=True)
+    copies = pl.pallas_call(
+        sum_kernel,
+        out_shape=jax.ShapeDtypeStruct((LOCATIONS, slots, width), BF16),
+        in_specs=vmem(1),
+        out_specs=vmem(1)[0],
+        name="sum_parts",
+    )(parts)
+    total = lax.all_to_all(copies, "site", 0, 0, tiled=True)
     result = pl.pallas_call(
         lambda *refs: apply_kernel(slots, *refs),
         out_shape=jax.ShapeDtypeStruct((rows, width), BF16),
         in_specs=[smem] + vmem(2),
         out_specs=vmem(1)[0],
-        scratch_shapes=[pltpu.VMEM((LOCATIONS * 128, width), BF16)] * 2,
+        scratch_shapes=[pltpu.VMEM((LOCATIONS * 128, width), BF16)],
         name="apply",
     )(tile_loc, got, total)
     returned = lax.all_to_all(

time: 132 us -> 78.4 us (0.59)
  waiting for transfers between devices: 67.4 us -> 0 us
  blocking collectives: 39.5 us -> 66.3 us
  between operations: 13.4 us -> 0.01 us
  local copies, waits for them, and re-layouts: 1.45 us -> 0 us
  Pallas kernels: 10.1 us -> 11.5 us
    psum x1 -> x0, waiting for transfers between devices: 67.4 us -> none  [per_device(): total = lax.psum(moment, 'site')]
    all_to_all x0 -> x2, blocking collectives: none -> 32.9 us  [the longest x1 19.2 us: per_device(): parts = lax.all_to_all(moment, 'site', 0, 0, tiled=True)]
    all_to_all x1, blocking collectives: 20.5 us -> 14.4 us  [per_device(): lax.all_to_all(result.reshape(pop_count, capacity, width), 'pop', 0, 0, t...]
    pallas_call x0 -> x1, Pallas kernels: none -> 1.63 us  [per_device(): pl.pallas_call(sum_kernel, out_shape=jax.ShapeDtypeStruct((LOCATIONS, slo...]
    unnamed x1 -> x0, local copies, waits for them, and re-layouts: 1.45 us -> none
  transfers between devices with their start and end apart: 1 -> 0, of which waited for: 1 -> 0; matrix products, arithmetic and copies ran while one was open for 0% -> 0% of each run, Pallas kernels for 0% -> 0%
where the time goes in v2:
time: 78.4 us; the launch traced here: 77.8 us
  blocking collectives  66.3 us (85%)
  Pallas kernels  11.5 us (15%)
    all_to_all x1, blocking collectives, per_device(): parts = lax.all_to_all(moment, 'site', 0, 0, tiled=True)  19.2 us
    all_to_all x1, blocking collectives, per_device(): lax.all_to_all(send.reshape(pop_count, capacity, 128 + width), 'pop', 0,...  19 us
    all_to_all x1, blocking collectives, per_device(): lax.all_to_all(result.reshape(pop_count, capacity, width), 'pop', 0, 0, t...  14.4 us
    all_to_all x1, blocking collectives, per_device(): total = lax.all_to_all(copies, 'site', 0, 0, tiled=True)  13.7 us
    pallas_call x1, Pallas kernels, per_device(): pl.pallas_call(lambda *refs: apply_kernel(slots, *refs), out_shape=jax.Sh...  3.03 us
    pallas_call x1, Pallas kernels, per_device(): pl.pallas_call(lambda *refs: pack_kernel(pop_count, *refs), out_shape=(ja...  2.71 us
    pallas_call x1, Pallas kernels, per_device(): pl.pallas_call(lambda *refs: moment_kernel(slots, *refs), out_shape=jax.S...  2.34 us
    pallas_call x1, Pallas kernels, per_device(): pl.pallas_call(finish_kernel, out_shape=jax.ShapeDtypeStruct((persons, wi...  1.84 us

profile of v2, /device:TPU:1, one launch (start us, length us, event | category | flops | bytes accessed | tf_op | source)
XLA Modules:
  0.0 77.8 jit_solution(6526445811532793759)
XLA Ops:
  0.0 2.7 %pack.1 = (bf16[768,256]{1,0:T(8,128)(2,1)}, bf16[128,768]{1,0:T(8,128)(2,1)}) custom-call(bf16[96,128]{1,0:T(8,128)(2,1)} %bitcast.15, bf16[128,128]{1,0:T(8,128)(2,1)} %refs_1_.1, s32[1,512]{1,0:T(1,128)} %bitcast.16, s32[1,512]{1,0:T(1,128)} %bitcast.17, s32[1,512]{1,0:T(1,128)} %bitcast.18, s32[1,512]{1,0:T(1,128)} %bitcast.19, s32[1,512]{1,0:T(1,128)} %bitcast.20), custom_call_target="tpu_custom_call" | custom-call | tf_op jit(solution)/shard_map/pack/pallas_call | solution.py:133
  2.7 19.0 %all_to_all.20 = bf16[32,24,256]{2,1,0:T(8,128)(2,1)} all-to-all(bf16[32,24,256]{2,1,0:T(8,128)(2,1)} %bitcast.14), channel_id=1, replica_groups=mesh['pop'=32,'site'=8] {'pop'}, dimensions={0} | all-to-all | bytes 786432 | tf_op jit(solution)/shard_map/all_to_all | solution.py:151
  21.7 2.3 %moments.1 = bf16[8,96,128]{2,1,0:T(8,128)(2,1)} custom-call(s32[8]{0:T(128)} %refs_0_.3, bf16[768,256]{1,0:T(8,128)(2,1)} %bitcast.10), custom_call_target="tpu_custom_call" | custom-call | tf_op jit(solution)/shard_map/moments/pallas_call | solution.py:155
  24.1 19.2 %all_to_all.21.parts_ref = bf16[8,96,128]{2,1,0:T(8,128)(2,1)} all-to-all(bf16[8,96,128]{2,1,0:T(8,128)(2,1)} %moments.1), channel_id=1, replica_groups=mesh['pop'=32,'site'=8] {'site'}, dimensions={0} | all-to-all | bytes 393216 | tf_op jit(solution)/shard_map/all_to_all | solution.py:162
  43.3 1.6 %sum_parts.1 = bf16[8,96,128]{2,1,0:T(8,128)(2,1)} custom-call(bf16[8,96,128]{2,1,0:T(8,128)(2,1)} %all_to_all.21.parts_ref), custom_call_target="tpu_custom_call" | custom-call | tf_op jit(solution)/shard_map/sum_parts/pallas_call | solution.py:163
  44.9 13.7 %all_to_all.22.refs_2_ = bf16[8,96,128]{2,1,0:T(8,128)(2,1)} all-to-all(bf16[8,96,128]{2,1,0:T(8,128)(2,1)} %sum_parts.1), channel_id=1, replica_groups=mesh['pop'=32,'site'=8] {'site'}, dimensions={0} | all-to-all | bytes 393216 | tf_op jit(solution)/shard_map/all_to_all | solution.py:170
  58.6 3.0 %apply.1 = bf16[768,128]{1,0:T(8,128)(2,1)} custom-call(s32[8]{0:T(128)} %refs_0_.3, bf16[768,256]{1,0:T(8,128)(2,1)} %bitcast.11, bf16[8,96,128]{2,1,0:T(8,128)(2,1)} %all_to_all.22.refs_2_), custom_call_target="tpu_custom_call" | custom-call | tf_op jit(solution)/shard_map/apply/pallas_call | solution.py:171
  61.6 14.4 %all_to_all.23 = bf16[32,24,128]{2,1,0:T(8,128)(2,1)} all-to-all(bf16[32,24,128]{2,1,0:T(8,128)(2,1)} %bitcast.13), channel_id=1, replica_groups=mesh['pop'=32,'site'=8] {'pop'}, dimensions={0} | all-to-all | bytes 393216 | tf_op jit(solution)/shard_map/all_to_all | solution.py:179
  76.0 1.8 %finish.1 = bf16[128,128]{1,0:T(8,128)(2,1)} custom-call(bf16[128,768]{1,0:T(8,128)(2,1)} %get-tuple-element.7.persons_ref, bf16[768,128]{1,0:T(8,128)(2,1)} %bitcast.12), custom_call_target="tpu_custom_call" | custom-call | tf_op jit(solution)/shard_map/finish/pallas_call | solution.py:182

commit v3 on v2

--- a/solution.py
+++ b/solution.py
@@ -120,6 +120,12 @@
     return [pl.BlockSpec(memory_space=pltpu.VMEM)] * count
 
 
+def exchange(array, axis):
+    blocks = array.reshape((lax.axis_size(axis), -1, array.shape[-1]))
+    moved = lax.all_to_all(blocks, axis, 0, 0, tiled=True).reshape(array.shape)
+    return pltpu.with_memory_space_constraint(moved, pltpu.VMEM)
+
+
 def per_device(
     profile, panel, visit_person, visit_owner, visit_row, visit_start, visit_length, tile_loc
 ):
@@ -133,8 +139,8 @@
     send, person_rows = pl.pallas_call(
         lambda *refs: pack_kernel(pop_count, *refs),
         out_shape=(
-            jax.ShapeDtypeStruct((rows, 128 + width), BF16),
-            jax.ShapeDtypeStruct((persons, rows), BF16),
+            pltpu.VMEM((rows, 128 + width), BF16),
+            pltpu.VMEM((persons, rows), BF16),
         ),
         in_specs=vmem(7),
         out_specs=tuple(vmem(2)),
@@ -148,44 +154,40 @@
         as_row(visit_start),
         as_row(visit_length),
     )
-    got = lax.all_to_all(
-        send.reshape(pop_count, capacity, 128 + width), "pop", 0, 0, tiled=True
-    ).reshape(rows, 128 + width)
+    got = exchange(send, "pop")
     smem = pl.BlockSpec(memory_space=pltpu.SMEM)
     moment = pl.pallas_call(
         lambda *refs: moment_kernel(slots, *refs),
-        out_shape=jax.ShapeDtypeStruct((LOCATIONS, slots, width), BF16),
+        out_shape=pltpu.VMEM((LOCATIONS, slots, width), BF16),
         in_specs=[smem] + vmem(1),
         out_specs=vmem(1)[0],
         name="moments",
     )(tile_loc, got)
-    parts = lax.all_to_all(moment, "site", 0, 0, tiled=True)
+    parts = exchange(moment, "site")
     copies = pl.pallas_call(
         sum_kernel,
-        out_shape=jax.ShapeDtypeStruct((LOCATIONS, slots, width), BF16),
+        out_shape=pltpu.VMEM((LOCATIONS, slots, width), BF16),
         in_specs=vmem(1),
         out_specs=vmem(1)[0],
         name="sum_parts",
     )(parts)
-    total = lax.all_to_all(copies, "site", 0, 0, tiled=True)
+    total = exchange(copies, "site")
     result = pl.pallas_call(
         lambda *refs: apply_kernel(slots, *refs),
-        out_shape=jax.ShapeDtypeStruct((rows, width), BF16),
+        out_shape=pltpu.VMEM((rows, width), BF16),
         in_specs=[smem] + vmem(2),
         out_specs=vmem(1)[0],
         scratch_shapes=[pltpu.VMEM((LOCATIONS * 128, width), BF16)],
         name="apply",
     )(tile_loc, got, total)
-    returned = lax.all_to_all(
-        result.reshape(pop_count, capacity, width), "pop", 0, 0, tiled=True
-    ).reshape(rows, width)
+    returned = exchange(result, "pop")
     return pl.pallas_call(
         finish_kernel,
         out_shape=jax.ShapeDtypeStruct((persons, width), BF16),
         in_specs=vmem(2),
         out_specs=vmem(1)[0],
         name="finish",
-    )(person_rows, returned)
+    )(pltpu.with_memory_space_constraint(person_rows, pltpu.VMEM), returned)
 
 
 def solution(mesh):

time: 78.4 us -> 69.3 us (0.88)
  Pallas kernels: 11.5 us -> 6.16 us
  blocking collectives: 66.3 us -> 62.8 us
    pallas_call x4, Pallas kernels: 9.71 us -> 5.35 us  [the longest x1 2.03 us: per_device(): pl.pallas_call(lambda *refs: pack_kernel(pop_count, *refs), out_shape=(pl...]
    all_to_all x4, blocking collectives: 66.3 us -> 62.8 us  [exchange(): moved = lax.all_to_all(blocks, axis, 0, 0, tiled=True).reshape(array.shape)]
    pallas_call x1, Pallas kernels: 1.84 us -> 0.82 us  [per_device(): pl.pallas_call(finish_kernel, out_shape=jax.ShapeDtypeStruct((persons, wi...]
where the time goes in v3:
time: 69.3 us; the launch traced here: 69 us
  blocking collectives  62.8 us (91%)
  Pallas kernels  6.16 us (9%)
    all_to_all x4, blocking collectives, exchange(): moved = lax.all_to_all(blocks, axis, 0, 0, tiled=True).reshape(array.shape)  62.8 us
    pallas_call x1, Pallas kernels, per_device(): pl.pallas_call(lambda *refs: pack_kernel(pop_count, *refs), out_shape=(pl...  2.03 us
    pallas_call x1, Pallas kernels, per_device(): pl.pallas_call(lambda *refs: apply_kernel(slots, *refs), out_shape=pltpu....  1.96 us

profile of v3, /device:TPU:1, one launch (start us, length us, event | category | flops | bytes accessed | tf_op | source)
XLA Modules:
  0.0 69.0 jit_solution(14267804957092781604)
XLA Ops:
  0.0 2.0 %pack.1 = (bf16[768,256]{1,0:T(8,128)(2,1)S(1)}, bf16[128,768]{1,0:T(8,128)(2,1)S(1)}) custom-call(bf16[96,128]{1,0:T(8,128)(2,1)} %bitcast.15, bf16[128,128]{1,0:T(8,128)(2,1)} %refs_1_.1, s32[1,512]{1,0:T(1,128)} %bitcast.16, s32[1,512]{1,0:T(1,128)} %bitcast.17, s32[1,512]{1,0:T(1,128)} %bitcast.18, s32[1,512]{1,0:T(1,128)} %bitcast.19, s32[1,512]{1,0:T(1,128)} %bitcast.20), custom_call_target="tpu_custom_call" | custom-call | tf_op jit(solution)/shard_map/pack/pallas_call | solution.py:139
  2.0 18.7 %all_to_all.20 = bf16[32,24,256]{2,1,0:T(8,128)(2,1)S(1)} all-to-all(bf16[32,24,256]{2,1,0:T(8,128)(2,1)S(1)} %bitcast.14), channel_id=1, replica_groups=mesh['pop'=32,'site'=8] {'pop'}, dimensions={0} | all-to-all | bytes 786432 | tf_op jit(solution)/shard_map/all_to_all | solution.py:125
  20.7 1.3 %moments.1 = bf16[8,96,128]{2,1,0:T(8,128)(2,1)S(1)} custom-call(s32[8]{0:T(128)} %refs_0_.3, bf16[768,256]{1,0:T(8,128)(2,1)S(1)} %bitcast.10), custom_call_target="tpu_custom_call" | custom-call | tf_op jit(solution)/shard_map/moments/pallas_call | solution.py:159
  22.1 18.9 %all_to_all.21.parts_ref = bf16[8,96,128]{2,1,0:T(8,128)(2,1)S(1)} all-to-all(bf16[8,96,128]{2,1,0:T(8,128)(2,1)S(1)} %moments.1), channel_id=1, replica_groups=mesh['pop'=32,'site'=8] {'site'}, dimensions={0} | all-to-all | bytes 393216 | tf_op jit(solution)/shard_map/all_to_all | solution.py:125
  41.0 12.1 %all_to_all.22.refs_2_ = bf16[8,96,128]{2,1,0:T(8,128)(2,1)S(1)} all-to-all(bf16[8,96,128]{2,1,0:T(8,128)(2,1)S(1)} %sum_parts.1), channel_id=1, replica_groups=mesh['pop'=32,'site'=8] {'site'}, dimensions={0} | all-to-all | bytes 393216 | tf_op jit(solution)/shard_map/all_to_all | solution.py:125
  53.1 2.0 %apply.1 = bf16[768,128]{1,0:T(8,128)(2,1)S(1)} custom-call(s32[8]{0:T(128)} %refs_0_.3, bf16[768,256]{1,0:T(8,128)(2,1)S(1)} %bitcast.11, bf16[8,96,128]{2,1,0:T(8,128)(2,1)S(1)} %all_to_all.22.refs_2_), custom_call_target="tpu_custom_call" | custom-call | tf_op jit(solution)/shard_map/apply/pallas_call | solution.py:175
  55.1 13.2 %all_to_all.23 = bf16[32,24,128]{2,1,0:T(8,128)(2,1)S(1)} all-to-all(bf16[32,24,128]{2,1,0:T(8,128)(2,1)S(1)} %bitcast.13), channel_id=1, replica_groups=mesh['pop'=32,'site'=8] {'pop'}, dimensions={0} | all-to-all | bytes 393216 | tf_op jit(solution)/shard_map/all_to_all | solution.py:125
  68.2 0.8 %finish.1 = bf16[128,128]{1,0:T(8,128)(2,1)} custom-call(bf16[128,768]{1,0:T(8,128)(2,1)S(1)} %get-tuple-element.7.persons_ref, bf16[768,128]{1,0:T(8,128)(2,1)S(1)} %bitcast.12), custom_call_target="tpu_custom_call" | custom-call | tf_op jit(solution)/shard_map/finish/pallas_call | solution.py:184
  (1 shorter events, 0.0 us)

commit v4 on v3

--- a/solution.py
+++ b/solution.py
@@ -8,6 +8,8 @@
 BF16 = jnp.bfloat16
 F32 = jnp.float32
 LOCATIONS = 8
+HALF = LOCATIONS // 2
+TILES = 8
 NT = (((1,), (1,)), ((), ()))
 
 
@@ -46,7 +48,7 @@
     owner = owner_ref[...]
     start = start_ref[...]
     finish = jnp.minimum(start + length_ref[...], slots)
-    tile = row_ref[...] >> 7
+    tile = (row_ref[...] >> 7) + TILES * (lax.axis_index("site") & 1)
     owner_hot = iota((pop_count, visits), 0) == owner
     earlier = as_bf16(iota((visits, visits), 0) < iota((visits, visits), 1))
     before = matmul(as_bf16(owner_hot), earlier)
@@ -74,34 +76,50 @@
     persons_ref[...] = matmul_nt(person_hot, place).astype(BF16)
 
 
-def moment_kernel(slots, tile_loc_ref, got_ref, moment_ref):
-    rows = got_ref.shape[0]
+def place_of(tile, loc_refs):
+    mine, sibling, neighbour, diagonal = loc_refs
+    core = lax.axis_index("pop") & 1
+    parity = lax.axis_index("site") & 1
+    place = jnp.zeros(tile.shape, jnp.int32)
+    for t in range(TILES):
+        same = jnp.where(core == parity, mine[t], sibling[t])
+        other = jnp.where(core == parity, neighbour[t], diagonal[t])
+        place = jnp.where(tile == t, jnp.where(parity == 0, same, other), place)
+        place = jnp.where(tile == TILES + t, jnp.where(parity == 0, other, same), place)
+    return place ^ (HALF * core)
+
+
+def moment_kernel(slots, *refs):
+    loc_refs = refs[:4]
+    got_ref, keep_ref, give_ref = refs[4:]
     unit = as_bf16(iota((128, 128), 0) == iota((128, 128), 1))
     flipped = matmul_nt(unit, got_ref[:, :128])
-    tile = flipped[slots : slots + 1, :].astype(jnp.int32)
-    place = jnp.zeros((1, rows), jnp.int32)
-    for t in range(tile_loc_ref.shape[0]):
-        place = jnp.where(tile == t, tile_loc_ref[t], place)
+    place = place_of(flipped[slots : slots + 1, :].astype(jnp.int32), loc_refs)
     weights = flipped[:slots, :]
     masked = [jnp.where(place == l, weights, 0.0).astype(BF16) for l in range(LOCATIONS)]
     moment = matmul(jnp.concatenate(masked, axis=0), got_ref[:, 128:])
-    moment_ref[...] = moment.reshape(moment_ref.shape).astype(moment_ref.dtype)
-
-
-def sum_kernel(parts_ref, copies_ref):
-    total = jnp.sum(parts_ref[...].astype(F32), axis=0).astype(BF16)
-    for member in range(copies_ref.shape[0]):
-        copies_ref[member] = total
-
-
-def apply_kernel(slots, tile_loc_ref, got_ref, total_ref, result_ref, wide_ref):
+    keep_ref[...] = moment[: HALF * slots]
+    give_ref[...] = moment[HALF * slots :].astype(BF16)
+
+
+def add_kernel(own_ref, far_ref, sum_ref, give_ref):
+    total = own_ref[...] + far_ref[...].astype(F32)
+    sum_ref[...] = total
+    give_ref[...] = total.astype(BF16)
+
+
+def last_add_kernel(own_ref, far_ref, give_ref):
+    give_ref[...] = (own_ref[...] + far_ref[...].astype(F32)).astype(BF16)
+
+
+def apply_kernel(slots, *refs):
+    loc_refs = refs[:4]
+    got_ref, own_ref, other_ref, result_ref, wide_ref = refs[4:]
     rows = got_ref.shape[0]
-    tile = got_ref[:, slots : slots + 1].astype(F32).astype(jnp.int32)
-    place = jnp.zeros((rows, 1), jnp.int32)
-    for t in range(tile_loc_ref.shape[0]):
-        place = jnp.where(tile == t, tile_loc_ref[t], place)
+    place = place_of(got_ref[:, slots : slots + 1].astype(F32).astype(jnp.int32), loc_refs)
     for l in range(LOCATIONS):
-        wide_ref[pl.ds(l * 128, slots), :] = total_ref[l]
+        half_ref = own_ref if l < HALF else other_ref
+        wide_ref[pl.ds(l * 128, slots), :] = half_ref[pl.ds(l % HALF * slots, slots), :]
         wide_ref[pl.ds(l * 128 + slots, 128 - slots), :] = jnp.zeros((128 - slots, 128), BF16)
     weights = got_ref[:, :128].astype(F32)
     weights = jnp.where(iota((rows, 128), 1) < slots, weights, 0.0)
@@ -120,10 +138,40 @@
     return [pl.BlockSpec(memory_space=pltpu.VMEM)] * count
 
 
-def exchange(array, axis):
-    blocks = array.reshape((lax.axis_size(axis), -1, array.shape[-1]))
-    moved = lax.all_to_all(blocks, axis, 0, 0, tiled=True).reshape(array.shape)
-    return pltpu.with_memory_space_constraint(moved, pltpu.VMEM)
+def in_vmem(array):
+    return pltpu.with_memory_space_constraint(array, pltpu.VMEM)
+
+
+def exchange(array):
+    pops, sites = lax.axis_size("pop"), lax.axis_size("site")
+    groups = [
+        [(pop * 2 + core) * sites + pair * 2 + odd for pop in range(pops // 2) for odd in range(2)]
+        for core in range(2)
+        for pair in range(sites // 2)
+    ]
+    blocks = array.reshape((pops, -1, array.shape[-1]))
+    moved = lax.all_to_all(
+        blocks, ("pop", "site"), 0, 0, tiled=True, axis_index_groups=groups
+    )
+    return in_vmem(moved.reshape(array.shape))
+
+
+def swap(array, pop_partner, site_partner):
+    pops, sites = lax.axis_size("pop"), lax.axis_size("site")
+    pairs = [
+        (pop * sites + site, pop_partner(pop) * sites + site_partner(site))
+        for pop in range(pops)
+        for site in range(sites)
+    ]
+    return lax.ppermute(array, ("pop", "site"), pairs)
+
+
+def flip(index):
+    return index ^ 1
+
+
+def stay(index):
+    return index
 
 
 def per_device(
@@ -154,40 +202,62 @@
         as_row(visit_start),
         as_row(visit_length),
     )
-    got = exchange(send, "pop")
-    smem = pl.BlockSpec(memory_space=pltpu.SMEM)
-    moment = pl.pallas_call(
+    tile_locs = [
+        tile_loc,
+        swap(tile_loc, flip, stay),
+        swap(tile_loc, stay, flip),
+        swap(tile_loc, flip, flip),
+    ]
+    got = exchange(send)
+    smem = [pl.BlockSpec(memory_space=pltpu.SMEM)] * 4
+    half = (HALF * slots, width)
+    kept, given = pl.pallas_call(
         lambda *refs: moment_kernel(slots, *refs),
-        out_shape=pltpu.VMEM((LOCATIONS, slots, width), BF16),
-        in_specs=[smem] + vmem(1),
-        out_specs=vmem(1)[0],
+        out_shape=(pltpu.VMEM(half, F32), pltpu.VMEM(half, BF16)),
+        in_specs=smem + vmem(1),
+        out_specs=tuple(vmem(2)),
         name="moments",
-    )(tile_loc, got)
-    parts = exchange(moment, "site")
-    copies = pl.pallas_call(
-        sum_kernel,
-        out_shape=pltpu.VMEM((LOCATIONS, slots, width), BF16),
-        in_specs=vmem(1),
-        out_specs=vmem(1)[0],
-        name="sum_parts",
-    )(parts)
-    total = exchange(copies, "site")
+    )(*tile_locs, got)
+    steps = (
+        (flip, stay),
+        (stay, lambda site: site ^ 2),
+        (stay, lambda site: (6 - site) % 8 if site % 2 == 0 else 8 - site),
+    )
+    for step, partners in enumerate(steps):
+        far = in_vmem(swap(given, *partners))
+        if step < 2:
+            kept, given = pl.pallas_call(
+                add_kernel,
+                out_shape=(pltpu.VMEM(half, F32), pltpu.VMEM(half, BF16)),
+                in_specs=vmem(2),
+                out_specs=tuple(vmem(2)),
+                name="add",
+            )(in_vmem(kept), far)
+        else:
+            given = pl.pallas_call(
+                last_add_kernel,
+                out_shape=pltpu.VMEM(half, BF16),
+                in_specs=vmem(2),
+                out_specs=vmem(1)[0],
+                name="last_add",
+            )(in_vmem(kept), far)
+    other = in_vmem(swap(given, flip, stay))
     result = pl.pallas_call(
         lambda *refs: apply_kernel(slots, *refs),
         out_shape=pltpu.VMEM((rows, width), BF16),
-        in_specs=[smem] + vmem(2),
+        in_specs=smem + vmem(3),
         out_specs=vmem(1)[0],
         scratch_shapes=[pltpu.VMEM((LOCATIONS * 128, width), BF16)],
         name="apply",
-    )(tile_loc, got, total)
-    returned = exchange(result, "pop")
+    )(*tile_locs, got, in_vmem(given), other)
+    returned = exchange(result)
     return pl.pallas_call(
         finish_kernel,
         out_shape=jax.ShapeDtypeStruct((persons, width), BF16),
         in_specs=vmem(2),
         out_specs=vmem(1)[0],
         name="finish",
-    )(pltpu.with_memory_space_constraint(person_rows, pltpu.VMEM), returned)
+    )(in_vmem(person_rows), returned)
 
 
 def solution(mesh):

time: 69.3 us -> 59.6 us (0.86)
  blocking collectives: 62.8 us -> 12.9 us
  starting transfers between devices: 0 us -> 21.7 us
  waiting for transfers between devices: 0 us -> 17.7 us
  Pallas kernels: 6.16 us -> 7.01 us
    all_to_all x4 -> x1, blocking collectives: 62.8 us -> 12.9 us  [exchange(): lax.all_to_all(blocks, ('pop', 'site'), 0, 0, tiled=True, axis_index_grou...]
    ppermute x0 -> x7, waiting for transfers between devices: none -> 14.6 us  [swap(): return lax.ppermute(array, ('pop', 'site'), pairs)]
    ppermute x0 -> x7, starting transfers between devices: none -> 12.4 us  [swap(): return lax.ppermute(array, ('pop', 'site'), pairs)]
    all_to_all x0 -> x1, starting transfers between devices: none -> 9.35 us  [exchange(): lax.all_to_all(blocks, ('pop', 'site'), 0, 0, tiled=True, axis_index_grou...]
    all_to_all x0 -> x1, waiting for transfers between devices: none -> 3.11 us  [exchange(): lax.all_to_all(blocks, ('pop', 'site'), 0, 0, tiled=True, axis_index_grou...]
    pallas_call x2 -> x4, Pallas kernels: 1.35 us -> 1.43 us  [the longest x1 1.36 us: per_device(): pl.pallas_call(lambda *refs: moment_kernel(slots, *refs), out_shape=(pltp...]
  transfers between devices with their start and end apart: 0 -> 8, of which waited for: 0 -> 6; matrix products, arithmetic and copies ran while one was open for 0% -> 0% of each run, Pallas kernels for 0% -> 0%
where the time goes in v4:
time: 59.6 us; the launch traced here: 59.4 us
  starting transfers between devices  21.7 us (36%)
  waiting for transfers between devices  17.7 us (30%)
  blocking collectives  12.9 us (22%)
  Pallas kernels  7.01 us (12%)
    ppermute x7, waiting for transfers between devices, swap(): return lax.ppermute(array, ('pop', 'site'), pairs)  14.6 us
    all_to_all x1, blocking collectives, exchange(): lax.all_to_all(blocks, ('pop', 'site'), 0, 0, tiled=True, axis_index_grou...  12.9 us
    ppermute x7, starting transfers between devices, swap(): return lax.ppermute(array, ('pop', 'site'), pairs)  12.4 us
    all_to_all x1, starting transfers between devices, exchange(): lax.all_to_all(blocks, ('pop', 'site'), 0, 0, tiled=True, axis_index_grou...  9.35 us
    all_to_all x1, waiting for transfers between devices, exchange(): lax.all_to_all(blocks, ('pop', 'site'), 0, 0, tiled=True, axis_index_grou...  3.11 us
    pallas_call x1, Pallas kernels, per_device(): pl.pallas_call(lambda *refs: pack_kernel(pop_count, *refs), out_shape=(pl...  2.56 us
    pallas_call x1, Pallas kernels, per_device(): pl.pallas_call(lambda *refs: apply_kernel(slots, *refs), out_shape=pltpu....  2.21 us
    pallas_call x1, Pallas kernels, per_device(): pl.pallas_call(lambda *refs: moment_kernel(slots, *refs), out_shape=(pltp...  1.36 us
  transfers between devices with their start and end apart: 8, of which 6 were waited for; matrix products, arithmetic and copies ran while one was open for 0% of the time, Pallas kernels for 0%

profile of v4, /device:TPU:1, one launch (start us, length us, event | category | flops | bytes accessed | tf_op | source)
XLA Modules:
  0.0 59.4 jit_solution(1240589340242397399)
XLA Ops:
  0.0 2.6 %pack.1 = (bf16[768,256]{1,0:T(8,128)(2,1)}, bf16[128,768]{1,0:T(8,128)(2,1)S(1)}) custom-call(bf16[96,128]{1,0:T(8,128)(2,1)} %bitcast.14, bf16[128,128]{1,0:T(8,128)(2,1)} %refs_1_.1, s32[1,512]{1,0:T(1,128)} %bitcast.15, s32[1,512]{1,0:T(1,128)} %bitcast.16, s32[1,512]{1,0:T(1,128)} %bitcast.17, s32[1,512]{1,0:T(1,128)} %bitcast.18, s32[1,512]{1,0:T(1,128)} %bitcast.19), custom_call_target="tpu_custom_call" | custom-call | tf_op jit(solution)/shard_map/pack/pallas_call | solution.py:187
  2.6 9.4 %all-to-all-start = ((bf16[32,24,256]{2,1,0:T(8,128)(2,1)}), bf16[32,24,256]{2,1,0:T(8,128)(2,1)S(1)}, u32[]{:S(2)}, u32[]{:S(2)}) async-start(bf16[32,24,256]{2,1,0:T(8,128)(2,1)} %bitcast.6), calls=%async_computation | async-start | bytes 786432 | tf_op jit(solution)/shard_map/all_to_all | solution.py:153
  11.9 0.0 copy-done
  11.9 2.4 %collective-permute-start.2 = (s32[8]{0:T(128)S(1)}, s32[8]{0:T(128)S(1)}, u32[]{:S(2)}, u32[]{:S(2)}) collective-permute-start(s32[8]{0:T(128)S(1)} %copy-done), channel_id=1, source_target_pairs={{0,9},{1,8},{2,11},{3,10},{4,13},{5,12},{6,15},{7,14},{8,1},{9,0},... | collective-permute-start | bytes 104 | tf_op jit(solution)/shard_map/ppermute | solution.py:166
  14.4 0.0 collective-permute-start.1
  14.4 0.5 collective-permute-start
  14.9 3.8 %collective-permute-done.2.refs_3_ = s32[8]{0:T(128)S(1)} collective-permute-done((s32[8]{0:T(128)S(1)}, s32[8]{0:T(128)S(1)}, u32[]{:S(2)}, u32[]{:S(2)}) %collective-permute-start.2) | collective-permute-done | bytes 64 | tf_op jit(solution)/shard_map/ppermute | solution.py:166
  18.7 0.0 collective-permute-done.1.refs_2_
  18.7 0.0 collective-permute-done.refs_1_
  18.7 0.0 copy-start.3
  18.7 3.1 %all-to-all-done = bf16[32,24,256]{2,1,0:T(8,128)(2,1)S(1)} async-done(((bf16[32,24,256]{2,1,0:T(8,128)(2,1)}), bf16[32,24,256]{2,1,0:T(8,128)(2,1)S(1)}, u32[]{:S(2)}, u32[]{:S(2)}) %all-to-all-start) | async-done | bytes 393248 | tf_op jit(solution)/shard_map/all_to_all | solution.py:153
  21.8 0.0 copy-done.1
  21.8 1.4 %moments.1 = (f32[384,128]{1,0:T(8,128)S(1)}, bf16[384,128]{1,0:T(8,128)(2,1)S(1)}) custom-call(s32[8]{0:T(128)} %refs_0_.3, s32[8]{0:T(128)} %copy-done.3, s32[8]{0:T(128)} %copy-done.2, s32[8]{0:T(128)} %copy-done.1, bf16[768,256]{1,0:T(8,128)(2,1)S(1)} %bitcast.10), custom_call_target="tpu_custom_call" | custom-call | tf_op jit(solution)/shard_map/moments/pallas_call | solution.py:214
  23.2 2.1 %collective-permute-start.3 = (bf16[384,128]{1,0:T(8,128)(2,1)S(1)}, bf16[384,128]{1,0:T(8,128)(2,1)S(1)}, u32[]{:S(2)}, u32[]{:S(2)}) collective-permute-start(bf16[384,128]{1,0:T(8,128)(2,1)S(1)} %get-tuple-element.16), channel_id=1, source_target_pairs={{0,8},{1,9},{2,10},{3,11},{4,12},{5,13},{6,14},{7,15},{8,0},{9,1},... | collective-permute-start | bytes 294920 | tf_op jit(solution)/shard_map/ppermute | solution.py:166
  25.3 0.9 %collective-permute-done.3.far_ref = bf16[384,128]{1,0:T(8,128)(2,1)S(1)} collective-permute-done((bf16[384,128]{1,0:T(8,128)(2,1)S(1)}, bf16[384,128]{1,0:T(8,128)(2,1)S(1)}, u32[]{:S(2)}, u32[]{:S(2)}) %collective-permute-start.3) | collective-permute-done | bytes 98336 | tf_op jit(solution)/shard_map/ppermute | solution.py:166
  26.2 3.1 %collective-permute-start.4 = (bf16[384,128]{1,0:T(8,128)(2,1)S(1)}, bf16[384,128]{1,0:T(8,128)(2,1)S(1)}, u32[]{:S(2)}, u32[]{:S(2)}) collective-permute-start(bf16[384,128]{1,0:T(8,128)(2,1)S(1)} %get-tuple-element.18), channel_id=1, source_target_pairs={{0,2},{1,3},{2,0},{3,1},{4,6},{5,7},{6,4},{7,5},{8,10},{9,11},{10,... | collective-permute-start | bytes 294920 | tf_op jit(solution)/shard_map/ppermute | solution.py:166
  29.3 5.3 %collective-permute-done.4.far_ref = bf16[384,128]{1,0:T(8,128)(2,1)S(1)} collective-permute-done((bf16[384,128]{1,0:T(8,128)(2,1)S(1)}, bf16[384,128]{1,0:T(8,128)(2,1)S(1)}, u32[]{:S(2)}, u32[]{:S(2)}) %collective-permute-start.4) | collective-permute-done | bytes 98336 | tf_op jit(solution)/shard_map/ppermute | solution.py:166
  34.6 2.6 %collective-permute-start.5 = (bf16[384,128]{1,0:T(8,128)(2,1)S(1)}, bf16[384,128]{1,0:T(8,128)(2,1)S(1)}, u32[]{:S(2)}, u32[]{:S(2)}) collective-permute-start(bf16[384,128]{1,0:T(8,128)(2,1)S(1)} %get-tuple-element.20), channel_id=1, source_target_pairs={{0,6},{1,7},{2,4},{3,5},{4,2},{5,3},{6,0},{7,1},{8,14},{9,15},{10,... | collective-permute-start | bytes 294920 | tf_op jit(solution)/shard_map/ppermute | solution.py:166
  37.3 3.6 %collective-permute-done.5.far_ref = bf16[384,128]{1,0:T(8,128)(2,1)S(1)} collective-permute-done((bf16[384,128]{1,0:T(8,128)(2,1)S(1)}, bf16[384,128]{1,0:T(8,128)(2,1)S(1)}, u32[]{:S(2)}, u32[]{:S(2)}) %collective-permute-start.5) | collective-permute-done | bytes 98336 | tf_op jit(solution)/shard_map/ppermute | solution.py:166
  40.8 1.7 %collective-permute-start.6 = (bf16[384,128]{1,0:T(8,128)(2,1)S(1)}, bf16[384,128]{1,0:T(8,128)(2,1)S(1)}, u32[]{:S(2)}, u32[]{:S(2)}) collective-permute-start(bf16[384,128]{1,0:T(8,128)(2,1)S(1)} %last_add.1.refs_5_), channel_id=1, source_target_pairs={{0,8},{1,9},{2,10},{3,11},{4,12},{5,13},{6,14},{7,15},{8,0},{9,1},... | collective-permute-start | bytes 294920 | tf_op jit(solution)/shard_map/ppermute | solution.py:166
  42.5 0.9 %collective-permute-done.6.refs_6_ = bf16[384,128]{1,0:T(8,128)(2,1)S(1)} collective-permute-done((bf16[384,128]{1,0:T(8,128)(2,1)S(1)}, bf16[384,128]{1,0:T(8,128)(2,1)S(1)}, u32[]{:S(2)}, u32[]{:S(2)}) %collective-permute-start.6) | collective-permute-done | bytes 98336 | tf_op jit(solution)/shard_map/ppermute | solution.py:166
  43.5 2.2 %apply.1 = bf16[768,128]{1,0:T(8,128)(2,1)S(1)} custom-call(s32[8]{0:T(128)} %refs_0_.3, s32[8]{0:T(128)} %copy-done.3, s32[8]{0:T(128)} %copy-done.2, s32[8]{0:T(128)} %copy-done.1, bf16[768,256]{1,0:T(8,128)(2,1)S(1)} %bitcast.11, bf16[384,128]{1,0:T(8,128)(2,1)S(1)} %last_add.1.refs_5_, bf16[384,128]{1,0:T(8,128)(2,1)S(1)} %collective-permute-done.6.refs_6_), custom_call_target="tpu_custom_call" | custom-call | tf_op jit(solution)/shard_map/apply/pallas_call | solution.py:245
  45.7 12.9 %all_to_all.10 = bf16[32,24,128]{2,1,0:T(8,128)(2,1)S(1)} all-to-all(bf16[32,24,128]{2,1,0:T(8,128)(2,1)S(1)} %bitcast.12), channel_id=1, replica_groups={{0,1,16,17,32,33,48,49,64,65,80,81,96,97,112,113,128,129,144,145,160,16..., dimensions={0} | all-to-all | bytes 393216 | tf_op jit(solution)/shard_map/all_to_all | solution.py:153
  58.6 0.8 %finish.1 = bf16[128,128]{1,0:T(8,128)(2,1)} custom-call(bf16[128,768]{1,0:T(8,128)(2,1)S(1)} %get-tuple-element.13.persons_ref, bf16[768,128]{1,0:T(8,128)(2,1)S(1)} %bitcast.13), custom_call_target="tpu_custom_call" | custom-call | tf_op jit(solution)/shard_map/finish/pallas_call | solution.py:254
  (8 shorter events, 0.1 us)
Async XLA Ops:
  2.6 9.4 %copy-start = (s32[8]{0:T(128)S(1)}, s32[8]{0:T(128)}, u32[]{:S(2)}) copy-start(s32[8]{0:T(128)} %refs_0_.3) | copy-start | bytes 100
  2.6 19.3 %all-to-all-start = ((bf16[32,24,256]{2,1,0:T(8,128)(2,1)}), bf16[32,24,256]{2,1,0:T(8,128)(2,1)S(1)}, u32[]{:S(2)}, u32[]{:S(2)}) async-start(bf16[32,24,256]{2,1,0:T(8,128)(2,1)} %bitcast.6), calls=%async_computation | async-start | bytes 786432 | tf_op jit(solution)/shard_map/all_to_all | solution.py:153
  11.9 6.8 %collective-permute-start.2 = (s32[8]{0:T(128)S(1)}, s32[8]{0:T(128)S(1)}, u32[]{:S(2)}, u32[]{:S(2)}) collective-permute-start(s32[8]{0:T(128)S(1)} %copy-done), channel_id=1, source_target_pairs={{0,9},{1,8},{2,11},{3,10},{4,13},{5,12},{6,15},{7,14},{8,1},{9,0},... | collective-permute-start | bytes 104 | tf_op jit(solution)/shard_map/ppermute | solution.py:166
  14.4 4.3 %collective-permute-start.1 = (s32[8]{0:T(128)S(1)}, s32[8]{0:T(128)S(1)}, u32[]{:S(2)}, u32[]{:S(2)}) collective-permute-start(s32[8]{0:T(128)S(1)} %copy-done), channel_id=1, source_target_pairs={{0,1},{1,0},{2,3},{3,2},{4,5},{5,4},{6,7},{7,6},{8,9},{9,8},{10,11... | collective-permute-start | bytes 104 | tf_op jit(solution)/shard_map/ppermute | solution.py:166
  14.4 4.3 %collective-permute-start = (s32[8]{0:T(128)S(1)}, s32[8]{0:T(128)S(1)}, u32[]{:S(2)}, u32[]{:S(2)}) collective-permute-start(s32[8]{0:T(128)S(1)} %copy-done), channel_id=1, source_target_pairs={{0,8},{1,9},{2,10},{3,11},{4,12},{5,13},{6,14},{7,15},{8,0},{9,1},... | collective-permute-start | bytes 104 | tf_op jit(solution)/shard_map/ppermute | solution.py:166
  18.7 3.1 %copy-start.1 = (s32[8]{0:T(128)}, s32[8]{0:T(128)S(1)}, u32[]{:S(2)}) copy-start(s32[8]{0:T(128)S(1)} %collective-permute-done.2.refs_3_) | copy-start | bytes 100
  18.7 3.1 %copy-start.2 = (s32[8]{0:T(128)}, s32[8]{0:T(128)S(1)}, u32[]{:S(2)}) copy-start(s32[8]{0:T(128)S(1)} %collective-permute-done.1.refs_2_) | copy-start | bytes 100
  18.7 3.1 %copy-start.3 = (s32[8]{0:T(128)}, s32[8]{0:T(128)S(1)}, u32[]{:S(2)}) copy-start(s32[8]{0:T(128)S(1)} %collective-permute-done.refs_1_) | copy-start | bytes 100
  23.2 3.0 %collective-permute-start.3 = (bf16[384,128]{1,0:T(8,128)(2,1)S(1)}, bf16[384,128]{1,0:T(8,128)(2,1)S(1)}, u32[]{:S(2)}, u32[]{:S(2)}) collective-permute-start(bf16[384,128]{1,0:T(8,128)(2,1)S(1)} %get-tuple-element.16), channel_id=1, source_target_pairs={{0,8},{1,9},{2,10},{3,11},{4,12},{5,13},{6,14},{7,15},{8,0},{9,1},... | collective-permute-start | bytes 294920 | tf_op jit(solution)/shard_map/ppermute | solution.py:166
  26.2 8.4 %collective-permute-start.4 = (bf16[384,128]{1,0:T(8,128)(2,1)S(1)}, bf16[384,128]{1,0:T(8,128)(2,1)S(1)}, u32[]{:S(2)}, u32[]{:S(2)}) collective-permute-start(bf16[384,128]{1,0:T(8,128)(2,1)S(1)} %get-tuple-element.18), channel_id=1, source_target_pairs={{0,2},{1,3},{2,0},{3,1},{4,6},{5,7},{6,4},{7,5},{8,10},{9,11},{10,... | collective-permute-start | bytes 294920 | tf_op jit(solution)/shard_map/ppermute | solution.py:166
  34.6 6.2 %collective-permute-start.5 = (bf16[384,128]{1,0:T(8,128)(2,1)S(1)}, bf16[384,128]{1,0:T(8,128)(2,1)S(1)}, u32[]{:S(2)}, u32[]{:S(2)}) collective-permute-start(bf16[384,128]{1,0:T(8,128)(2,1)S(1)} %get-tuple-element.20), channel_id=1, source_target_pairs={{0,6},{1,7},{2,4},{3,5},{4,2},{5,3},{6,0},{7,1},{8,14},{9,15},{10,... | collective-permute-start | bytes 294920 | tf_op jit(solution)/shard_map/ppermute | solution.py:166
  40.8 2.6 %collective-permute-start.6 = (bf16[384,128]{1,0:T(8,128)(2,1)S(1)}, bf16[384,128]{1,0:T(8,128)(2,1)S(1)}, u32[]{:S(2)}, u32[]{:S(2)}) collective-permute-start(bf16[384,128]{1,0:T(8,128)(2,1)S(1)} %last_add.1.refs_5_), channel_id=1, source_target_pairs={{0,8},{1,9},{2,10},{3,11},{4,12},{5,13},{6,14},{7,15},{8,0},{9,1},... | collective-permute-start | bytes 294920 | tf_op jit(solution)/shard_map/ppermute | solution.py:166

commit v5 on v4

--- a/solution.py
+++ b/solution.py
@@ -76,30 +76,60 @@
     persons_ref[...] = matmul_nt(person_hot, place).astype(BF16)
 
 
-def place_of(tile, loc_refs):
-    mine, sibling, neighbour, diagonal = loc_refs
+def stamp_kernel(slots, pop_count, mine_ref, sibling_ref, send_ref, out_ref):
+    rows = send_ref.shape[0]
+    capacity = rows // pop_count
+    shape = (capacity, 128)
     core = lax.axis_index("pop") & 1
-    parity = lax.axis_index("site") & 1
-    place = jnp.zeros(tile.shape, jnp.int32)
-    for t in range(TILES):
-        same = jnp.where(core == parity, mine[t], sibling[t])
-        other = jnp.where(core == parity, neighbour[t], diagonal[t])
-        place = jnp.where(tile == t, jnp.where(parity == 0, same, other), place)
-        place = jnp.where(tile == TILES + t, jnp.where(parity == 0, other, same), place)
-    return place ^ (HALF * core)
-
-
-def moment_kernel(slots, *refs):
-    loc_refs = refs[:4]
-    got_ref, keep_ref, give_ref = refs[4:]
+    lane = iota(shape, 1)
+    inside = (lane >= slots + TILES) & (lane < slots + 2 * TILES)
+    first = jnp.where(core == 0, mine_ref[...], sibling_ref[...]).astype(F32)
+    second = jnp.where(core == 0, sibling_ref[...], mine_ref[...]).astype(F32)
+    for owner in range(pop_count):
+        part = pl.ds(owner * capacity, capacity)
+        stamp = jnp.broadcast_to(second if owner % 2 else first, shape)
+        old = send_ref[part, :128].astype(F32)
+        out_ref[part, :128] = jnp.where(inside, stamp, old).astype(BF16)
+    out_ref[:, 128:] = send_ref[:, 128:]
+
+
+def masked_moments(weights, place, panel, locations):
+    masked = [jnp.where(place == l, weights, 0.0).astype(BF16) for l in locations]
+    return matmul(jnp.concatenate(masked, axis=0), panel)
+
+
+def give_kernel(slots, pop_count, got_ref, give_ref, flipped_ref, place_ref):
+    rows = got_ref.shape[0]
     unit = as_bf16(iota((128, 128), 0) == iota((128, 128), 1))
     flipped = matmul_nt(unit, got_ref[:, :128])
-    place = place_of(flipped[slots : slots + 1, :].astype(jnp.int32), loc_refs)
+    tile = flipped[slots : slots + 1, :]
+    table = flipped[slots + TILES : slots + 2 * TILES, :]
+    capacity = rows // pop_count
+    pop = lax.axis_index("pop")
+    start = (pop - (pop & 1)) * capacity
+    column = iota((TILES, rows), 1)
+    even = jnp.sum(jnp.where(column == start, table, 0.0), axis=1, keepdims=True)
+    odd = jnp.sum(jnp.where(column == start + capacity, table, 0.0), axis=1, keepdims=True)
+    line = iota((TILES, rows), 0).astype(F32)
+    chosen = jnp.where(tile == line, even, jnp.where(tile == line + TILES, odd, 0.0))
+    place = jnp.sum(chosen, axis=0, keepdims=True).astype(jnp.int32) ^ (HALF * (pop & 1))
     weights = flipped[:slots, :]
-    masked = [jnp.where(place == l, weights, 0.0).astype(BF16) for l in range(LOCATIONS)]
-    moment = matmul(jnp.concatenate(masked, axis=0), got_ref[:, 128:])
-    keep_ref[...] = moment[: HALF * slots]
-    give_ref[...] = moment[HALF * slots :].astype(BF16)
+    panel = got_ref[:, 128:]
+    give_ref[...] = masked_moments(weights, place, panel, range(HALF, LOCATIONS)).astype(BF16)
+    flipped_ref[...] = weights.astype(BF16)
+    place_ref[...] = jnp.broadcast_to(place, place_ref.shape).astype(F32)
+
+
+def keep_kernel(flipped_ref, place_ref, got_ref, keep_ref):
+    weights = flipped_ref[...].astype(F32)
+    place = place_ref[0:1, :].astype(jnp.int32)
+    keep_ref[...] = masked_moments(weights, place, got_ref[:, 128:], range(HALF))
+
+
+def columns_kernel(slots, place_ref, columns_ref):
+    place = jnp.transpose(place_ref[...])[:, 0:1]
+    inside = iota(columns_ref.shape, 1) < slots
+    columns_ref[...] = jnp.where(inside, place, -1.0).astype(BF16)
 
 
 def add_kernel(own_ref, far_ref, sum_ref, give_ref):
@@ -112,22 +142,29 @@
     give_ref[...] = (own_ref[...] + far_ref[...].astype(F32)).astype(BF16)
 
 
-def apply_kernel(slots, *refs):
-    loc_refs = refs[:4]
-    got_ref, own_ref, other_ref, result_ref, wide_ref = refs[4:]
-    rows = got_ref.shape[0]
-    place = place_of(got_ref[:, slots : slots + 1].astype(F32).astype(jnp.int32), loc_refs)
-    for l in range(LOCATIONS):
-        half_ref = own_ref if l < HALF else other_ref
-        wide_ref[pl.ds(l * 128, slots), :] = half_ref[pl.ds(l % HALF * slots, slots), :]
+def widen(slots, half_ref, wide_ref):
+    for l in range(HALF):
+        wide_ref[pl.ds(l * 128, slots), :] = half_ref[pl.ds(l * slots, slots), :]
         wide_ref[pl.ds(l * 128 + slots, 128 - slots), :] = jnp.zeros((128 - slots, 128), BF16)
+
+
+def masked_weights(columns_ref, got_ref, location):
     weights = got_ref[:, :128].astype(F32)
-    weights = jnp.where(iota((rows, 128), 1) < slots, weights, 0.0)
-    spread = jnp.concatenate(
-        [jnp.where(place == l, weights, 0.0).astype(BF16) for l in range(LOCATIONS)], axis=1
-    )
-    result = matmul(spread, wide_ref[...])
-    result_ref[...] = (result / slots).astype(BF16)
+    return jnp.where(columns_ref[...].astype(F32) == location, weights, 0.0).astype(BF16)
+
+
+def own_kernel(slots, columns_ref, got_ref, own_ref, part_ref, spread_ref, wide_ref):
+    widen(slots, own_ref, wide_ref)
+    spread = [masked_weights(columns_ref, got_ref, l) for l in range(HALF)]
+    part_ref[...] = matmul(jnp.concatenate(spread, axis=1), wide_ref[...])
+    for l in range(HALF):
+        spread_ref[:, l * 128 : (l + 1) * 128] = masked_weights(columns_ref, got_ref, HALF + l)
+
+
+def other_kernel(slots, spread_ref, other_ref, part_ref, result_ref, wide_ref):
+    widen(slots, other_ref, wide_ref)
+    result = part_ref[...] + matmul(spread_ref[...], wide_ref[...])
+    result_ref[...] = (result * (1.0 / slots)).astype(BF16)
 
 
 def finish_kernel(persons_ref, results_ref, out_ref):
@@ -136,6 +173,20 @@
 
 def vmem(count):
     return [pl.BlockSpec(memory_space=pltpu.VMEM)] * count
+
+
+def call(kernel, name, outs, *args, scratch=(), cost=0.5):
+    return pl.pallas_call(
+        kernel,
+        out_shape=tuple(pltpu.VMEM(shape, kind) for shape, kind in outs),
+        in_specs=vmem(len(args)),
+        out_specs=tuple(vmem(len(outs))),
+        scratch_shapes=list(scratch),
+        cost_estimate=pl.CostEstimate(
+            flops=int(cost * 5e8), bytes_accessed=int(cost * 2e6), transcendentals=0
+        ),
+        name=name,
+    )(*args)
 
 
 def in_vmem(array):
@@ -184,16 +235,13 @@
     capacity = visits // pop_count * 3 // 2
     rows = pop_count * capacity
     as_row = lambda x: x.reshape(1, visits)
-    send, person_rows = pl.pallas_call(
+    place_row = lambda x: jnp.pad(x, (slots + TILES, 128 - slots - 2 * TILES)).reshape(1, 128)
+    mine = place_row(tile_loc)
+    sibling = in_vmem(swap(mine, flip, stay))
+    send, person_rows = call(
         lambda *refs: pack_kernel(pop_count, *refs),
-        out_shape=(
-            pltpu.VMEM((rows, 128 + width), BF16),
-            pltpu.VMEM((persons, rows), BF16),
-        ),
-        in_specs=vmem(7),
-        out_specs=tuple(vmem(2)),
-        name="pack",
-    )(
+        "pack",
+        [((rows, 128 + width), BF16), ((persons, rows), BF16)],
         profile.T,
         panel,
         as_row(visit_person),
@@ -202,54 +250,58 @@
         as_row(visit_start),
         as_row(visit_length),
     )
-    tile_locs = [
-        tile_loc,
-        swap(tile_loc, flip, stay),
-        swap(tile_loc, stay, flip),
-        swap(tile_loc, flip, flip),
-    ]
+    (send,) = call(
+        lambda *refs: stamp_kernel(slots, pop_count, *refs),
+        "stamp",
+        [((rows, 128 + width), BF16)],
+        in_vmem(mine),
+        sibling,
+        in_vmem(send),
+    )
     got = exchange(send)
-    smem = [pl.BlockSpec(memory_space=pltpu.SMEM)] * 4
     half = (HALF * slots, width)
-    kept, given = pl.pallas_call(
-        lambda *refs: moment_kernel(slots, *refs),
-        out_shape=(pltpu.VMEM(half, F32), pltpu.VMEM(half, BF16)),
-        in_specs=smem + vmem(1),
-        out_specs=tuple(vmem(2)),
-        name="moments",
-    )(*tile_locs, got)
-    steps = (
-        (flip, stay),
-        (stay, lambda site: site ^ 2),
-        (stay, lambda site: (6 - site) % 8 if site % 2 == 0 else 8 - site),
-    )
-    for step, partners in enumerate(steps):
-        far = in_vmem(swap(given, *partners))
-        if step < 2:
-            kept, given = pl.pallas_call(
-                add_kernel,
-                out_shape=(pltpu.VMEM(half, F32), pltpu.VMEM(half, BF16)),
-                in_specs=vmem(2),
-                out_specs=tuple(vmem(2)),
-                name="add",
-            )(in_vmem(kept), far)
-        else:
-            given = pl.pallas_call(
-                last_add_kernel,
-                out_shape=pltpu.VMEM(half, BF16),
-                in_specs=vmem(2),
-                out_specs=vmem(1)[0],
-                name="last_add",
-            )(in_vmem(kept), far)
-    other = in_vmem(swap(given, flip, stay))
-    result = pl.pallas_call(
-        lambda *refs: apply_kernel(slots, *refs),
-        out_shape=pltpu.VMEM((rows, width), BF16),
-        in_specs=smem + vmem(3),
-        out_specs=vmem(1)[0],
-        scratch_shapes=[pltpu.VMEM((LOCATIONS * 128, width), BF16)],
-        name="apply",
-    )(*tile_locs, got, in_vmem(given), other)
+    give, flipped, place = call(
+        lambda *refs: give_kernel(slots, pop_count, *refs),
+        "give",
+        [(half, BF16), ((slots, rows), BF16), ((8, rows), F32)],
+        got,
+    )
+    flipped, place = in_vmem(flipped), in_vmem(place)
+    far = in_vmem(swap(give, flip, stay))
+    (keep,) = call(keep_kernel, "keep", [(half, F32)], flipped, place, got, cost=0.6)
+    keep, give = call(add_kernel, "add", [(half, F32), (half, BF16)], in_vmem(keep), far)
+    moved = swap(give, stay, lambda site: site ^ 2)
+    (columns,) = call(
+        lambda *refs: columns_kernel(slots, *refs), "columns", [((rows, 128), BF16)], place
+    )
+    moved, columns = lax.optimization_barrier((moved, columns))
+    far, columns = in_vmem(moved), in_vmem(columns)
+    keep, give = call(add_kernel, "add", [(half, F32), (half, BF16)], in_vmem(keep), far)
+    far = in_vmem(
+        swap(give, stay, lambda site: (6 - site) % 8 if site % 2 == 0 else 8 - site)
+    )
+    (give,) = call(last_add_kernel, "last_add", [(half, BF16)], in_vmem(keep), far)
+    other = in_vmem(swap(give, flip, stay))
+    wide = [pltpu.VMEM((HALF * 128, width), BF16)]
+    part, spread = call(
+        lambda *refs: own_kernel(slots, *refs),
+        "own",
+        [((rows, width), F32), ((rows, HALF * 128), BF16)],
+        columns,
+        got,
+        in_vmem(give),
+        scratch=wide,
+        cost=0.6,
+    )
+    (result,) = call(
+        lambda *refs: other_kernel(slots, *refs),
+        "other",
+        [((rows, width), BF16)],
+        in_vmem(spread),
+        other,
+        in_vmem(part),
+        scratch=wide,
+    )
     returned = exchange(result)
     return pl.pallas_call(
         finish_kernel,

time: 59.6 us -> 57.9 us (0.971)
  blocking collectives: 12.9 us -> 29.9 us
  starting transfers between devices: 21.7 us -> 12.2 us
  waiting for transfers between devices: 17.7 us -> 9.32 us
  Pallas kernels: 7.01 us -> 5.4 us
  local copies, waits for them, and re-layouts: 0.02 us -> 0.73 us
    all_to_all x1 -> x2, blocking collectives: 12.9 us -> 29.9 us  [exchange(): lax.all_to_all(blocks, ('pop', 'site'), 0, 0, tiled=True, axis_index_grou...]
    all_to_all x1 -> x0, starting transfers between devices: 9.35 us -> none  [exchange(): lax.all_to_all(blocks, ('pop', 'site'), 0, 0, tiled=True, axis_index_grou...]
    ppermute x7 -> x5, waiting for transfers between devices: 14.6 us -> 9.32 us  [swap(): return lax.ppermute(array, ('pop', 'site'), pairs)]
    all_to_all x1 -> x0, waiting for transfers between devices: 3.11 us -> none  [exchange(): lax.all_to_all(blocks, ('pop', 'site'), 0, 0, tiled=True, axis_index_grou...]
    pallas_call x6 -> x10, Pallas kernels: 6.2 us -> 4.58 us  [call(): pl.pallas_call(kernel, out_shape=tuple((pltpu.VMEM(shape, kind) for shape...]
    reshape x0 -> x1, local copies, waits for them, and re-layouts: none -> 0.73 us  [per_device(): jnp.pad(x, (slots + TILES, 128 - slots - 2 * TILES)).reshape(1, 128)]
    ppermute x7 -> x5, starting transfers between devices: 12.4 us -> 12.2 us  [swap(): return lax.ppermute(array, ('pop', 'site'), pairs)]
  transfers between devices with their start and end apart: 8 -> 5, of which waited for: 6 -> 4; matrix products, arithmetic and copies ran while one was open for 0% -> 0% of each run, Pallas kernels for 0% -> 6%
where the time goes in v5:
time: 57.9 us; the launch traced here: 57.7 us
  blocking collectives  29.9 us (52%)
  starting transfers between devices  12.2 us (21%)
  waiting for transfers between devices  9.32 us (16%)
  Pallas kernels  5.4 us (9%)
  local copies, waits for them, and re-layouts  0.73 us (1%)
    all_to_all x2, blocking collectives, exchange(): lax.all_to_all(blocks, ('pop', 'site'), 0, 0, tiled=True, axis_index_grou...  29.9 us
    ppermute x5, starting transfers between devices, swap(): return lax.ppermute(array, ('pop', 'site'), pairs)  12.2 us
    ppermute x5, waiting for transfers between devices, swap(): return lax.ppermute(array, ('pop', 'site'), pairs)  9.32 us
    pallas_call x10, Pallas kernels, call(): pl.pallas_call(kernel, out_shape=tuple((pltpu.VMEM(shape, kind) for shape...  4.58 us
  transfers between devices with their start and end apart: 5, of which 4 were waited for; matrix products, arithmetic and copies ran while one was open for 0% of the time, Pallas kernels for 6%

profile of v5, /device:TPU:1, one launch (start us, length us, event | category | flops | bytes accessed | tf_op | source)
XLA Modules:
  0.0 57.7 jit_solution(7331278186772751537)
XLA Ops:
  0.0 0.7 %pad_bitcast_fusion.refs_0_ = s32[1,128]{1,0:T(1,128)S(1)} fusion(s32[8]{0:T(128)} %param.15), kind=kLoop, calls=%fused_computation | loop fusion | bytes 544 | tf_op jit(solution)/shard_map/reshape | solution.py:238
  0.7 3.2 %collective-permute-start = (s32[1,128]{1,0:T(1,128)S(1)}, s32[1,128]{1,0:T(1,128)S(1)}, u32[]{:S(2)}, u32[]{:S(2)}) collective-permute-start(s32[1,128]{1,0:T(1,128)S(1)} %pad_bitcast_fusion.refs_0_), channel_id=1, source_target_pairs={{0,8},{1,9},{2,10},{3,11},{4,12},{5,13},{6,14},{7,15},{8,0},{9,1},... | collective-permute-start | bytes 1544 | tf_op jit(solution)/shard_map/ppermute | solution.py:217
  4.0 2.0 %pack.1 = (bf16[768,256]{1,0:T(8,128)(2,1)S(1)}, bf16[128,768]{1,0:T(8,128)(2,1)S(1)}) custom-call(bf16[96,128]{1,0:T(8,128)(2,1)} %bitcast.18, bf16[128,128]{1,0:T(8,128)(2,1)} %refs_1_.1, s32[1,512]{1,0:T(1,128)} %bitcast.19, s32[1,512]{1,0:T(1,128)} %bitcast.20, s32[1,512]{1,0:T(1,128)} %bitcast.21, s32[1,512]{1,0:T(1,128)} %bitcast.22, s32[1,512]{1,0:T(1,128)} %bitcast.23), custom_call_target="tpu_custom_call" | custom-call | flops 250000000 | bytes 1000000 | tf_op jit(solution)/shard_map/pack/pallas_call | solution.py:179
  6.0 0.0 collective-permute-done.refs_1_
  6.0 0.1 stamp.1
  6.1 16.8 %all_to_all.10 = bf16[32,24,256]{2,1,0:T(8,128)(2,1)S(1)} all-to-all(bf16[32,24,256]{2,1,0:T(8,128)(2,1)S(1)} %bitcast.17), channel_id=1, replica_groups={{0,1,16,17,32,33,48,49,64,65,80,81,96,97,112,113,128,129,144,145,160,16..., dimensions={0} | all-to-all | bytes 786432 | tf_op jit(solution)/shard_map/all_to_all | solution.py:204
  22.9 0.7 %give.1 = (bf16[384,128]{1,0:T(8,128)(2,1)S(1)}, bf16[96,768]{1,0:T(8,128)(2,1)S(1)}, f32[8,768]{1,0:T(8,128)S(1)}) custom-call(bf16[768,256]{1,0:T(8,128)(2,1)S(1)} %bitcast.14), custom_call_target="tpu_custom_call" | custom-call | flops 250000000 | bytes 1000000 | tf_op jit(solution)/shard_map/give/pallas_call | solution.py:179
  23.6 1.6 %collective-permute-start.1 = (bf16[384,128]{1,0:T(8,128)(2,1)S(1)}, bf16[384,128]{1,0:T(8,128)(2,1)S(1)}, u32[]{:S(2)}, u32[]{:S(2)}) collective-permute-start(bf16[384,128]{1,0:T(8,128)(2,1)S(1)} %get-tuple-element.22), channel_id=1, source_target_pairs={{0,8},{1,9},{2,10},{3,11},{4,12},{5,13},{6,14},{7,15},{8,0},{9,1},... | collective-permute-start | bytes 294920 | tf_op jit(solution)/shard_map/ppermute | solution.py:217
  25.2 0.3 keep.1.own_ref
  25.5 0.6 %collective-permute-done.1.far_ref = bf16[384,128]{1,0:T(8,128)(2,1)S(1)} collective-permute-done((bf16[384,128]{1,0:T(8,128)(2,1)S(1)}, bf16[384,128]{1,0:T(8,128)(2,1)S(1)}, u32[]{:S(2)}, u32[]{:S(2)}) %collective-permute-start.1) | collective-permute-done | bytes 98336 | tf_op jit(solution)/shard_map/ppermute | solution.py:217
  26.2 3.1 %collective-permute-start.2 = (bf16[384,128]{1,0:T(8,128)(2,1)S(1)}, bf16[384,128]{1,0:T(8,128)(2,1)S(1)}, u32[]{:S(2)}, u32[]{:S(2)}) collective-permute-start(bf16[384,128]{1,0:T(8,128)(2,1)S(1)} %get-tuple-element.23), channel_id=1, source_target_pairs={{0,2},{1,3},{2,0},{3,1},{4,6},{5,7},{6,4},{7,5},{8,10},{9,11},{10,... | collective-permute-start | bytes 294920 | tf_op jit(solution)/shard_map/ppermute | solution.py:217
  29.2 0.3 columns.1.refs_0_
  29.5 5.0 %collective-permute-done.2.far_ref = bf16[384,128]{1,0:T(8,128)(2,1)S(1)} collective-permute-done((bf16[384,128]{1,0:T(8,128)(2,1)S(1)}, bf16[384,128]{1,0:T(8,128)(2,1)S(1)}, u32[]{:S(2)}, u32[]{:S(2)}) %collective-permute-start.2) | collective-permute-done | bytes 98336 | tf_op jit(solution)/shard_map/ppermute | solution.py:217
  34.5 2.6 %collective-permute-start.3 = (bf16[384,128]{1,0:T(8,128)(2,1)S(1)}, bf16[384,128]{1,0:T(8,128)(2,1)S(1)}, u32[]{:S(2)}, u32[]{:S(2)}) collective-permute-start(bf16[384,128]{1,0:T(8,128)(2,1)S(1)} %get-tuple-element.28), channel_id=1, source_target_pairs={{0,6},{1,7},{2,4},{3,5},{4,2},{5,3},{6,0},{7,1},{8,14},{9,15},{10,... | collective-permute-start | bytes 294920 | tf_op jit(solution)/shard_map/ppermute | solution.py:217
  37.2 3.5 %collective-permute-done.3.far_ref = bf16[384,128]{1,0:T(8,128)(2,1)S(1)} collective-permute-done((bf16[384,128]{1,0:T(8,128)(2,1)S(1)}, bf16[384,128]{1,0:T(8,128)(2,1)S(1)}, u32[]{:S(2)}, u32[]{:S(2)}) %collective-permute-start.3) | collective-permute-done | bytes 98336 | tf_op jit(solution)/shard_map/ppermute | solution.py:217
  40.7 1.7 %collective-permute-start.4 = (bf16[384,128]{1,0:T(8,128)(2,1)S(1)}, bf16[384,128]{1,0:T(8,128)(2,1)S(1)}, u32[]{:S(2)}, u32[]{:S(2)}) collective-permute-start(bf16[384,128]{1,0:T(8,128)(2,1)S(1)} %last_add.1.refs_2_), channel_id=1, source_target_pairs={{0,8},{1,9},{2,10},{3,11},{4,12},{5,13},{6,14},{7,15},{8,0},{9,1},... | collective-permute-start | bytes 294920 | tf_op jit(solution)/shard_map/ppermute | solution.py:217
  42.4 0.8 %own.1 = (f32[768,128]{1,0:T(8,128)S(1)}, bf16[768,512]{1,0:T(8,128)(2,1)S(1)}) custom-call(bf16[768,128]{1,0:T(8,128)(2,1)S(1)} %columns.1.refs_0_, bf16[768,256]{1,0:T(8,128)(2,1)S(1)} %bitcast.16, bf16[384,128]{1,0:T(8,128)(2,1)S(1)} %last_add.1.refs_2_), custom_call_target="tpu_custom_call" | custom-call | flops 300000000 | bytes 1200000 | tf_op jit(solution)/shard_map/own/pallas_call | solution.py:179
  43.2 0.1 collective-permute-done.4.refs_1_
  43.4 0.4 other.1
  43.8 13.1 %all_to_all.11 = bf16[32,24,128]{2,1,0:T(8,128)(2,1)S(1)} all-to-all(bf16[32,24,128]{2,1,0:T(8,128)(2,1)S(1)} %bitcast.13), channel_id=1, replica_groups={{0,1,16,17,32,33,48,49,64,65,80,81,96,97,112,113,128,129,144,145,160,16..., dimensions={0} | all-to-all | bytes 393216 | tf_op jit(solution)/shard_map/all_to_all | solution.py:204
  56.8 0.8 %finish.1 = bf16[128,128]{1,0:T(8,128)(2,1)} custom-call(bf16[128,768]{1,0:T(8,128)(2,1)S(1)} %get-tuple-element.18.persons_ref, bf16[768,128]{1,0:T(8,128)(2,1)S(1)} %bitcast.12), custom_call_target="tpu_custom_call" | custom-call | tf_op jit(solution)/shard_map/finish/pallas_call | solution.py:306
  (3 shorter events, 0.1 us)
Async XLA Ops:
  0.7 5.3 %collective-permute-start = (s32[1,128]{1,0:T(1,128)S(1)}, s32[1,128]{1,0:T(1,128)S(1)}, u32[]{:S(2)}, u32[]{:S(2)}) collective-permute-start(s32[1,128]{1,0:T(1,128)S(1)} %pad_bitcast_fusion.refs_0_), channel_id=1, source_target_pairs={{0,8},{1,9},{2,10},{3,11},{4,12},{5,13},{6,14},{7,15},{8,0},{9,1},... | collective-permute-start | bytes 1544 | tf_op jit(solution)/shard_map/ppermute | solution.py:217
  23.6 2.5 %collective-permute-start.1 = (bf16[384,128]{1,0:T(8,128)(2,1)S(1)}, bf16[384,128]{1,0:T(8,128)(2,1)S(1)}, u32[]{:S(2)}, u32[]{:S(2)}) collective-permute-start(bf16[384,128]{1,0:T(8,128)(2,1)S(1)} %get-tuple-element.22), channel_id=1, source_target_pairs={{0,8},{1,9},{2,10},{3,11},{4,12},{5,13},{6,14},{7,15},{8,0},{9,1},... | collective-permute-start | bytes 294920 | tf_op jit(solution)/shard_map/ppermute | solution.py:217
  26.2 8.4 %collective-permute-start.2 = (bf16[384,128]{1,0:T(8,128)(2,1)S(1)}, bf16[384,128]{1,0:T(8,128)(2,1)S(1)}, u32[]{:S(2)}, u32[]{:S(2)}) collective-permute-start(bf16[384,128]{1,0:T(8,128)(2,1)S(1)} %get-tuple-element.23), channel_id=1, source_target_pairs={{0,2},{1,3},{2,0},{3,1},{4,6},{5,7},{6,4},{7,5},{8,10},{9,11},{10,... | collective-permute-start | bytes 294920 | tf_op jit(solution)/shard_map/ppermute | solution.py:217
  34.5 6.2 %collective-permute-start.3 = (bf16[384,128]{1,0:T(8,128)(2,1)S(1)}, bf16[384,128]{1,0:T(8,128)(2,1)S(1)}, u32[]{:S(2)}, u32[]{:S(2)}) collective-permute-start(bf16[384,128]{1,0:T(8,128)(2,1)S(1)} %get-tuple-element.28), channel_id=1, source_target_pairs={{0,6},{1,7},{2,4},{3,5},{4,2},{5,3},{6,0},{7,1},{8,14},{9,15},{10,... | collective-permute-start | bytes 294920 | tf_op jit(solution)/shard_map/ppermute | solution.py:217
  40.7 2.6 %collective-permute-start.4 = (bf16[384,128]{1,0:T(8,128)(2,1)S(1)}, bf16[384,128]{1,0:T(8,128)(2,1)S(1)}, u32[]{:S(2)}, u32[]{:S(2)}) collective-permute-start(bf16[384,128]{1,0:T(8,128)(2,1)S(1)} %last_add.1.refs_2_), channel_id=1, source_target_pairs={{0,8},{1,9},{2,10},{3,11},{4,12},{5,13},{6,14},{7,15},{8,0},{9,1},... | collective-permute-start | bytes 294920 | tf_op jit(solution)/shard_map/ppermute | solution.py:217

commit v6 on v5

--- a/solution.py
+++ b/solution.py
@@ -50,9 +50,17 @@
     finish = jnp.minimum(start + length_ref[...], slots)
     tile = (row_ref[...] >> 7) + TILES * (lax.axis_index("site") & 1)
     owner_hot = iota((pop_count, visits), 0) == owner
-    earlier = as_bf16(iota((visits, visits), 0) < iota((visits, visits), 1))
-    before = matmul(as_bf16(owner_hot), earlier)
-    position = jnp.sum(jnp.where(owner_hot, before, 0.0), axis=0, keepdims=True)
+    marks = jnp.where(owner_hot, 1.0, 0.0)
+    earlier = as_bf16(iota((128, 128), 0) < iota((128, 128), 1))
+    chunks = [marks[:, at : at + 128] for at in range(0, visits, 128)]
+    counts = matmul(jnp.concatenate(chunks, axis=0).astype(BF16), earlier)
+    seen = jnp.zeros((pop_count, 1), F32)
+    positions = []
+    for number, chunk in enumerate(chunks):
+        before = counts[number * pop_count : (number + 1) * pop_count] + seen
+        positions.append(jnp.sum(chunk * before, axis=0, keepdims=True))
+        seen = seen + jnp.sum(chunk, axis=1, keepdims=True)
+    position = jnp.concatenate(positions, axis=1)
     slot = owner * capacity + position.astype(jnp.int32)
     place = as_bf16(iota((rows, visits), 0) == slot)
     person_hot = as_bf16(iota((persons, visits), 0) == person_ref[...])
@@ -73,7 +81,7 @@
     weights = jnp.where(lane == slots, tile_at, weights)
     send_ref[:, :128] = weights.astype(BF16)
     send_ref[:, 128:] = matmul(hot, panel_ref[...]).astype(BF16)
-    persons_ref[...] = matmul_nt(person_hot, place).astype(BF16)
+    persons_ref[...] = hot
 
 
 def stamp_kernel(slots, pop_count, mine_ref, sibling_ref, send_ref, out_ref):
@@ -83,8 +91,13 @@
     core = lax.axis_index("pop") & 1
     lane = iota(shape, 1)
     inside = (lane >= slots + TILES) & (lane < slots + 2 * TILES)
-    first = jnp.where(core == 0, mine_ref[...], sibling_ref[...]).astype(F32)
-    second = jnp.where(core == 0, sibling_ref[...], mine_ref[...]).astype(F32)
+    mine, sibling = mine_ref[...].astype(F32), sibling_ref[...].astype(F32)
+    pair = (TILES, TILES)
+    mine, sibling = jnp.broadcast_to(mine, pair), jnp.broadcast_to(sibling, pair)
+    line, column = iota((TILES, 128), 0), iota((TILES, 128), 1)
+    shift = as_bf16(column == line + slots + TILES)
+    first = matmul(jnp.where(core == 0, mine, sibling).astype(BF16), shift)[0:1, :]
+    second = matmul(jnp.where(core == 0, sibling, mine).astype(BF16), shift)[0:1, :]
     for owner in range(pop_count):
         part = pl.ds(owner * capacity, capacity)
         stamp = jnp.broadcast_to(second if owner % 2 else first, shape)
@@ -132,6 +145,10 @@
     columns_ref[...] = jnp.where(inside, place, -1.0).astype(BF16)
 
 
+def flip_kernel(rows_ref, flipped_ref):
+    flipped_ref[...] = jnp.transpose(rows_ref[...].astype(F32)).astype(BF16)
+
+
 def add_kernel(own_ref, far_ref, sum_ref, give_ref):
     total = own_ref[...] + far_ref[...].astype(F32)
     sum_ref[...] = total
@@ -235,13 +252,12 @@
     capacity = visits // pop_count * 3 // 2
     rows = pop_count * capacity
     as_row = lambda x: x.reshape(1, visits)
-    place_row = lambda x: jnp.pad(x, (slots + TILES, 128 - slots - 2 * TILES)).reshape(1, 128)
-    mine = place_row(tile_loc)
+    mine = tile_loc.reshape(1, TILES)
     sibling = in_vmem(swap(mine, flip, stay))
     send, person_rows = call(
         lambda *refs: pack_kernel(pop_count, *refs),
         "pack",
-        [((rows, 128 + width), BF16), ((persons, rows), BF16)],
+        [((rows, 128 + width), BF16), ((rows, persons), BF16)],
         profile.T,
         panel,
         as_row(visit_person),
@@ -254,7 +270,7 @@
         lambda *refs: stamp_kernel(slots, pop_count, *refs),
         "stamp",
         [((rows, 128 + width), BF16)],
-        in_vmem(mine),
+        mine,
         sibling,
         in_vmem(send),
     )
@@ -277,9 +293,10 @@
     moved, columns = lax.optimization_barrier((moved, columns))
     far, columns = in_vmem(moved), in_vmem(columns)
     keep, give = call(add_kernel, "add", [(half, F32), (half, BF16)], in_vmem(keep), far)
-    far = in_vmem(
-        swap(give, stay, lambda site: (6 - site) % 8 if site % 2 == 0 else 8 - site)
-    )
+    moved = swap(give, stay, lambda site: (6 - site) % 8 if site % 2 == 0 else 8 - site)
+    (person_rows,) = call(flip_kernel, "flip", [((persons, rows), BF16)], in_vmem(person_rows))
+    moved, person_rows = lax.optimization_barrier((moved, person_rows))
+    far = in_vmem(moved)
     (give,) = call(last_add_kernel, "last_add", [(half, BF16)], in_vmem(keep), far)
     other = in_vmem(swap(give, flip, stay))
     wide = [pltpu.VMEM((HALF * 128, width), BF16)]

time: 57.9 us -> 58.2 us (level)
    reshape x1 -> x0, local copies, waits for them, and re-layouts: 0.73 us -> none  [per_device(): jnp.pad(x, (slots + TILES, 128 - slots - 2 * TILES)).reshape(1, 128)]
    unnamed x0 -> x2, local copies, waits for them, and re-layouts: none -> 0.65 us
    pallas_call x10 -> x11, Pallas kernels: 4.58 us -> 5.16 us  [call(): pl.pallas_call(kernel, out_shape=tuple((pltpu.VMEM(shape, kind) for shape...]
  transfers between devices with their start and end apart: 5 -> 5, of which waited for: 4 -> 4; matrix products, arithmetic and copies ran while one was open for 0% -> 0% of each run, Pallas kernels for 6% -> 5%
where the time goes in v6:
time: 58.2 us; the launch traced here: 58 us
  blocking collectives  29.9 us (51%)
  starting transfers between devices  12.2 us (21%)
  waiting for transfers between devices  9.18 us (16%)
  Pallas kernels  5.97 us (10%)
  local copies, waits for them, and re-layouts  0.65 us (1%)
    all_to_all x2, blocking collectives, exchange(): lax.all_to_all(blocks, ('pop', 'site'), 0, 0, tiled=True, axis_index_grou...  29.9 us
    ppermute x5, starting transfers between devices, swap(): return lax.ppermute(array, ('pop', 'site'), pairs)  12.2 us
    ppermute x5, waiting for transfers between devices, swap(): return lax.ppermute(array, ('pop', 'site'), pairs)  9.18 us
    pallas_call x11, Pallas kernels, call(): pl.pallas_call(kernel, out_shape=tuple((pltpu.VMEM(shape, kind) for shape...  5.16 us
  transfers between devices with their start and end apart: 5, of which 4 were waited for; matrix products, arithmetic and copies ran while one was open for 0% of the time, Pallas kernels for 5%

profile of v6, /device:TPU:1, one launch (start us, length us, event | category | flops | bytes accessed | tf_op | source)
XLA Modules:
  0.0 58.0 jit_solution(12922243079676491755)
XLA Ops:
  0.0 0.0 copy-start
  0.0 0.7 %copy-done = s32[8]{0:T(128)S(1)} copy-done((s32[8]{0:T(128)S(1)}, s32[8]{0:T(128)}, u32[]{:S(2)}) %copy-start) | copy-done | bytes 56
  0.7 3.2 %collective-permute-start = (s32[1,8]{1,0:T(1,128)S(1)}, s32[1,8]{1,0:T(1,128)S(1)}, u32[]{:S(2)}, u32[]{:S(2)}) collective-permute-start(s32[1,8]{1,0:T(1,128)S(1)} %bitcast.24), channel_id=1, source_target_pairs={{0,8},{1,9},{2,10},{3,11},{4,12},{5,13},{6,14},{7,15},{8,0},{9,1},... | collective-permute-start | bytes 104 | tf_op jit(solution)/shard_map/ppermute | solution.py:234
  3.9 1.7 %pack.1 = (bf16[768,256]{1,0:T(8,128)(2,1)S(1)}, bf16[768,128]{1,0:T(8,128)(2,1)S(1)}) custom-call(bf16[96,128]{1,0:T(8,128)(2,1)} %bitcast.17, bf16[128,128]{1,0:T(8,128)(2,1)} %refs_1_.1, s32[1,512]{1,0:T(1,128)} %bitcast.18, s32[1,512]{1,0:T(1,128)} %bitcast.19, s32[1,512]{1,0:T(1,128)} %bitcast.20, s32[1,512]{1,0:T(1,128)} %bitcast.21, s32[1,512]{1,0:T(1,128)} %bitcast.22), custom_call_target="tpu_custom_call" | custom-call | flops 250000000 | bytes 1000000 | tf_op jit(solution)/shard_map/pack/pallas_call | solution.py:196
  5.6 0.0 collective-permute-done.refs_1_
  5.6 0.9 %stamp.1 = bf16[768,256]{1,0:T(8,128)(2,1)S(1)} custom-call(s32[1,8]{1,0:T(1,128)} %bitcast.23, s32[1,8]{1,0:T(1,128)S(1)} %collective-permute-done.refs_1_, bf16[768,256]{1,0:T(8,128)(2,1)S(1)} %get-tuple-element.20.refs_2_), custom_call_target="tpu_custom_call" | custom-call | flops 250000000 | bytes 1000000 | tf_op jit(solution)/shard_map/stamp/pallas_call | solution.py:196
  6.5 16.8 %all_to_all.10 = bf16[32,24,256]{2,1,0:T(8,128)(2,1)S(1)} all-to-all(bf16[32,24,256]{2,1,0:T(8,128)(2,1)S(1)} %bitcast.16), channel_id=1, replica_groups={{0,1,16,17,32,33,48,49,64,65,80,81,96,97,112,113,128,129,144,145,160,16..., dimensions={0} | all-to-all | bytes 786432 | tf_op jit(solution)/shard_map/all_to_all | solution.py:221
  23.3 0.7 %give.1 = (bf16[384,128]{1,0:T(8,128)(2,1)S(1)}, bf16[96,768]{1,0:T(8,128)(2,1)S(1)}, f32[8,768]{1,0:T(8,128)S(1)}) custom-call(bf16[768,256]{1,0:T(8,128)(2,1)S(1)} %bitcast.13), custom_call_target="tpu_custom_call" | custom-call | flops 250000000 | bytes 1000000 | tf_op jit(solution)/shard_map/give/pallas_call | solution.py:196
  23.9 1.6 %collective-permute-start.1 = (bf16[384,128]{1,0:T(8,128)(2,1)S(1)}, bf16[384,128]{1,0:T(8,128)(2,1)S(1)}, u32[]{:S(2)}, u32[]{:S(2)}) collective-permute-start(bf16[384,128]{1,0:T(8,128)(2,1)S(1)} %get-tuple-element.23), channel_id=1, source_target_pairs={{0,8},{1,9},{2,10},{3,11},{4,12},{5,13},{6,14},{7,15},{8,0},{9,1},... | collective-permute-start | bytes 294920 | tf_op jit(solution)/shard_map/ppermute | solution.py:234
  25.5 0.3 keep.1.own_ref
  25.9 0.6 %collective-permute-done.1.far_ref = bf16[384,128]{1,0:T(8,128)(2,1)S(1)} collective-permute-done((bf16[384,128]{1,0:T(8,128)(2,1)S(1)}, bf16[384,128]{1,0:T(8,128)(2,1)S(1)}, u32[]{:S(2)}, u32[]{:S(2)}) %collective-permute-start.1) | collective-permute-done | bytes 98336 | tf_op jit(solution)/shard_map/ppermute | solution.py:234
  26.5 3.1 %collective-permute-start.2 = (bf16[384,128]{1,0:T(8,128)(2,1)S(1)}, bf16[384,128]{1,0:T(8,128)(2,1)S(1)}, u32[]{:S(2)}, u32[]{:S(2)}) collective-permute-start(bf16[384,128]{1,0:T(8,128)(2,1)S(1)} %get-tuple-element.25), channel_id=1, source_target_pairs={{0,2},{1,3},{2,0},{3,1},{4,6},{5,7},{6,4},{7,5},{8,10},{9,11},{10,... | collective-permute-start | bytes 294920 | tf_op jit(solution)/shard_map/ppermute | solution.py:234
  29.6 0.3 columns.1.refs_0_
  29.9 5.0 %collective-permute-done.2.far_ref = bf16[384,128]{1,0:T(8,128)(2,1)S(1)} collective-permute-done((bf16[384,128]{1,0:T(8,128)(2,1)S(1)}, bf16[384,128]{1,0:T(8,128)(2,1)S(1)}, u32[]{:S(2)}, u32[]{:S(2)}) %collective-permute-start.2) | collective-permute-done | bytes 98336 | tf_op jit(solution)/shard_map/ppermute | solution.py:234
  34.9 2.6 %collective-permute-start.3 = (bf16[384,128]{1,0:T(8,128)(2,1)S(1)}, bf16[384,128]{1,0:T(8,128)(2,1)S(1)}, u32[]{:S(2)}, u32[]{:S(2)}) collective-permute-start(bf16[384,128]{1,0:T(8,128)(2,1)S(1)} %get-tuple-element.27), channel_id=1, source_target_pairs={{0,6},{1,7},{2,4},{3,5},{4,2},{5,3},{6,0},{7,1},{8,14},{9,15},{10,... | collective-permute-start | bytes 294920 | tf_op jit(solution)/shard_map/ppermute | solution.py:234
  37.5 0.1 flip.1.persons_ref
  37.7 3.4 %collective-permute-done.3.far_ref = bf16[384,128]{1,0:T(8,128)(2,1)S(1)} collective-permute-done((bf16[384,128]{1,0:T(8,128)(2,1)S(1)}, bf16[384,128]{1,0:T(8,128)(2,1)S(1)}, u32[]{:S(2)}, u32[]{:S(2)}) %collective-permute-start.3) | collective-permute-done | bytes 98336 | tf_op jit(solution)/shard_map/ppermute | solution.py:234
  41.1 1.7 %collective-permute-start.4 = (bf16[384,128]{1,0:T(8,128)(2,1)S(1)}, bf16[384,128]{1,0:T(8,128)(2,1)S(1)}, u32[]{:S(2)}, u32[]{:S(2)}) collective-permute-start(bf16[384,128]{1,0:T(8,128)(2,1)S(1)} %last_add.1.refs_2_), channel_id=1, source_target_pairs={{0,8},{1,9},{2,10},{3,11},{4,12},{5,13},{6,14},{7,15},{8,0},{9,1},... | collective-permute-start | bytes 294920 | tf_op jit(solution)/shard_map/ppermute | solution.py:234
  42.8 0.8 %own.1 = (f32[768,128]{1,0:T(8,128)S(1)}, bf16[768,512]{1,0:T(8,128)(2,1)S(1)}) custom-call(bf16[768,128]{1,0:T(8,128)(2,1)S(1)} %columns.1.refs_0_, bf16[768,256]{1,0:T(8,128)(2,1)S(1)} %bitcast.15, bf16[384,128]{1,0:T(8,128)(2,1)S(1)} %last_add.1.refs_2_), custom_call_target="tpu_custom_call" | custom-call | flops 300000000 | bytes 1200000 | tf_op jit(solution)/shard_map/own/pallas_call | solution.py:196
  43.6 0.1 collective-permute-done.4.refs_1_
  43.7 0.4 other.1
  44.1 13.1 %all_to_all.11 = bf16[32,24,128]{2,1,0:T(8,128)(2,1)S(1)} all-to-all(bf16[32,24,128]{2,1,0:T(8,128)(2,1)S(1)} %bitcast.12), channel_id=1, replica_groups={{0,1,16,17,32,33,48,49,64,65,80,81,96,97,112,113,128,129,144,145,160,16..., dimensions={0} | all-to-all | bytes 393216 | tf_op jit(solution)/shard_map/all_to_all | solution.py:221
  57.2 0.8 %finish.1 = bf16[128,128]{1,0:T(8,128)(2,1)} custom-call(bf16[128,768]{1,0:T(8,128)(2,1)S(1)} %flip.1.persons_ref, bf16[768,128]{1,0:T(8,128)(2,1)S(1)} %bitcast.11), custom_call_target="tpu_custom_call" | custom-call | tf_op jit(solution)/shard_map/finish/pallas_call | solution.py:323
  (3 shorter events, 0.1 us)
Async XLA Ops:
  0.0 0.7 %copy-start = (s32[8]{0:T(128)S(1)}, s32[8]{0:T(128)}, u32[]{:S(2)}) copy-start(s32[8]{0:T(128)} %param.15) | copy-start | bytes 100
  0.7 4.9 %collective-permute-start = (s32[1,8]{1,0:T(1,128)S(1)}, s32[1,8]{1,0:T(1,128)S(1)}, u32[]{:S(2)}, u32[]{:S(2)}) collective-permute-start(s32[1,8]{1,0:T(1,128)S(1)} %bitcast.24), channel_id=1, source_target_pairs={{0,8},{1,9},{2,10},{3,11},{4,12},{5,13},{6,14},{7,15},{8,0},{9,1},... | collective-permute-start | bytes 104 | tf_op jit(solution)/shard_map/ppermute | solution.py:234
  23.9 2.5 %collective-permute-start.1 = (bf16[384,128]{1,0:T(8,128)(2,1)S(1)}, bf16[384,128]{1,0:T(8,128)(2,1)S(1)}, u32[]{:S(2)}, u32[]{:S(2)}) collective-permute-start(bf16[384,128]{1,0:T(8,128)(2,1)S(1)} %get-tuple-element.23), channel_id=1, source_target_pairs={{0,8},{1,9},{2,10},{3,11},{4,12},{5,13},{6,14},{7,15},{8,0},{9,1},... | collective-permute-start | bytes 294920 | tf_op jit(solution)/shard_map/ppermute | solution.py:234
  26.5 8.4 %collective-permute-start.2 = (bf16[384,128]{1,0:T(8,128)(2,1)S(1)}, bf16[384,128]{1,0:T(8,128)(2,1)S(1)}, u32[]{:S(2)}, u32[]{:S(2)}) collective-permute-start(bf16[384,128]{1,0:T(8,128)(2,1)S(1)} %get-tuple-element.25), channel_id=1, source_target_pairs={{0,2},{1,3},{2,0},{3,1},{4,6},{5,7},{6,4},{7,5},{8,10},{9,11},{10,... | collective-permute-start | bytes 294920 | tf_op jit(solution)/shard_map/ppermute | solution.py:234
  34.9 6.2 %collective-permute-start.3 = (bf16[384,128]{1,0:T(8,128)(2,1)S(1)}, bf16[384,128]{1,0:T(8,128)(2,1)S(1)}, u32[]{:S(2)}, u32[]{:S(2)}) collective-permute-start(bf16[384,128]{1,0:T(8,128)(2,1)S(1)} %get-tuple-element.27), channel_id=1, source_target_pairs={{0,6},{1,7},{2,4},{3,5},{4,2},{5,3},{6,0},{7,1},{8,14},{9,15},{10,... | collective-permute-start | bytes 294920 | tf_op jit(solution)/shard_map/ppermute | solution.py:234
  41.1 2.6 %collective-permute-start.4 = (bf16[384,128]{1,0:T(8,128)(2,1)S(1)}, bf16[384,128]{1,0:T(8,128)(2,1)S(1)}, u32[]{:S(2)}, u32[]{:S(2)}) collective-permute-start(bf16[384,128]{1,0:T(8,128)(2,1)S(1)} %last_add.1.refs_2_), channel_id=1, source_target_pairs={{0,8},{1,9},{2,10},{3,11},{4,12},{5,13},{6,14},{7,15},{8,0},{9,1},... | collective-permute-start | bytes 294920 | tf_op jit(solution)/shard_map/ppermute | solution.py:234

commit v7 on v6

--- a/solution.py
+++ b/solution.py
@@ -1,3 +1,5 @@
+import functools
+
 import jax
 import jax.numpy as jnp
 from jax import lax
@@ -224,22 +226,24 @@
     return in_vmem(moved.reshape(array.shape))
 
 
-def swap(array, pop_partner, site_partner):
+def swap(array, partner):
     pops, sites = lax.axis_size("pop"), lax.axis_size("site")
-    pairs = [
-        (pop * sites + site, pop_partner(pop) * sites + site_partner(site))
-        for pop in range(pops)
-        for site in range(sites)
-    ]
+    pairs = []
+    for pop in range(pops):
+        for site in range(sites):
+            far_pop, far_site = partner(pop, site)
+            pairs.append((pop * sites + site, far_pop * sites + far_site))
     return lax.ppermute(array, ("pop", "site"), pairs)
 
 
-def flip(index):
-    return index ^ 1
-
-
-def stay(index):
-    return index
+def sibling_core(pop, site):
+    return pop ^ 1, site
+
+
+def site_step(step, pop, site):
+    if (step + pop) % 2 == 0:
+        return pop, site ^ 2
+    return pop, (8 - site if site % 2 else 6 - site) % 8
 
 
 def per_device(
@@ -253,7 +257,7 @@
     rows = pop_count * capacity
     as_row = lambda x: x.reshape(1, visits)
     mine = tile_loc.reshape(1, TILES)
-    sibling = in_vmem(swap(mine, flip, stay))
+    sibling = in_vmem(swap(mine, sibling_core))
     send, person_rows = call(
         lambda *refs: pack_kernel(pop_count, *refs),
         "pack",
@@ -270,7 +274,7 @@
         lambda *refs: stamp_kernel(slots, pop_count, *refs),
         "stamp",
         [((rows, 128 + width), BF16)],
-        mine,
+        in_vmem(mine),
         sibling,
         in_vmem(send),
     )
@@ -283,22 +287,22 @@
         got,
     )
     flipped, place = in_vmem(flipped), in_vmem(place)
-    far = in_vmem(swap(give, flip, stay))
+    far = in_vmem(swap(give, sibling_core))
     (keep,) = call(keep_kernel, "keep", [(half, F32)], flipped, place, got, cost=0.6)
     keep, give = call(add_kernel, "add", [(half, F32), (half, BF16)], in_vmem(keep), far)
-    moved = swap(give, stay, lambda site: site ^ 2)
+    moved = swap(give, functools.partial(site_step, 0))
     (columns,) = call(
         lambda *refs: columns_kernel(slots, *refs), "columns", [((rows, 128), BF16)], place
     )
     moved, columns = lax.optimization_barrier((moved, columns))
     far, columns = in_vmem(moved), in_vmem(columns)
     keep, give = call(add_kernel, "add", [(half, F32), (half, BF16)], in_vmem(keep), far)
-    moved = swap(give, stay, lambda site: (6 - site) % 8 if site % 2 == 0 else 8 - site)
+    moved = swap(give, functools.partial(site_step, 1))
     (person_rows,) = call(flip_kernel, "flip", [((persons, rows), BF16)], in_vmem(person_rows))
     moved, person_rows = lax.optimization_barrier((moved, person_rows))
     far = in_vmem(moved)
     (give,) = call(last_add_kernel, "last_add", [(half, BF16)], in_vmem(keep), far)
-    other = in_vmem(swap(give, flip, stay))
+    other = in_vmem(swap(give, sibling_core))
     wide = [pltpu.VMEM((HALF * 128, width), BF16)]
     part, spread = call(
         lambda *refs: own_kernel(slots, *refs),

time: 58.2 us -> 55.7 us (0.957)
  waiting for transfers between devices: 9.18 us -> 5.99 us
  starting transfers between devices: 12.2 us -> 15.3 us
  blocking collectives: 29.9 us -> 28.2 us
  Pallas kernels: 5.97 us -> 5.29 us
    ppermute x5, waiting for transfers between devices: 9.18 us -> 5.99 us  [swap(): return lax.ppermute(array, ('pop', 'site'), pairs)]
    ppermute x5, starting transfers between devices: 12.2 us -> 15.3 us  [swap(): return lax.ppermute(array, ('pop', 'site'), pairs)]
    all_to_all x2, blocking collectives: 29.9 us -> 28.2 us  [exchange(): lax.all_to_all(blocks, ('pop', 'site'), 0, 0, tiled=True, axis_index_grou...]
    pallas_call x11, Pallas kernels: 5.16 us -> 4.48 us  [call(): pl.pallas_call(kernel, out_shape=tuple((pltpu.VMEM(shape, kind) for shape...]
  transfers between devices with their start and end apart: 5 -> 5, of which waited for: 4 -> 4; matrix products, arithmetic and copies ran while one was open for 0% -> 0% of each run, Pallas kernels for 5% -> 6%
where the time goes in v7:
time: 55.7 us; the launch traced here: 55.5 us
  blocking collectives  28.2 us (51%)
  starting transfers between devices  15.3 us (27%)
  waiting for transfers between devices  5.99 us (11%)
  Pallas kernels  5.29 us (9%)
  local copies, waits for them, and re-layouts  0.65 us (1%)
    all_to_all x2, blocking collectives, exchange(): lax.all_to_all(blocks, ('pop', 'site'), 0, 0, tiled=True, axis_index_grou...  28.2 us
    ppermute x5, starting transfers between devices, swap(): return lax.ppermute(array, ('pop', 'site'), pairs)  15.3 us
    ppermute x5, waiting for transfers between devices, swap(): return lax.ppermute(array, ('pop', 'site'), pairs)  5.99 us
    pallas_call x11, Pallas kernels, call(): pl.pallas_call(kernel, out_shape=tuple((pltpu.VMEM(shape, kind) for shape...  4.48 us
  transfers between devices with their start and end apart: 5, of which 4 were waited for; matrix products, arithmetic and copies ran while one was open for 0% of the time, Pallas kernels for 6%

profile of v7, /device:TPU:1, one launch (start us, length us, event | category | flops | bytes accessed | tf_op | source)
XLA Modules:
  0.0 55.5 jit_solution(7672794974680978829)
XLA Ops:
  0.0 0.0 copy-start
  0.0 0.7 %copy-done = s32[8]{0:T(128)S(1)} copy-done((s32[8]{0:T(128)S(1)}, s32[8]{0:T(128)}, u32[]{:S(2)}) %copy-start) | copy-done | bytes 56
  0.7 3.2 %collective-permute-start = (s32[1,8]{1,0:T(1,128)S(1)}, s32[1,8]{1,0:T(1,128)S(1)}, u32[]{:S(2)}, u32[]{:S(2)}) collective-permute-start(s32[1,8]{1,0:T(1,128)S(1)} %bitcast.17), channel_id=1, source_target_pairs={{0,8},{1,9},{2,10},{3,11},{4,12},{5,13},{6,14},{7,15},{8,0},{9,1},... | collective-permute-start | bytes 104 | tf_op jit(solution)/shard_map/ppermute | solution.py:236
  3.9 1.7 %pack.1 = (bf16[768,256]{1,0:T(8,128)(2,1)S(1)}, bf16[768,128]{1,0:T(8,128)(2,1)S(1)}) custom-call(bf16[96,128]{1,0:T(8,128)(2,1)} %bitcast.19, bf16[128,128]{1,0:T(8,128)(2,1)} %refs_1_.1, s32[1,512]{1,0:T(1,128)} %bitcast.20, s32[1,512]{1,0:T(1,128)} %bitcast.21, s32[1,512]{1,0:T(1,128)} %bitcast.22, s32[1,512]{1,0:T(1,128)} %bitcast.23, s32[1,512]{1,0:T(1,128)} %bitcast.24), custom_call_target="tpu_custom_call" | custom-call | flops 250000000 | bytes 1000000 | tf_op jit(solution)/shard_map/pack/pallas_call | solution.py:198
  5.6 0.0 collective-permute-done.refs_1_
  5.6 0.2 stamp.1
  5.8 16.8 %all_to_all.10 = bf16[32,24,256]{2,1,0:T(8,128)(2,1)S(1)} all-to-all(bf16[32,24,256]{2,1,0:T(8,128)(2,1)S(1)} %bitcast.16), channel_id=1, replica_groups={{0,1,16,17,32,33,48,49,64,65,80,81,96,97,112,113,128,129,144,145,160,16..., dimensions={0} | all-to-all | bytes 786432 | tf_op jit(solution)/shard_map/all_to_all | solution.py:223
  22.6 0.7 %give.1 = (bf16[384,128]{1,0:T(8,128)(2,1)S(1)}, bf16[96,768]{1,0:T(8,128)(2,1)S(1)}, f32[8,768]{1,0:T(8,128)S(1)}) custom-call(bf16[768,256]{1,0:T(8,128)(2,1)S(1)} %bitcast.13), custom_call_target="tpu_custom_call" | custom-call | flops 250000000 | bytes 1000000 | tf_op jit(solution)/shard_map/give/pallas_call | solution.py:198
  23.3 1.6 %collective-permute-start.1 = (bf16[384,128]{1,0:T(8,128)(2,1)S(1)}, bf16[384,128]{1,0:T(8,128)(2,1)S(1)}, u32[]{:S(2)}, u32[]{:S(2)}) collective-permute-start(bf16[384,128]{1,0:T(8,128)(2,1)S(1)} %get-tuple-element.23), channel_id=1, source_target_pairs={{0,8},{1,9},{2,10},{3,11},{4,12},{5,13},{6,14},{7,15},{8,0},{9,1},... | collective-permute-start | bytes 294920 | tf_op jit(solution)/shard_map/ppermute | solution.py:236
  24.9 0.3 keep.1.own_ref
  25.2 0.6 %collective-permute-done.1.far_ref = bf16[384,128]{1,0:T(8,128)(2,1)S(1)} collective-permute-done((bf16[384,128]{1,0:T(8,128)(2,1)S(1)}, bf16[384,128]{1,0:T(8,128)(2,1)S(1)}, u32[]{:S(2)}, u32[]{:S(2)}) %collective-permute-start.1) | collective-permute-done | bytes 98336 | tf_op jit(solution)/shard_map/ppermute | solution.py:236
  25.8 5.2 %collective-permute-start.2 = (bf16[384,128]{1,0:T(8,128)(2,1)S(1)}, bf16[384,128]{1,0:T(8,128)(2,1)S(1)}, u32[]{:S(2)}, u32[]{:S(2)}) collective-permute-start(bf16[384,128]{1,0:T(8,128)(2,1)S(1)} %get-tuple-element.25), channel_id=1, source_target_pairs={{0,2},{1,3},{2,0},{3,1},{4,6},{5,7},{6,4},{7,5},{8,14},{9,15},{10,... | collective-permute-start | bytes 294920 | tf_op jit(solution)/shard_map/ppermute | solution.py:236
  31.0 0.3 columns.1.refs_0_
  31.3 2.3 %collective-permute-done.2.far_ref = bf16[384,128]{1,0:T(8,128)(2,1)S(1)} collective-permute-done((bf16[384,128]{1,0:T(8,128)(2,1)S(1)}, bf16[384,128]{1,0:T(8,128)(2,1)S(1)}, u32[]{:S(2)}, u32[]{:S(2)}) %collective-permute-start.2) | collective-permute-done | bytes 98336 | tf_op jit(solution)/shard_map/ppermute | solution.py:236
  33.7 1.8 %collective-permute-start.3 = (bf16[384,128]{1,0:T(8,128)(2,1)S(1)}, bf16[384,128]{1,0:T(8,128)(2,1)S(1)}, u32[]{:S(2)}, u32[]{:S(2)}) collective-permute-start(bf16[384,128]{1,0:T(8,128)(2,1)S(1)} %get-tuple-element.27), channel_id=1, source_target_pairs={{0,6},{1,7},{2,4},{3,5},{4,2},{5,3},{6,0},{7,1},{8,10},{9,11},{10,... | collective-permute-start | bytes 294920 | tf_op jit(solution)/shard_map/ppermute | solution.py:236
  35.5 0.1 flip.1.persons_ref
  35.7 2.9 %collective-permute-done.3.far_ref = bf16[384,128]{1,0:T(8,128)(2,1)S(1)} collective-permute-done((bf16[384,128]{1,0:T(8,128)(2,1)S(1)}, bf16[384,128]{1,0:T(8,128)(2,1)S(1)}, u32[]{:S(2)}, u32[]{:S(2)}) %collective-permute-start.3) | collective-permute-done | bytes 98336 | tf_op jit(solution)/shard_map/ppermute | solution.py:236
  38.6 3.4 %collective-permute-start.4 = (bf16[384,128]{1,0:T(8,128)(2,1)S(1)}, bf16[384,128]{1,0:T(8,128)(2,1)S(1)}, u32[]{:S(2)}, u32[]{:S(2)}) collective-permute-start(bf16[384,128]{1,0:T(8,128)(2,1)S(1)} %last_add.1.refs_2_), channel_id=1, source_target_pairs={{0,8},{1,9},{2,10},{3,11},{4,12},{5,13},{6,14},{7,15},{8,0},{9,1},... | collective-permute-start | bytes 294920 | tf_op jit(solution)/shard_map/ppermute | solution.py:236
  42.0 0.8 %own.1 = (f32[768,128]{1,0:T(8,128)S(1)}, bf16[768,512]{1,0:T(8,128)(2,1)S(1)}) custom-call(bf16[768,128]{1,0:T(8,128)(2,1)S(1)} %columns.1.refs_0_, bf16[768,256]{1,0:T(8,128)(2,1)S(1)} %bitcast.15, bf16[384,128]{1,0:T(8,128)(2,1)S(1)} %last_add.1.refs_2_), custom_call_target="tpu_custom_call" | custom-call | flops 300000000 | bytes 1200000 | tf_op jit(solution)/shard_map/own/pallas_call | solution.py:198
  42.8 0.1 collective-permute-done.4.refs_1_
  42.9 0.4 other.1
  43.3 11.4 %all_to_all.11 = bf16[32,24,128]{2,1,0:T(8,128)(2,1)S(1)} all-to-all(bf16[32,24,128]{2,1,0:T(8,128)(2,1)S(1)} %bitcast.12), channel_id=1, replica_groups={{0,1,16,17,32,33,48,49,64,65,80,81,96,97,112,113,128,129,144,145,160,16..., dimensions={0} | all-to-all | bytes 393216 | tf_op jit(solution)/shard_map/all_to_all | solution.py:223
  54.7 0.8 %finish.1 = bf16[128,128]{1,0:T(8,128)(2,1)} custom-call(bf16[128,768]{1,0:T(8,128)(2,1)S(1)} %flip.1.persons_ref, bf16[768,128]{1,0:T(8,128)(2,1)S(1)} %bitcast.11), custom_call_target="tpu_custom_call" | custom-call | tf_op jit(solution)/shard_map/finish/pallas_call | solution.py:327
  (3 shorter events, 0.1 us)
Async XLA Ops:
  0.0 0.7 %copy-start = (s32[8]{0:T(128)S(1)}, s32[8]{0:T(128)}, u32[]{:S(2)}) copy-start(s32[8]{0:T(128)} %param.15) | copy-start | bytes 100
  0.7 4.9 %collective-permute-start = (s32[1,8]{1,0:T(1,128)S(1)}, s32[1,8]{1,0:T(1,128)S(1)}, u32[]{:S(2)}, u32[]{:S(2)}) collective-permute-start(s32[1,8]{1,0:T(1,128)S(1)} %bitcast.17), channel_id=1, source_target_pairs={{0,8},{1,9},{2,10},{3,11},{4,12},{5,13},{6,14},{7,15},{8,0},{9,1},... | collective-permute-start | bytes 104 | tf_op jit(solution)/shard_map/ppermute | solution.py:236
  23.3 2.5 %collective-permute-start.1 = (bf16[384,128]{1,0:T(8,128)(2,1)S(1)}, bf16[384,128]{1,0:T(8,128)(2,1)S(1)}, u32[]{:S(2)}, u32[]{:S(2)}) collective-permute-start(bf16[384,128]{1,0:T(8,128)(2,1)S(1)} %get-tuple-element.23), channel_id=1, source_target_pairs={{0,8},{1,9},{2,10},{3,11},{4,12},{5,13},{6,14},{7,15},{8,0},{9,1},... | collective-permute-start | bytes 294920 | tf_op jit(solution)/shard_map/ppermute | solution.py:236
  25.8 7.8 %collective-permute-start.2 = (bf16[384,128]{1,0:T(8,128)(2,1)S(1)}, bf16[384,128]{1,0:T(8,128)(2,1)S(1)}, u32[]{:S(2)}, u32[]{:S(2)}) collective-permute-start(bf16[384,128]{1,0:T(8,128)(2,1)S(1)} %get-tuple-element.25), channel_id=1, source_target_pairs={{0,2},{1,3},{2,0},{3,1},{4,6},{5,7},{6,4},{7,5},{8,14},{9,15},{10,... | collective-permute-start | bytes 294920 | tf_op jit(solution)/shard_map/ppermute | solution.py:236
  33.7 4.9 %collective-permute-start.3 = (bf16[384,128]{1,0:T(8,128)(2,1)S(1)}, bf16[384,128]{1,0:T(8,128)(2,1)S(1)}, u32[]{:S(2)}, u32[]{:S(2)}) collective-permute-start(bf16[384,128]{1,0:T(8,128)(2,1)S(1)} %get-tuple-element.27), channel_id=1, source_target_pairs={{0,6},{1,7},{2,4},{3,5},{4,2},{5,3},{6,0},{7,1},{8,10},{9,11},{10,... | collective-permute-start | bytes 294920 | tf_op jit(solution)/shard_map/ppermute | solution.py:236
  38.6 4.3 %collective-permute-start.4 = (bf16[384,128]{1,0:T(8,128)(2,1)S(1)}, bf16[384,128]{1,0:T(8,128)(2,1)S(1)}, u32[]{:S(2)}, u32[]{:S(2)}) collective-permute-start(bf16[384,128]{1,0:T(8,128)(2,1)S(1)} %last_add.1.refs_2_), channel_id=1, source_target_pairs={{0,8},{1,9},{2,10},{3,11},{4,12},{5,13},{6,14},{7,15},{8,0},{9,1},... | collective-permute-start | bytes 294920 | tf_op jit(solution)/shard_map/ppermute | solution.py:236

commit v8 on v7

--- a/solution.py
+++ b/solution.py
@@ -86,26 +86,11 @@
     persons_ref[...] = hot
 
 
-def stamp_kernel(slots, pop_count, mine_ref, sibling_ref, send_ref, out_ref):
-    rows = send_ref.shape[0]
-    capacity = rows // pop_count
-    shape = (capacity, 128)
-    core = lax.axis_index("pop") & 1
-    lane = iota(shape, 1)
-    inside = (lane >= slots + TILES) & (lane < slots + 2 * TILES)
-    mine, sibling = mine_ref[...].astype(F32), sibling_ref[...].astype(F32)
-    pair = (TILES, TILES)
-    mine, sibling = jnp.broadcast_to(mine, pair), jnp.broadcast_to(sibling, pair)
-    line, column = iota((TILES, 128), 0), iota((TILES, 128), 1)
-    shift = as_bf16(column == line + slots + TILES)
-    first = matmul(jnp.where(core == 0, mine, sibling).astype(BF16), shift)[0:1, :]
-    second = matmul(jnp.where(core == 0, sibling, mine).astype(BF16), shift)[0:1, :]
-    for owner in range(pop_count):
-        part = pl.ds(owner * capacity, capacity)
-        stamp = jnp.broadcast_to(second if owner % 2 else first, shape)
-        old = send_ref[part, :128].astype(F32)
-        out_ref[part, :128] = jnp.where(inside, stamp, old).astype(BF16)
-    out_ref[:, 128:] = send_ref[:, 128:]
+def as_column(row):
+    size = row.shape[1]
+    square = jnp.broadcast_to(row.astype(F32), (size, size))
+    diagonal = iota((size, size), 0) == iota((size, size), 1)
+    return jnp.sum(jnp.where(diagonal, square, 0.0), axis=1, keepdims=True)
 
 
 def masked_moments(weights, place, panel, locations):
@@ -113,21 +98,22 @@
     return matmul(jnp.concatenate(masked, axis=0), panel)
 
 
-def give_kernel(slots, pop_count, got_ref, give_ref, flipped_ref, place_ref):
+def give_kernel(slots, *refs):
+    mine, sibling, neighbour, diagonal = [ref[...] for ref in refs[:4]]
+    got_ref, give_ref, flipped_ref, place_ref = refs[4:]
     rows = got_ref.shape[0]
+    core = lax.axis_index("pop") & 1
+    parity = lax.axis_index("site") & 1
+    near = jnp.where(core == parity, mine, sibling)
+    far = jnp.where(core == parity, neighbour, diagonal)
+    even = as_column(jnp.where(parity == 0, near, far))
+    odd = as_column(jnp.where(parity == 0, far, near))
     unit = as_bf16(iota((128, 128), 0) == iota((128, 128), 1))
     flipped = matmul_nt(unit, got_ref[:, :128])
     tile = flipped[slots : slots + 1, :]
-    table = flipped[slots + TILES : slots + 2 * TILES, :]
-    capacity = rows // pop_count
-    pop = lax.axis_index("pop")
-    start = (pop - (pop & 1)) * capacity
-    column = iota((TILES, rows), 1)
-    even = jnp.sum(jnp.where(column == start, table, 0.0), axis=1, keepdims=True)
-    odd = jnp.sum(jnp.where(column == start + capacity, table, 0.0), axis=1, keepdims=True)
     line = iota((TILES, rows), 0).astype(F32)
     chosen = jnp.where(tile == line, even, jnp.where(tile == line + TILES, odd, 0.0))
-    place = jnp.sum(chosen, axis=0, keepdims=True).astype(jnp.int32) ^ (HALF * (pop & 1))
+    place = jnp.sum(chosen, axis=0, keepdims=True).astype(jnp.int32) ^ (HALF * core)
     weights = flipped[:slots, :]
     panel = got_ref[:, 128:]
     give_ref[...] = masked_moments(weights, place, panel, range(HALF, LOCATIONS)).astype(BF16)
@@ -256,8 +242,6 @@
     capacity = visits // pop_count * 3 // 2
     rows = pop_count * capacity
     as_row = lambda x: x.reshape(1, visits)
-    mine = tile_loc.reshape(1, TILES)
-    sibling = in_vmem(swap(mine, sibling_core))
     send, person_rows = call(
         lambda *refs: pack_kernel(pop_count, *refs),
         "pack",
@@ -270,20 +254,17 @@
         as_row(visit_start),
         as_row(visit_length),
     )
-    (send,) = call(
-        lambda *refs: stamp_kernel(slots, pop_count, *refs),
-        "stamp",
-        [((rows, 128 + width), BF16)],
-        in_vmem(mine),
-        sibling,
-        in_vmem(send),
-    )
+    mine = tile_loc.reshape(1, TILES)
+    neighbour_site = lambda pop, site: (pop, site ^ 1)
+    diagonal = lambda pop, site: (pop ^ 1, site ^ 1)
+    tables = [mine] + [swap(mine, far) for far in (sibling_core, neighbour_site, diagonal)]
     got = exchange(send)
     half = (HALF * slots, width)
     give, flipped, place = call(
-        lambda *refs: give_kernel(slots, pop_count, *refs),
+        lambda *refs: give_kernel(slots, *refs),
         "give",
         [(half, BF16), ((slots, rows), BF16), ((8, rows), F32)],
+        *[in_vmem(table) for table in tables],
         got,
     )
     flipped, place = in_vmem(flipped), in_vmem(place)

time: 55.7 us -> 55.1 us (0.989)
  blocking collectives: 28.2 us -> 11.4 us
  starting transfers between devices: 15.3 us -> 24.3 us
  waiting for transfers between devices: 5.99 us -> 12.6 us
    all_to_all x2 -> x1, blocking collectives: 28.2 us -> 11.4 us  [exchange(): lax.all_to_all(blocks, ('pop', 'site'), 0, 0, tiled=True, axis_index_grou...]
    all_to_all x0 -> x1, starting transfers between devices: none -> 9.22 us  [exchange(): lax.all_to_all(blocks, ('pop', 'site'), 0, 0, tiled=True, axis_index_grou...]
    ppermute x5 -> x7, waiting for transfers between devices: 5.99 us -> 9.52 us  [swap(): return lax.ppermute(array, ('pop', 'site'), pairs)]
    all_to_all x0 -> x1, waiting for transfers between devices: none -> 3.13 us  [exchange(): lax.all_to_all(blocks, ('pop', 'site'), 0, 0, tiled=True, axis_index_grou...]
    pallas_call x11 -> x10, Pallas kernels: 4.48 us -> 4.92 us  [call(): pl.pallas_call(kernel, out_shape=tuple((pltpu.VMEM(shape, kind) for shape...]
    ppermute x5 -> x7, starting transfers between devices: 15.3 us -> 15.1 us  [swap(): return lax.ppermute(array, ('pop', 'site'), pairs)]
  transfers between devices with their start and end apart: 5 -> 8, of which waited for: 4 -> 7; matrix products, arithmetic and copies ran while one was open for 0% -> 0% of each run, Pallas kernels for 6% -> 3%
where the time goes in v8:
time: 55.1 us; the launch traced here: 54.9 us
  starting transfers between devices  24.3 us (44%)
  waiting for transfers between devices  12.6 us (23%)
  blocking collectives  11.4 us (21%)
  Pallas kernels  5.73 us (10%)
  local copies, waits for them, and re-layouts  0.65 us (1%)
    ppermute x7, starting transfers between devices, swap(): return lax.ppermute(array, ('pop', 'site'), pairs)  15.1 us
    all_to_all x1, blocking collectives, exchange(): lax.all_to_all(blocks, ('pop', 'site'), 0, 0, tiled=True, axis_index_grou...  11.4 us
    ppermute x7, waiting for transfers between devices, swap(): return lax.ppermute(array, ('pop', 'site'), pairs)  9.52 us
    all_to_all x1, starting transfers between devices, exchange(): lax.all_to_all(blocks, ('pop', 'site'), 0, 0, tiled=True, axis_index_grou...  9.22 us
    pallas_call x10, Pallas kernels, call(): pl.pallas_call(kernel, out_shape=tuple((pltpu.VMEM(shape, kind) for shape...  4.92 us
    all_to_all x1, waiting for transfers between devices, exchange(): lax.all_to_all(blocks, ('pop', 'site'), 0, 0, tiled=True, axis_index_grou...  3.13 us
  transfers between devices with their start and end apart: 8, of which 7 were waited for; matrix products, arithmetic and copies ran while one was open for 0% of the time, Pallas kernels for 3%

profile of v8, /device:TPU:1, one launch (start us, length us, event | category | flops | bytes accessed | tf_op | source)
XLA Modules:
  0.0 54.9 jit_solution(7793100844508249701)
XLA Ops:
  0.0 2.4 %pack.1 = (bf16[768,256]{1,0:T(8,128)(2,1)}, bf16[768,128]{1,0:T(8,128)(2,1)S(1)}) custom-call(bf16[96,128]{1,0:T(8,128)(2,1)} %bitcast.20, bf16[128,128]{1,0:T(8,128)(2,1)} %refs_1_.1, s32[1,512]{1,0:T(1,128)} %bitcast.21, s32[1,512]{1,0:T(1,128)} %bitcast.22, s32[1,512]{1,0:T(1,128)} %bitcast.23, s32[1,512]{1,0:T(1,128)} %bitcast.24, s32[1,512]{1,0:T(1,128)} %bitcast.25), custom_call_target="tpu_custom_call" | custom-call | flops 250000000 | bytes 1000000 | tf_op jit(solution)/shard_map/pack/pallas_call | solution.py:184
  2.4 9.2 %all-to-all-start = ((bf16[32,24,256]{2,1,0:T(8,128)(2,1)}), bf16[32,24,256]{2,1,0:T(8,128)(2,1)S(1)}, u32[]{:S(2)}, u32[]{:S(2)}) async-start(bf16[32,24,256]{2,1,0:T(8,128)(2,1)} %bitcast.7), calls=%async_computation | async-start | bytes 786432 | tf_op jit(solution)/shard_map/all_to_all | solution.py:209
  11.7 0.6 %copy-done = s32[8]{0:T(128)S(1)} copy-done((s32[8]{0:T(128)S(1)}, s32[8]{0:T(128)}, u32[]{:S(2)}) %copy-start) | copy-done | bytes 56
  12.3 1.0 %collective-permute-start = (s32[1,8]{1,0:T(1,128)S(1)}, s32[1,8]{1,0:T(1,128)S(1)}, u32[]{:S(2)}, u32[]{:S(2)}) collective-permute-start(s32[1,8]{1,0:T(1,128)S(1)} %bitcast.16), channel_id=1, source_target_pairs={{0,8},{1,9},{2,10},{3,11},{4,12},{5,13},{6,14},{7,15},{8,0},{9,1},... | collective-permute-start | bytes 104 | tf_op jit(solution)/shard_map/ppermute | solution.py:222
  13.3 1.5 %collective-permute-start.1 = (s32[1,8]{1,0:T(1,128)S(1)}, s32[1,8]{1,0:T(1,128)S(1)}, u32[]{:S(2)}, u32[]{:S(2)}) collective-permute-start(s32[1,8]{1,0:T(1,128)S(1)} %bitcast.17), channel_id=1, source_target_pairs={{0,1},{1,0},{2,3},{3,2},{4,5},{5,4},{6,7},{7,6},{8,9},{9,8},{10,11... | collective-permute-start | bytes 104 | tf_op jit(solution)/shard_map/ppermute | solution.py:222
  14.9 2.0 %collective-permute-done.1.refs_2_ = s32[1,8]{1,0:T(1,128)S(1)} collective-permute-done((s32[1,8]{1,0:T(1,128)S(1)}, s32[1,8]{1,0:T(1,128)S(1)}, u32[]{:S(2)}, u32[]{:S(2)}) %collective-permute-start.1) | collective-permute-done | bytes 64 | tf_op jit(solution)/shard_map/ppermute | solution.py:222
  16.9 1.5 %collective-permute-done.2.refs_3_ = s32[1,8]{1,0:T(1,128)S(1)} collective-permute-done((s32[1,8]{1,0:T(1,128)S(1)}, s32[1,8]{1,0:T(1,128)S(1)}, u32[]{:S(2)}, u32[]{:S(2)}) %collective-permute-start.2) | collective-permute-done | bytes 64 | tf_op jit(solution)/shard_map/ppermute | solution.py:222
  18.4 3.1 %all-to-all-done = bf16[32,24,256]{2,1,0:T(8,128)(2,1)S(1)} async-done(((bf16[32,24,256]{2,1,0:T(8,128)(2,1)}), bf16[32,24,256]{2,1,0:T(8,128)(2,1)S(1)}, u32[]{:S(2)}, u32[]{:S(2)}) %all-to-all-start) | async-done | bytes 393248 | tf_op jit(solution)/shard_map/all_to_all | solution.py:209
  21.6 0.5 give.1
  22.1 2.1 %collective-permute-start.3 = (bf16[384,128]{1,0:T(8,128)(2,1)S(1)}, bf16[384,128]{1,0:T(8,128)(2,1)S(1)}, u32[]{:S(2)}, u32[]{:S(2)}) collective-permute-start(bf16[384,128]{1,0:T(8,128)(2,1)S(1)} %get-tuple-element.23), channel_id=1, source_target_pairs={{0,8},{1,9},{2,10},{3,11},{4,12},{5,13},{6,14},{7,15},{8,0},{9,1},... | collective-permute-start | bytes 294920 | tf_op jit(solution)/shard_map/ppermute | solution.py:222
  24.2 0.3 keep.1.own_ref
  24.5 0.6 %collective-permute-done.3.far_ref = bf16[384,128]{1,0:T(8,128)(2,1)S(1)} collective-permute-done((bf16[384,128]{1,0:T(8,128)(2,1)S(1)}, bf16[384,128]{1,0:T(8,128)(2,1)S(1)}, u32[]{:S(2)}, u32[]{:S(2)}) %collective-permute-start.3) | collective-permute-done | bytes 98336 | tf_op jit(solution)/shard_map/ppermute | solution.py:222
  25.2 5.2 %collective-permute-start.4 = (bf16[384,128]{1,0:T(8,128)(2,1)S(1)}, bf16[384,128]{1,0:T(8,128)(2,1)S(1)}, u32[]{:S(2)}, u32[]{:S(2)}) collective-permute-start(bf16[384,128]{1,0:T(8,128)(2,1)S(1)} %get-tuple-element.25), channel_id=1, source_target_pairs={{0,2},{1,3},{2,0},{3,1},{4,6},{5,7},{6,4},{7,5},{8,14},{9,15},{10,... | collective-permute-start | bytes 294920 | tf_op jit(solution)/shard_map/ppermute | solution.py:222
  30.4 0.3 columns.1.refs_0_
  30.6 2.3 %collective-permute-done.4.far_ref = bf16[384,128]{1,0:T(8,128)(2,1)S(1)} collective-permute-done((bf16[384,128]{1,0:T(8,128)(2,1)S(1)}, bf16[384,128]{1,0:T(8,128)(2,1)S(1)}, u32[]{:S(2)}, u32[]{:S(2)}) %collective-permute-start.4) | collective-permute-done | bytes 98336 | tf_op jit(solution)/shard_map/ppermute | solution.py:222
  33.0 1.9 %collective-permute-start.5 = (bf16[384,128]{1,0:T(8,128)(2,1)S(1)}, bf16[384,128]{1,0:T(8,128)(2,1)S(1)}, u32[]{:S(2)}, u32[]{:S(2)}) collective-permute-start(bf16[384,128]{1,0:T(8,128)(2,1)S(1)} %get-tuple-element.27), channel_id=1, source_target_pairs={{0,6},{1,7},{2,4},{3,5},{4,2},{5,3},{6,0},{7,1},{8,10},{9,11},{10,... | collective-permute-start | bytes 294920 | tf_op jit(solution)/shard_map/ppermute | solution.py:222
  34.9 0.1 flip.1.persons_ref
  35.0 2.9 %collective-permute-done.5.far_ref = bf16[384,128]{1,0:T(8,128)(2,1)S(1)} collective-permute-done((bf16[384,128]{1,0:T(8,128)(2,1)S(1)}, bf16[384,128]{1,0:T(8,128)(2,1)S(1)}, u32[]{:S(2)}, u32[]{:S(2)}) %collective-permute-start.5) | collective-permute-done | bytes 98336 | tf_op jit(solution)/shard_map/ppermute | solution.py:222
  37.9 3.4 %collective-permute-start.6 = (bf16[384,128]{1,0:T(8,128)(2,1)S(1)}, bf16[384,128]{1,0:T(8,128)(2,1)S(1)}, u32[]{:S(2)}, u32[]{:S(2)}) collective-permute-start(bf16[384,128]{1,0:T(8,128)(2,1)S(1)} %last_add.1.refs_2_), channel_id=1, source_target_pairs={{0,8},{1,9},{2,10},{3,11},{4,12},{5,13},{6,14},{7,15},{8,0},{9,1},... | collective-permute-start | bytes 294920 | tf_op jit(solution)/shard_map/ppermute | solution.py:222
  41.3 0.8 %own.1 = (f32[768,128]{1,0:T(8,128)S(1)}, bf16[768,512]{1,0:T(8,128)(2,1)S(1)}) custom-call(bf16[768,128]{1,0:T(8,128)(2,1)S(1)} %columns.1.refs_0_, bf16[768,256]{1,0:T(8,128)(2,1)S(1)} %bitcast.15, bf16[384,128]{1,0:T(8,128)(2,1)S(1)} %last_add.1.refs_2_), custom_call_target="tpu_custom_call" | custom-call | flops 300000000 | bytes 1200000 | tf_op jit(solution)/shard_map/own/pallas_call | solution.py:184
  42.1 0.1 collective-permute-done.6.refs_1_
  42.3 0.4 other.1
  42.6 11.4 %all_to_all.10 = bf16[32,24,128]{2,1,0:T(8,128)(2,1)S(1)} all-to-all(bf16[32,24,128]{2,1,0:T(8,128)(2,1)S(1)} %bitcast.12), channel_id=1, replica_groups={{0,1,16,17,32,33,48,49,64,65,80,81,96,97,112,113,128,129,144,145,160,16..., dimensions={0} | all-to-all | bytes 393216 | tf_op jit(solution)/shard_map/all_to_all | solution.py:209
  54.1 0.8 %finish.1 = bf16[128,128]{1,0:T(8,128)(2,1)} custom-call(bf16[128,768]{1,0:T(8,128)(2,1)S(1)} %flip.1.persons_ref, bf16[768,128]{1,0:T(8,128)(2,1)S(1)} %bitcast.11), custom_call_target="tpu_custom_call" | custom-call | tf_op jit(solution)/shard_map/finish/pallas_call | solution.py:308
  (6 shorter events, 0.2 us)
Async XLA Ops:
  2.4 19.1 %all-to-all-start = ((bf16[32,24,256]{2,1,0:T(8,128)(2,1)}), bf16[32,24,256]{2,1,0:T(8,128)(2,1)S(1)}, u32[]{:S(2)}, u32[]{:S(2)}) async-start(bf16[32,24,256]{2,1,0:T(8,128)(2,1)} %bitcast.7), calls=%async_computation | async-start | bytes 786432 | tf_op jit(solution)/shard_map/all_to_all | solution.py:209
  11.6 0.7 %copy-start = (s32[8]{0:T(128)S(1)}, s32[8]{0:T(128)}, u32[]{:S(2)}) copy-start(s32[8]{0:T(128)} %param.15) | copy-start | bytes 100
  12.3 2.6 %collective-permute-start = (s32[1,8]{1,0:T(1,128)S(1)}, s32[1,8]{1,0:T(1,128)S(1)}, u32[]{:S(2)}, u32[]{:S(2)}) collective-permute-start(s32[1,8]{1,0:T(1,128)S(1)} %bitcast.16), channel_id=1, source_target_pairs={{0,8},{1,9},{2,10},{3,11},{4,12},{5,13},{6,14},{7,15},{8,0},{9,1},... | collective-permute-start | bytes 104 | tf_op jit(solution)/shard_map/ppermute | solution.py:222
  13.3 3.7 %collective-permute-start.1 = (s32[1,8]{1,0:T(1,128)S(1)}, s32[1,8]{1,0:T(1,128)S(1)}, u32[]{:S(2)}, u32[]{:S(2)}) collective-permute-start(s32[1,8]{1,0:T(1,128)S(1)} %bitcast.17), channel_id=1, source_target_pairs={{0,1},{1,0},{2,3},{3,2},{4,5},{5,4},{6,7},{7,6},{8,9},{9,8},{10,11... | collective-permute-start | bytes 104 | tf_op jit(solution)/shard_map/ppermute | solution.py:222
  14.8 3.7 %collective-permute-start.2 = (s32[1,8]{1,0:T(1,128)S(1)}, s32[1,8]{1,0:T(1,128)S(1)}, u32[]{:S(2)}, u32[]{:S(2)}) collective-permute-start(s32[1,8]{1,0:T(1,128)S(1)} %bitcast.18), channel_id=1, source_target_pairs={{0,9},{1,8},{2,11},{3,10},{4,13},{5,12},{6,15},{7,14},{8,1},{9,0},... | collective-permute-start | bytes 104 | tf_op jit(solution)/shard_map/ppermute | solution.py:222
  22.1 3.0 %collective-permute-start.3 = (bf16[384,128]{1,0:T(8,128)(2,1)S(1)}, bf16[384,128]{1,0:T(8,128)(2,1)S(1)}, u32[]{:S(2)}, u32[]{:S(2)}) collective-permute-start(bf16[384,128]{1,0:T(8,128)(2,1)S(1)} %get-tuple-element.23), channel_id=1, source_target_pairs={{0,8},{1,9},{2,10},{3,11},{4,12},{5,13},{6,14},{7,15},{8,0},{9,1},... | collective-permute-start | bytes 294920 | tf_op jit(solution)/shard_map/ppermute | solution.py:222
  25.2 7.8 %collective-permute-start.4 = (bf16[384,128]{1,0:T(8,128)(2,1)S(1)}, bf16[384,128]{1,0:T(8,128)(2,1)S(1)}, u32[]{:S(2)}, u32[]{:S(2)}) collective-permute-start(bf16[384,128]{1,0:T(8,128)(2,1)S(1)} %get-tuple-element.25), channel_id=1, source_target_pairs={{0,2},{1,3},{2,0},{3,1},{4,6},{5,7},{6,4},{7,5},{8,14},{9,15},{10,... | collective-permute-start | bytes 294920 | tf_op jit(solution)/shard_map/ppermute | solution.py:222
  33.0 4.9 %collective-permute-start.5 = (bf16[384,128]{1,0:T(8,128)(2,1)S(1)}, bf16[384,128]{1,0:T(8,128)(2,1)S(1)}, u32[]{:S(2)}, u32[]{:S(2)}) collective-permute-start(bf16[384,128]{1,0:T(8,128)(2,1)S(1)} %get-tuple-element.27), channel_id=1, source_target_pairs={{0,6},{1,7},{2,4},{3,5},{4,2},{5,3},{6,0},{7,1},{8,10},{9,11},{10,... | collective-permute-start | bytes 294920 | tf_op jit(solution)/shard_map/ppermute | solution.py:222
  37.9 4.3 %collective-permute-start.6 = (bf16[384,128]{1,0:T(8,128)(2,1)S(1)}, bf16[384,128]{1,0:T(8,128)(2,1)S(1)}, u32[]{:S(2)}, u32[]{:S(2)}) collective-permute-start(bf16[384,128]{1,0:T(8,128)(2,1)S(1)} %last_add.1.refs_2_), channel_id=1, source_target_pairs={{0,8},{1,9},{2,10},{3,11},{4,12},{5,13},{6,14},{7,15},{8,0},{9,1},... | collective-permute-start | bytes 294920 | tf_op jit(solution)/shard_map/ppermute | solution.py:222

commit v9 on v8

--- a/solution.py
+++ b/solution.py
@@ -40,8 +40,10 @@
     row_ref,
     start_ref,
     length_ref,
+    tile_loc_ref,
     send_ref,
     persons_ref,
+    table_ref,
 ):
     visits = person_ref.shape[1]
     slots, persons = profile_ref.shape
@@ -84,6 +86,7 @@
     send_ref[:, :128] = weights.astype(BF16)
     send_ref[:, 128:] = matmul(hot, panel_ref[...]).astype(BF16)
     persons_ref[...] = hot
+    table_ref[...] = tile_loc_ref[...]
 
 
 def as_column(row):
@@ -242,10 +245,10 @@
     capacity = visits // pop_count * 3 // 2
     rows = pop_count * capacity
     as_row = lambda x: x.reshape(1, visits)
-    send, person_rows = call(
+    send, person_rows, mine = call(
         lambda *refs: pack_kernel(pop_count, *refs),
         "pack",
-        [((rows, 128 + width), BF16), ((rows, persons), BF16)],
+        [((rows, 128 + width), BF16), ((rows, persons), BF16), ((1, TILES), jnp.int32)],
         profile.T,
         panel,
         as_row(visit_person),
@@ -253,8 +256,8 @@
         as_row(visit_row),
         as_row(visit_start),
         as_row(visit_length),
-    )
-    mine = tile_loc.reshape(1, TILES)
+        tile_loc.reshape(1, TILES),
+    )
     neighbour_site = lambda pop, site: (pop, site ^ 1)
     diagonal = lambda pop, site: (pop ^ 1, site ^ 1)
     tables = [mine] + [swap(mine, far) for far in (sibling_core, neighbour_site, diagonal)]

time: 55.1 us -> 55.1 us (level)
  local copies, waits for them, and re-layouts: 0.65 us -> 0 us
    unnamed x2 -> x0, local copies, waits for them, and re-layouts: 0.65 us -> none
where the time goes in v9:
time: 55.1 us; the launch traced here: 54.9 us
  starting transfers between devices  24.5 us (44%)
  waiting for transfers between devices  13.1 us (24%)
  blocking collectives  11.4 us (21%)
  Pallas kernels  5.74 us (10%)
    ppermute x7, starting transfers between devices, swap(): return lax.ppermute(array, ('pop', 'site'), pairs)  15.3 us
    all_to_all x1, blocking collectives, exchange(): lax.all_to_all(blocks, ('pop', 'site'), 0, 0, tiled=True, axis_index_grou...  11.4 us
    ppermute x7, waiting for transfers between devices, swap(): return lax.ppermute(array, ('pop', 'site'), pairs)  9.98 us
    all_to_all x1, starting transfers between devices, exchange(): lax.all_to_all(blocks, ('pop', 'site'), 0, 0, tiled=True, axis_index_grou...  9.22 us
    pallas_call x10, Pallas kernels, call(): pl.pallas_call(kernel, out_shape=tuple((pltpu.VMEM(shape, kind) for shape...  4.93 us
    all_to_all x1, waiting for transfers between devices, exchange(): lax.all_to_all(blocks, ('pop', 'site'), 0, 0, tiled=True, axis_index_grou...  3.12 us
  transfers between devices with their start and end apart: 8, of which 7 were waited for; matrix products, arithmetic and copies ran while one was open for 0% of the time, Pallas kernels for 3%

profile of v9, /device:TPU:1, one launch (start us, length us, event | category | flops | bytes accessed | tf_op | source)
XLA Modules:
  0.0 54.9 jit_solution(10792880412439829729)
XLA Ops:
  0.0 2.4 %pack.1 = (bf16[768,256]{1,0:T(8,128)(2,1)}, bf16[768,128]{1,0:T(8,128)(2,1)S(1)}, s32[1,8]{1,0:T(1,128)S(1)}) custom-call(bf16[96,128]{1,0:T(8,128)(2,1)} %bitcast.16, bf16[128,128]{1,0:T(8,128)(2,1)} %refs_1_.1, s32[1,512]{1,0:T(1,128)} %bitcast.17, s32[1,512]{1,0:T(1,128)} %bitcast.18, s32[1,512]{1,0:T(1,128)} %bitcast.19, s32[1,512]{1,0:T(1,128)} %bitcast.20, ...), custom_call_target="tpu_custom_call" | custom-call | flops 250000000 | bytes 1000000 | tf_op jit(solution)/shard_map/pack/pallas_call | solution.py:187
  2.4 9.2 %all-to-all-start = ((bf16[32,24,256]{2,1,0:T(8,128)(2,1)}), bf16[32,24,256]{2,1,0:T(8,128)(2,1)S(1)}, u32[]{:S(2)}, u32[]{:S(2)}) async-start(bf16[32,24,256]{2,1,0:T(8,128)(2,1)} %bitcast.7), calls=%async_computation | async-start | bytes 786432 | tf_op jit(solution)/shard_map/all_to_all | solution.py:212
  11.7 1.0 %collective-permute-start = (s32[1,8]{1,0:T(1,128)S(1)}, s32[1,8]{1,0:T(1,128)S(1)}, u32[]{:S(2)}, u32[]{:S(2)}) collective-permute-start(s32[1,8]{1,0:T(1,128)S(1)} %get-tuple-element.21.refs_0_), channel_id=1, source_target_pairs={{0,8},{1,9},{2,10},{3,11},{4,12},{5,13},{6,14},{7,15},{8,0},{9,1},... | collective-permute-start | bytes 104 | tf_op jit(solution)/shard_map/ppermute | solution.py:225
  12.7 1.5 %collective-permute-start.1 = (s32[1,8]{1,0:T(1,128)S(1)}, s32[1,8]{1,0:T(1,128)S(1)}, u32[]{:S(2)}, u32[]{:S(2)}) collective-permute-start(s32[1,8]{1,0:T(1,128)S(1)} %get-tuple-element.21.refs_0_), channel_id=1, source_target_pairs={{0,1},{1,0},{2,3},{3,2},{4,5},{5,4},{6,7},{7,6},{8,9},{9,8},{10,11... | collective-permute-start | bytes 104 | tf_op jit(solution)/shard_map/ppermute | solution.py:225
  14.2 0.2 collective-permute-start.2
  14.4 2.5 %collective-permute-done.1.refs_2_ = s32[1,8]{1,0:T(1,128)S(1)} collective-permute-done((s32[1,8]{1,0:T(1,128)S(1)}, s32[1,8]{1,0:T(1,128)S(1)}, u32[]{:S(2)}, u32[]{:S(2)}) %collective-permute-start.1) | collective-permute-done | bytes 64 | tf_op jit(solution)/shard_map/ppermute | solution.py:225
  16.9 1.5 %collective-permute-done.2.refs_3_ = s32[1,8]{1,0:T(1,128)S(1)} collective-permute-done((s32[1,8]{1,0:T(1,128)S(1)}, s32[1,8]{1,0:T(1,128)S(1)}, u32[]{:S(2)}, u32[]{:S(2)}) %collective-permute-start.2) | collective-permute-done | bytes 64 | tf_op jit(solution)/shard_map/ppermute | solution.py:225
  18.4 3.1 %all-to-all-done = bf16[32,24,256]{2,1,0:T(8,128)(2,1)S(1)} async-done(((bf16[32,24,256]{2,1,0:T(8,128)(2,1)}), bf16[32,24,256]{2,1,0:T(8,128)(2,1)S(1)}, u32[]{:S(2)}, u32[]{:S(2)}) %all-to-all-start) | async-done | bytes 393248 | tf_op jit(solution)/shard_map/all_to_all | solution.py:212
  21.5 0.5 give.1
  22.1 2.1 %collective-permute-start.3 = (bf16[384,128]{1,0:T(8,128)(2,1)S(1)}, bf16[384,128]{1,0:T(8,128)(2,1)S(1)}, u32[]{:S(2)}, u32[]{:S(2)}) collective-permute-start(bf16[384,128]{1,0:T(8,128)(2,1)S(1)} %get-tuple-element.25), channel_id=1, source_target_pairs={{0,8},{1,9},{2,10},{3,11},{4,12},{5,13},{6,14},{7,15},{8,0},{9,1},... | collective-permute-start | bytes 294920 | tf_op jit(solution)/shard_map/ppermute | solution.py:225
  24.2 0.3 keep.1.own_ref
  24.5 0.6 %collective-permute-done.3.far_ref = bf16[384,128]{1,0:T(8,128)(2,1)S(1)} collective-permute-done((bf16[384,128]{1,0:T(8,128)(2,1)S(1)}, bf16[384,128]{1,0:T(8,128)(2,1)S(1)}, u32[]{:S(2)}, u32[]{:S(2)}) %collective-permute-start.3) | collective-permute-done | bytes 98336 | tf_op jit(solution)/shard_map/ppermute | solution.py:225
  25.2 5.2 %collective-permute-start.4 = (bf16[384,128]{1,0:T(8,128)(2,1)S(1)}, bf16[384,128]{1,0:T(8,128)(2,1)S(1)}, u32[]{:S(2)}, u32[]{:S(2)}) collective-permute-start(bf16[384,128]{1,0:T(8,128)(2,1)S(1)} %get-tuple-element.27), channel_id=1, source_target_pairs={{0,2},{1,3},{2,0},{3,1},{4,6},{5,7},{6,4},{7,5},{8,14},{9,15},{10,... | collective-permute-start | bytes 294920 | tf_op jit(solution)/shard_map/ppermute | solution.py:225
  30.4 0.3 columns.1.refs_0_
  30.6 2.3 %collective-permute-done.4.far_ref = bf16[384,128]{1,0:T(8,128)(2,1)S(1)} collective-permute-done((bf16[384,128]{1,0:T(8,128)(2,1)S(1)}, bf16[384,128]{1,0:T(8,128)(2,1)S(1)}, u32[]{:S(2)}, u32[]{:S(2)}) %collective-permute-start.4) | collective-permute-done | bytes 98336 | tf_op jit(solution)/shard_map/ppermute | solution.py:225
  33.0 1.9 %collective-permute-start.5 = (bf16[384,128]{1,0:T(8,128)(2,1)S(1)}, bf16[384,128]{1,0:T(8,128)(2,1)S(1)}, u32[]{:S(2)}, u32[]{:S(2)}) collective-permute-start(bf16[384,128]{1,0:T(8,128)(2,1)S(1)} %get-tuple-element.29), channel_id=1, source_target_pairs={{0,6},{1,7},{2,4},{3,5},{4,2},{5,3},{6,0},{7,1},{8,10},{9,11},{10,... | collective-permute-start | bytes 294920 | tf_op jit(solution)/shard_map/ppermute | solution.py:225
  34.9 0.1 flip.1.persons_ref
  35.0 2.9 %collective-permute-done.5.far_ref = bf16[384,128]{1,0:T(8,128)(2,1)S(1)} collective-permute-done((bf16[384,128]{1,0:T(8,128)(2,1)S(1)}, bf16[384,128]{1,0:T(8,128)(2,1)S(1)}, u32[]{:S(2)}, u32[]{:S(2)}) %collective-permute-start.5) | collective-permute-done | bytes 98336 | tf_op jit(solution)/shard_map/ppermute | solution.py:225
  37.9 3.4 %collective-permute-start.6 = (bf16[384,128]{1,0:T(8,128)(2,1)S(1)}, bf16[384,128]{1,0:T(8,128)(2,1)S(1)}, u32[]{:S(2)}, u32[]{:S(2)}) collective-permute-start(bf16[384,128]{1,0:T(8,128)(2,1)S(1)} %last_add.1.refs_2_), channel_id=1, source_target_pairs={{0,8},{1,9},{2,10},{3,11},{4,12},{5,13},{6,14},{7,15},{8,0},{9,1},... | collective-permute-start | bytes 294920 | tf_op jit(solution)/shard_map/ppermute | solution.py:225
  41.3 0.8 %own.1 = (f32[768,128]{1,0:T(8,128)S(1)}, bf16[768,512]{1,0:T(8,128)(2,1)S(1)}) custom-call(bf16[768,128]{1,0:T(8,128)(2,1)S(1)} %columns.1.refs_0_, bf16[768,256]{1,0:T(8,128)(2,1)S(1)} %bitcast.15, bf16[384,128]{1,0:T(8,128)(2,1)S(1)} %last_add.1.refs_2_), custom_call_target="tpu_custom_call" | custom-call | flops 300000000 | bytes 1200000 | tf_op jit(solution)/shard_map/own/pallas_call | solution.py:187
  42.1 0.1 collective-permute-done.6.refs_1_
  42.3 0.4 other.1
  42.6 11.4 %all_to_all.10 = bf16[32,24,128]{2,1,0:T(8,128)(2,1)S(1)} all-to-all(bf16[32,24,128]{2,1,0:T(8,128)(2,1)S(1)} %bitcast.12), channel_id=1, replica_groups={{0,1,16,17,32,33,48,49,64,65,80,81,96,97,112,113,128,129,144,145,160,16..., dimensions={0} | all-to-all | bytes 393216 | tf_op jit(solution)/shard_map/all_to_all | solution.py:212
  54.1 0.8 %finish.1 = bf16[128,128]{1,0:T(8,128)(2,1)} custom-call(bf16[128,768]{1,0:T(8,128)(2,1)S(1)} %flip.1.persons_ref, bf16[768,128]{1,0:T(8,128)(2,1)S(1)} %bitcast.11), custom_call_target="tpu_custom_call" | custom-call | tf_op jit(solution)/shard_map/finish/pallas_call | solution.py:311
  (4 shorter events, 0.1 us)
Async XLA Ops:
  2.4 19.1 %all-to-all-start = ((bf16[32,24,256]{2,1,0:T(8,128)(2,1)}), bf16[32,24,256]{2,1,0:T(8,128)(2,1)S(1)}, u32[]{:S(2)}, u32[]{:S(2)}) async-start(bf16[32,24,256]{2,1,0:T(8,128)(2,1)} %bitcast.7), calls=%async_computation | async-start | bytes 786432 | tf_op jit(solution)/shard_map/all_to_all | solution.py:212
  11.7 2.8 %collective-permute-start = (s32[1,8]{1,0:T(1,128)S(1)}, s32[1,8]{1,0:T(1,128)S(1)}, u32[]{:S(2)}, u32[]{:S(2)}) collective-permute-start(s32[1,8]{1,0:T(1,128)S(1)} %get-tuple-element.21.refs_0_), channel_id=1, source_target_pairs={{0,8},{1,9},{2,10},{3,11},{4,12},{5,13},{6,14},{7,15},{8,0},{9,1},... | collective-permute-start | bytes 104 | tf_op jit(solution)/shard_map/ppermute | solution.py:225
  12.7 4.2 %collective-permute-start.1 = (s32[1,8]{1,0:T(1,128)S(1)}, s32[1,8]{1,0:T(1,128)S(1)}, u32[]{:S(2)}, u32[]{:S(2)}) collective-permute-start(s32[1,8]{1,0:T(1,128)S(1)} %get-tuple-element.21.refs_0_), channel_id=1, source_target_pairs={{0,1},{1,0},{2,3},{3,2},{4,5},{5,4},{6,7},{7,6},{8,9},{9,8},{10,11... | collective-permute-start | bytes 104 | tf_op jit(solution)/shard_map/ppermute | solution.py:225
  14.2 4.2 %collective-permute-start.2 = (s32[1,8]{1,0:T(1,128)S(1)}, s32[1,8]{1,0:T(1,128)S(1)}, u32[]{:S(2)}, u32[]{:S(2)}) collective-permute-start(s32[1,8]{1,0:T(1,128)S(1)} %get-tuple-element.21.refs_0_), channel_id=1, source_target_pairs={{0,9},{1,8},{2,11},{3,10},{4,13},{5,12},{6,15},{7,14},{8,1},{9,0},... | collective-permute-start | bytes 104 | tf_op jit(solution)/shard_map/ppermute | solution.py:225
  22.1 3.0 %collective-permute-start.3 = (bf16[384,128]{1,0:T(8,128)(2,1)S(1)}, bf16[384,128]{1,0:T(8,128)(2,1)S(1)}, u32[]{:S(2)}, u32[]{:S(2)}) collective-permute-start(bf16[384,128]{1,0:T(8,128)(2,1)S(1)} %get-tuple-element.25), channel_id=1, source_target_pairs={{0,8},{1,9},{2,10},{3,11},{4,12},{5,13},{6,14},{7,15},{8,0},{9,1},... | collective-permute-start | bytes 294920 | tf_op jit(solution)/shard_map/ppermute | solution.py:225
  25.2 7.8 %collective-permute-start.4 = (bf16[384,128]{1,0:T(8,128)(2,1)S(1)}, bf16[384,128]{1,0:T(8,128)(2,1)S(1)}, u32[]{:S(2)}, u32[]{:S(2)}) collective-permute-start(bf16[384,128]{1,0:T(8,128)(2,1)S(1)} %get-tuple-element.27), channel_id=1, source_target_pairs={{0,2},{1,3},{2,0},{3,1},{4,6},{5,7},{6,4},{7,5},{8,14},{9,15},{10,... | collective-permute-start | bytes 294920 | tf_op jit(solution)/shard_map/ppermute | solution.py:225
  33.0 4.9 %collective-permute-start.5 = (bf16[384,128]{1,0:T(8,128)(2,1)S(1)}, bf16[384,128]{1,0:T(8,128)(2,1)S(1)}, u32[]{:S(2)}, u32[]{:S(2)}) collective-permute-start(bf16[384,128]{1,0:T(8,128)(2,1)S(1)} %get-tuple-element.29), channel_id=1, source_target_pairs={{0,6},{1,7},{2,4},{3,5},{4,2},{5,3},{6,0},{7,1},{8,10},{9,11},{10,... | collective-permute-start | bytes 294920 | tf_op jit(solution)/shard_map/ppermute | solution.py:225
  37.9 4.3 %collective-permute-start.6 = (bf16[384,128]{1,0:T(8,128)(2,1)S(1)}, bf16[384,128]{1,0:T(8,128)(2,1)S(1)}, u32[]{:S(2)}, u32[]{:S(2)}) collective-permute-start(bf16[384,128]{1,0:T(8,128)(2,1)S(1)} %last_add.1.refs_2_), channel_id=1, source_target_pairs={{0,8},{1,9},{2,10},{3,11},{4,12},{5,13},{6,14},{7,15},{8,0},{9,1},... | collective-permute-start | bytes 294920 | tf_op jit(solution)/shard_map/ppermute | solution.py:225

commit v10 on v9

--- a/solution.py
+++ b/solution.py
@@ -12,6 +12,7 @@
 LOCATIONS = 8
 HALF = LOCATIONS // 2
 TILES = 8
+PARTS = 4
 NT = (((1,), (1,)), ((), ()))
 
 
@@ -44,6 +45,8 @@
     send_ref,
     persons_ref,
     table_ref,
+    message_ref,
+    done_sems,
 ):
     visits = person_ref.shape[1]
     slots, persons = profile_ref.shape
@@ -66,27 +69,41 @@
         seen = seen + jnp.sum(chunk, axis=1, keepdims=True)
     position = jnp.concatenate(positions, axis=1)
     slot = owner * capacity + position.astype(jnp.int32)
-    place = as_bf16(iota((rows, visits), 0) == slot)
     person_hot = as_bf16(iota((persons, visits), 0) == person_ref[...])
-    line = iota((128, visits), 0)
+    line = iota((16, visits), 0)
     facts = jnp.where(line == 0, start, jnp.where(line == 1, finish, jnp.where(line == 2, tile, 0)))
     table = jnp.concatenate([person_hot, facts.astype(F32).astype(BF16)], axis=0)
-    placed = matmul_nt(place, table)
-    hot = placed[:, :persons].astype(BF16)
-    start_at = placed[:, persons : persons + 1]
-    finish_at = placed[:, persons + 1 : persons + 2]
-    tile_at = placed[:, persons + 2 : persons + 3]
     no_slots = jnp.zeros((128 - slots, persons), BF16)
-    weights = matmul_nt(hot, jnp.concatenate([profile_ref[...], no_slots], axis=0))
-    lane = iota((rows, 128), 1)
-    lane_f = lane.astype(F32)
-    inside = (lane_f >= start_at) & (lane_f < finish_at)
-    weights = jnp.where(inside, weights, 0.0)
-    weights = jnp.where(lane == slots, tile_at, weights)
-    send_ref[:, :128] = weights.astype(BF16)
-    send_ref[:, 128:] = matmul(hot, panel_ref[...]).astype(BF16)
-    persons_ref[...] = hot
+    panel = jnp.transpose(panel_ref[...].astype(F32)).astype(BF16)
+    values = jnp.concatenate([profile_ref[...], no_slots, panel], axis=0)
+    part = rows // PARTS
+    copies = []
+    for number in range(PARTS):
+        here = pl.ds(number * part, part)
+        place = as_bf16(iota((part, visits), 0) + number * part == slot)
+        placed = matmul_nt(place, table)
+        hot = placed[:, :persons].astype(BF16)
+        start_at = placed[:, persons : persons + 1]
+        finish_at = placed[:, persons + 1 : persons + 2]
+        tile_at = placed[:, persons + 2 : persons + 3]
+        chosen = matmul_nt(hot, values)
+        lane = iota((part, 128), 1)
+        lane_f = lane.astype(F32)
+        inside = (lane_f >= start_at) & (lane_f < finish_at)
+        weights = jnp.where(inside, chosen[:, :128], 0.0)
+        weights = jnp.where(lane == slots, tile_at, weights)
+        message_ref[here, :128] = weights.astype(BF16)
+        message_ref[here, 128:] = chosen[:, 128:].astype(BF16)
+        persons_ref[here, :] = hot
+        copies.append(
+            pltpu.make_async_copy(
+                message_ref.at[here, :], send_ref.at[here, :], done_sems.at[number]
+            )
+        )
+        copies[-1].start()
     table_ref[...] = tile_loc_ref[...]
+    for copy in copies:
+        copy.wait()
 
 
 def as_column(row):
@@ -245,10 +262,21 @@
     capacity = visits // pop_count * 3 // 2
     rows = pop_count * capacity
     as_row = lambda x: x.reshape(1, visits)
-    send, person_rows, mine = call(
+    send, person_rows, mine = pl.pallas_call(
         lambda *refs: pack_kernel(pop_count, *refs),
-        "pack",
-        [((rows, 128 + width), BF16), ((rows, persons), BF16), ((1, TILES), jnp.int32)],
+        out_shape=(
+            jax.ShapeDtypeStruct((rows, 128 + width), BF16),
+            pltpu.VMEM((rows, persons), BF16),
+            pltpu.VMEM((1, TILES), jnp.int32),
+        ),
+        in_specs=vmem(8),
+        out_specs=(pl.BlockSpec(memory_space=pl.ANY), *vmem(2)),
+        scratch_shapes=[
+            pltpu.VMEM((rows, 128 + width), BF16),
+            pltpu.SemaphoreType.DMA((PARTS,)),
+        ],
+        name="pack",
+    )(
         profile.T,
         panel,
         as_row(visit_person),

time: 55.1 us -> 55.4 us (level)
    pallas_call x0 -> x1, Pallas kernels: none -> 2.65 us  [per_device(): pl.pallas_call(lambda *refs: pack_kernel(pop_count, *refs), out_shape=(ja...]
    pallas_call x10 -> x9, Pallas kernels: 4.93 us -> 2.52 us  [call(): pl.pallas_call(kernel, out_shape=tuple((pltpu.VMEM(shape, kind) for shape...]
where the time goes in v10:
time: 55.4 us; the launch traced here: 55.1 us
  starting transfers between devices  24.5 us (44%)
  waiting for transfers between devices  13.1 us (24%)
  blocking collectives  11.4 us (21%)
  Pallas kernels  5.98 us (11%)
    ppermute x7, starting transfers between devices, swap(): return lax.ppermute(array, ('pop', 'site'), pairs)  15.3 us
    all_to_all x1, blocking collectives, exchange(): lax.all_to_all(blocks, ('pop', 'site'), 0, 0, tiled=True, axis_index_grou...  11.4 us
    ppermute x7, waiting for transfers between devices, swap(): return lax.ppermute(array, ('pop', 'site'), pairs)  9.98 us
    all_to_all x1, starting transfers between devices, exchange(): lax.all_to_all(blocks, ('pop', 'site'), 0, 0, tiled=True, axis_index_grou...  9.23 us
    all_to_all x1, waiting for transfers between devices, exchange(): lax.all_to_all(blocks, ('pop', 'site'), 0, 0, tiled=True, axis_index_grou...  3.13 us
    pallas_call x1, Pallas kernels, per_device(): pl.pallas_call(lambda *refs: pack_kernel(pop_count, *refs), out_shape=(ja...  2.65 us
    pallas_call x9, Pallas kernels, call(): pl.pallas_call(kernel, out_shape=tuple((pltpu.VMEM(shape, kind) for shape...  2.52 us
  transfers between devices with their start and end apart: 8, of which 7 were waited for; matrix products, arithmetic and copies ran while one was open for 0% of the time, Pallas kernels for 3%

profile of v10, /device:TPU:1, one launch (start us, length us, event | category | flops | bytes accessed | tf_op | source)
XLA Modules:
  0.0 55.1 jit_solution(16597101181181534866)
XLA Ops:
  0.0 2.7 %pack.1 = (bf16[768,256]{1,0:T(8,128)(2,1)}, bf16[768,128]{1,0:T(8,128)(2,1)S(1)}, s32[1,8]{1,0:T(1,128)S(1)}) custom-call(bf16[96,128]{1,0:T(8,128)(2,1)} %bitcast.17, bf16[128,128]{1,0:T(8,128)(2,1)} %refs_1_.1, s32[1,512]{1,0:T(1,128)} %bitcast.18, s32[1,512]{1,0:T(1,128)} %bitcast.19, s32[1,512]{1,0:T(1,128)} %bitcast.20, s32[1,512]{1,0:T(1,128)} %bitcast.21, ...), custom_call_target="tpu_custom_call" | custom-call | tf_op jit(solution)/shard_map/pack/pallas_call | solution.py:265
  2.7 9.2 %all-to-all-start = ((bf16[32,24,256]{2,1,0:T(8,128)(2,1)}), bf16[32,24,256]{2,1,0:T(8,128)(2,1)S(1)}, u32[]{:S(2)}, u32[]{:S(2)}) async-start(bf16[32,24,256]{2,1,0:T(8,128)(2,1)} %bitcast.16), calls=%async_computation | async-start | bytes 786432 | tf_op jit(solution)/shard_map/all_to_all | solution.py:229
  11.9 1.0 %collective-permute-start = (s32[1,8]{1,0:T(1,128)S(1)}, s32[1,8]{1,0:T(1,128)S(1)}, u32[]{:S(2)}, u32[]{:S(2)}) collective-permute-start(s32[1,8]{1,0:T(1,128)S(1)} %get-tuple-element.21.refs_0_), channel_id=1, source_target_pairs={{0,8},{1,9},{2,10},{3,11},{4,12},{5,13},{6,14},{7,15},{8,0},{9,1},... | collective-permute-start | bytes 104 | tf_op jit(solution)/shard_map/ppermute | solution.py:242
  12.9 1.5 %collective-permute-start.1 = (s32[1,8]{1,0:T(1,128)S(1)}, s32[1,8]{1,0:T(1,128)S(1)}, u32[]{:S(2)}, u32[]{:S(2)}) collective-permute-start(s32[1,8]{1,0:T(1,128)S(1)} %get-tuple-element.21.refs_0_), channel_id=1, source_target_pairs={{0,1},{1,0},{2,3},{3,2},{4,5},{5,4},{6,7},{7,6},{8,9},{9,8},{10,11... | collective-permute-start | bytes 104 | tf_op jit(solution)/shard_map/ppermute | solution.py:242
  14.5 0.2 collective-permute-start.2
  14.7 2.5 %collective-permute-done.1.refs_2_ = s32[1,8]{1,0:T(1,128)S(1)} collective-permute-done((s32[1,8]{1,0:T(1,128)S(1)}, s32[1,8]{1,0:T(1,128)S(1)}, u32[]{:S(2)}, u32[]{:S(2)}) %collective-permute-start.1) | collective-permute-done | bytes 64 | tf_op jit(solution)/shard_map/ppermute | solution.py:242
  17.2 1.5 %collective-permute-done.2.refs_3_ = s32[1,8]{1,0:T(1,128)S(1)} collective-permute-done((s32[1,8]{1,0:T(1,128)S(1)}, s32[1,8]{1,0:T(1,128)S(1)}, u32[]{:S(2)}, u32[]{:S(2)}) %collective-permute-start.2) | collective-permute-done | bytes 64 | tf_op jit(solution)/shard_map/ppermute | solution.py:242
  18.7 3.1 %all-to-all-done = bf16[32,24,256]{2,1,0:T(8,128)(2,1)S(1)} async-done(((bf16[32,24,256]{2,1,0:T(8,128)(2,1)}), bf16[32,24,256]{2,1,0:T(8,128)(2,1)S(1)}, u32[]{:S(2)}, u32[]{:S(2)}) %all-to-all-start) | async-done | bytes 393248 | tf_op jit(solution)/shard_map/all_to_all | solution.py:229
  21.8 0.5 give.1
  22.4 2.1 %collective-permute-start.3 = (bf16[384,128]{1,0:T(8,128)(2,1)S(1)}, bf16[384,128]{1,0:T(8,128)(2,1)S(1)}, u32[]{:S(2)}, u32[]{:S(2)}) collective-permute-start(bf16[384,128]{1,0:T(8,128)(2,1)S(1)} %get-tuple-element.25), channel_id=1, source_target_pairs={{0,8},{1,9},{2,10},{3,11},{4,12},{5,13},{6,14},{7,15},{8,0},{9,1},... | collective-permute-start | bytes 294920 | tf_op jit(solution)/shard_map/ppermute | solution.py:242
  24.4 0.3 keep.1.own_ref
  24.8 0.6 %collective-permute-done.3.far_ref = bf16[384,128]{1,0:T(8,128)(2,1)S(1)} collective-permute-done((bf16[384,128]{1,0:T(8,128)(2,1)S(1)}, bf16[384,128]{1,0:T(8,128)(2,1)S(1)}, u32[]{:S(2)}, u32[]{:S(2)}) %collective-permute-start.3) | collective-permute-done | bytes 98336 | tf_op jit(solution)/shard_map/ppermute | solution.py:242
  25.4 5.2 %collective-permute-start.4 = (bf16[384,128]{1,0:T(8,128)(2,1)S(1)}, bf16[384,128]{1,0:T(8,128)(2,1)S(1)}, u32[]{:S(2)}, u32[]{:S(2)}) collective-permute-start(bf16[384,128]{1,0:T(8,128)(2,1)S(1)} %get-tuple-element.27), channel_id=1, source_target_pairs={{0,2},{1,3},{2,0},{3,1},{4,6},{5,7},{6,4},{7,5},{8,14},{9,15},{10,... | collective-permute-start | bytes 294920 | tf_op jit(solution)/shard_map/ppermute | solution.py:242
  30.6 0.3 columns.1.refs_0_
  30.9 2.3 %collective-permute-done.4.far_ref = bf16[384,128]{1,0:T(8,128)(2,1)S(1)} collective-permute-done((bf16[384,128]{1,0:T(8,128)(2,1)S(1)}, bf16[384,128]{1,0:T(8,128)(2,1)S(1)}, u32[]{:S(2)}, u32[]{:S(2)}) %collective-permute-start.4) | collective-permute-done | bytes 98336 | tf_op jit(solution)/shard_map/ppermute | solution.py:242
  33.3 1.9 %collective-permute-start.5 = (bf16[384,128]{1,0:T(8,128)(2,1)S(1)}, bf16[384,128]{1,0:T(8,128)(2,1)S(1)}, u32[]{:S(2)}, u32[]{:S(2)}) collective-permute-start(bf16[384,128]{1,0:T(8,128)(2,1)S(1)} %get-tuple-element.29), channel_id=1, source_target_pairs={{0,6},{1,7},{2,4},{3,5},{4,2},{5,3},{6,0},{7,1},{8,10},{9,11},{10,... | collective-permute-start | bytes 294920 | tf_op jit(solution)/shard_map/ppermute | solution.py:242
  35.1 0.1 flip.1.persons_ref
  35.3 2.9 %collective-permute-done.5.far_ref = bf16[384,128]{1,0:T(8,128)(2,1)S(1)} collective-permute-done((bf16[384,128]{1,0:T(8,128)(2,1)S(1)}, bf16[384,128]{1,0:T(8,128)(2,1)S(1)}, u32[]{:S(2)}, u32[]{:S(2)}) %collective-permute-start.5) | collective-permute-done | bytes 98336 | tf_op jit(solution)/shard_map/ppermute | solution.py:242
  38.2 3.4 %collective-permute-start.6 = (bf16[384,128]{1,0:T(8,128)(2,1)S(1)}, bf16[384,128]{1,0:T(8,128)(2,1)S(1)}, u32[]{:S(2)}, u32[]{:S(2)}) collective-permute-start(bf16[384,128]{1,0:T(8,128)(2,1)S(1)} %last_add.1.refs_2_), channel_id=1, source_target_pairs={{0,8},{1,9},{2,10},{3,11},{4,12},{5,13},{6,14},{7,15},{8,0},{9,1},... | collective-permute-start | bytes 294920 | tf_op jit(solution)/shard_map/ppermute | solution.py:242
  41.6 0.8 %own.1 = (f32[768,128]{1,0:T(8,128)S(1)}, bf16[768,512]{1,0:T(8,128)(2,1)S(1)}) custom-call(bf16[768,128]{1,0:T(8,128)(2,1)S(1)} %columns.1.refs_0_, bf16[768,256]{1,0:T(8,128)(2,1)S(1)} %bitcast.15, bf16[384,128]{1,0:T(8,128)(2,1)S(1)} %last_add.1.refs_2_), custom_call_target="tpu_custom_call" | custom-call | flops 300000000 | bytes 1200000 | tf_op jit(solution)/shard_map/own/pallas_call | solution.py:204
  42.4 0.1 collective-permute-done.6.refs_1_
  42.5 0.4 other.1
  42.9 11.4 %all_to_all.10 = bf16[32,24,128]{2,1,0:T(8,128)(2,1)S(1)} all-to-all(bf16[32,24,128]{2,1,0:T(8,128)(2,1)S(1)} %bitcast.12), channel_id=1, replica_groups={{0,1,16,17,32,33,48,49,64,65,80,81,96,97,112,113,128,129,144,145,160,16..., dimensions={0} | all-to-all | bytes 393216 | tf_op jit(solution)/shard_map/all_to_all | solution.py:229
  54.3 0.8 %finish.1 = bf16[128,128]{1,0:T(8,128)(2,1)} custom-call(bf16[128,768]{1,0:T(8,128)(2,1)S(1)} %flip.1.persons_ref, bf16[768,128]{1,0:T(8,128)(2,1)S(1)} %bitcast.11), custom_call_target="tpu_custom_call" | custom-call | tf_op jit(solution)/shard_map/finish/pallas_call | solution.py:339
  (4 shorter events, 0.1 us)
Async XLA Ops:
  2.7 19.1 %all-to-all-start = ((bf16[32,24,256]{2,1,0:T(8,128)(2,1)}), bf16[32,24,256]{2,1,0:T(8,128)(2,1)S(1)}, u32[]{:S(2)}, u32[]{:S(2)}) async-start(bf16[32,24,256]{2,1,0:T(8,128)(2,1)} %bitcast.16), calls=%async_computation | async-start | bytes 786432 | tf_op jit(solution)/shard_map/all_to_all | solution.py:229
  11.9 2.8 %collective-permute-start = (s32[1,8]{1,0:T(1,128)S(1)}, s32[1,8]{1,0:T(1,128)S(1)}, u32[]{:S(2)}, u32[]{:S(2)}) collective-permute-start(s32[1,8]{1,0:T(1,128)S(1)} %get-tuple-element.21.refs_0_), channel_id=1, source_target_pairs={{0,8},{1,9},{2,10},{3,11},{4,12},{5,13},{6,14},{7,15},{8,0},{9,1},... | collective-permute-start | bytes 104 | tf_op jit(solution)/shard_map/ppermute | solution.py:242
  12.9 4.3 %collective-permute-start.1 = (s32[1,8]{1,0:T(1,128)S(1)}, s32[1,8]{1,0:T(1,128)S(1)}, u32[]{:S(2)}, u32[]{:S(2)}) collective-permute-start(s32[1,8]{1,0:T(1,128)S(1)} %get-tuple-element.21.refs_0_), channel_id=1, source_target_pairs={{0,1},{1,0},{2,3},{3,2},{4,5},{5,4},{6,7},{7,6},{8,9},{9,8},{10,11... | collective-permute-start | bytes 104 | tf_op jit(solution)/shard_map/ppermute | solution.py:242
  14.5 4.2 %collective-permute-start.2 = (s32[1,8]{1,0:T(1,128)S(1)}, s32[1,8]{1,0:T(1,128)S(1)}, u32[]{:S(2)}, u32[]{:S(2)}) collective-permute-start(s32[1,8]{1,0:T(1,128)S(1)} %get-tuple-element.21.refs_0_), channel_id=1, source_target_pairs={{0,9},{1,8},{2,11},{3,10},{4,13},{5,12},{6,15},{7,14},{8,1},{9,0},... | collective-permute-start | bytes 104 | tf_op jit(solution)/shard_map/ppermute | solution.py:242
  22.4 3.0 %collective-permute-start.3 = (bf16[384,128]{1,0:T(8,128)(2,1)S(1)}, bf16[384,128]{1,0:T(8,128)(2,1)S(1)}, u32[]{:S(2)}, u32[]{:S(2)}) collective-permute-start(bf16[384,128]{1,0:T(8,128)(2,1)S(1)} %get-tuple-element.25), channel_id=1, source_target_pairs={{0,8},{1,9},{2,10},{3,11},{4,12},{5,13},{6,14},{7,15},{8,0},{9,1},... | collective-permute-start | bytes 294920 | tf_op jit(solution)/shard_map/ppermute | solution.py:242
  25.4 7.8 %collective-permute-start.4 = (bf16[384,128]{1,0:T(8,128)(2,1)S(1)}, bf16[384,128]{1,0:T(8,128)(2,1)S(1)}, u32[]{:S(2)}, u32[]{:S(2)}) collective-permute-start(bf16[384,128]{1,0:T(8,128)(2,1)S(1)} %get-tuple-element.27), channel_id=1, source_target_pairs={{0,2},{1,3},{2,0},{3,1},{4,6},{5,7},{6,4},{7,5},{8,14},{9,15},{10,... | collective-permute-start | bytes 294920 | tf_op jit(solution)/shard_map/ppermute | solution.py:242
  33.3 4.9 %collective-permute-start.5 = (bf16[384,128]{1,0:T(8,128)(2,1)S(1)}, bf16[384,128]{1,0:T(8,128)(2,1)S(1)}, u32[]{:S(2)}, u32[]{:S(2)}) collective-permute-start(bf16[384,128]{1,0:T(8,128)(2,1)S(1)} %get-tuple-element.29), channel_id=1, source_target_pairs={{0,6},{1,7},{2,4},{3,5},{4,2},{5,3},{6,0},{7,1},{8,10},{9,11},{10,... | collective-permute-start | bytes 294920 | tf_op jit(solution)/shard_map/ppermute | solution.py:242
  38.2 4.3 %collective-permute-start.6 = (bf16[384,128]{1,0:T(8,128)(2,1)S(1)}, bf16[384,128]{1,0:T(8,128)(2,1)S(1)}, u32[]{:S(2)}, u32[]{:S(2)}) collective-permute-start(bf16[384,128]{1,0:T(8,128)(2,1)S(1)} %last_add.1.refs_2_), channel_id=1, source_target_pairs={{0,8},{1,9},{2,10},{3,11},{4,12},{5,13},{6,14},{7,15},{8,0},{9,1},... | collective-permute-start | bytes 294920 | tf_op jit(solution)/shard_map/ppermute | solution.py:242

commit v11 on v9

--- a/solution.py
+++ b/solution.py
@@ -68,7 +68,7 @@
     slot = owner * capacity + position.astype(jnp.int32)
     place = as_bf16(iota((rows, visits), 0) == slot)
     person_hot = as_bf16(iota((persons, visits), 0) == person_ref[...])
-    line = iota((128, visits), 0)
+    line = iota((16, visits), 0)
     facts = jnp.where(line == 0, start, jnp.where(line == 1, finish, jnp.where(line == 2, tile, 0)))
     table = jnp.concatenate([person_hot, facts.astype(F32).astype(BF16)], axis=0)
     placed = matmul_nt(place, table)
@@ -77,14 +77,15 @@
     finish_at = placed[:, persons + 1 : persons + 2]
     tile_at = placed[:, persons + 2 : persons + 3]
     no_slots = jnp.zeros((128 - slots, persons), BF16)
-    weights = matmul_nt(hot, jnp.concatenate([profile_ref[...], no_slots], axis=0))
+    panel = jnp.transpose(panel_ref[...].astype(F32)).astype(BF16)
+    chosen = matmul_nt(hot, jnp.concatenate([profile_ref[...], no_slots, panel], axis=0))
     lane = iota((rows, 128), 1)
     lane_f = lane.astype(F32)
     inside = (lane_f >= start_at) & (lane_f < finish_at)
-    weights = jnp.where(inside, weights, 0.0)
+    weights = jnp.where(inside, chosen[:, :128], 0.0)
     weights = jnp.where(lane == slots, tile_at, weights)
     send_ref[:, :128] = weights.astype(BF16)
-    send_ref[:, 128:] = matmul(hot, panel_ref[...]).astype(BF16)
+    send_ref[:, 128:] = chosen[:, 128:].astype(BF16)
     persons_ref[...] = hot
     table_ref[...] = tile_loc_ref[...]
 
@@ -230,7 +231,7 @@
 
 
 def site_step(step, pop, site):
-    if (step + pop) % 2 == 0:
+    if (step + pop) % 2 == 1:
         return pop, site ^ 2
     return pop, (8 - site if site % 2 else 6 - site) % 8
 

time: 55.1 us -> 54.6 us (level)
  no operation moved by 1% of the time
where the time goes in v11:
time: 54.6 us; the launch traced here: 54.3 us
  starting transfers between devices  24.2 us (44%)
  waiting for transfers between devices  12.9 us (24%)
  blocking collectives  11.3 us (21%)
  Pallas kernels  5.74 us (11%)
    ppermute x7, starting transfers between devices, swap(): return lax.ppermute(array, ('pop', 'site'), pairs)  15 us
    all_to_all x1, blocking collectives, exchange(): lax.all_to_all(blocks, ('pop', 'site'), 0, 0, tiled=True, axis_index_grou...  11.3 us
    ppermute x7, waiting for transfers between devices, swap(): return lax.ppermute(array, ('pop', 'site'), pairs)  9.8 us
    all_to_all x1, starting transfers between devices, exchange(): lax.all_to_all(blocks, ('pop', 'site'), 0, 0, tiled=True, axis_index_grou...  9.22 us
    pallas_call x10, Pallas kernels, call(): pl.pallas_call(kernel, out_shape=tuple((pltpu.VMEM(shape, kind) for shape...  4.93 us
    all_to_all x1, waiting for transfers between devices, exchange(): lax.all_to_all(blocks, ('pop', 'site'), 0, 0, tiled=True, axis_index_grou...  3.12 us
  transfers between devices with their start and end apart: 8, of which 7 were waited for; matrix products, arithmetic and copies ran while one was open for 0% of the time, Pallas kernels for 3%

profile of v11, /device:TPU:1, one launch (start us, length us, event | category | flops | bytes accessed | tf_op | source)
XLA Modules:
  0.0 54.3 jit_solution(11353848563309966636)
XLA Ops:
  0.0 2.4 %pack.1 = (bf16[768,256]{1,0:T(8,128)(2,1)}, bf16[768,128]{1,0:T(8,128)(2,1)S(1)}, s32[1,8]{1,0:T(1,128)S(1)}) custom-call(bf16[96,128]{1,0:T(8,128)(2,1)} %bitcast.16, bf16[128,128]{1,0:T(8,128)(2,1)} %refs_1_.1, s32[1,512]{1,0:T(1,128)} %bitcast.17, s32[1,512]{1,0:T(1,128)} %bitcast.18, s32[1,512]{1,0:T(1,128)} %bitcast.19, s32[1,512]{1,0:T(1,128)} %bitcast.20, ...), custom_call_target="tpu_custom_call" | custom-call | flops 250000000 | bytes 1000000 | tf_op jit(solution)/shard_map/pack/pallas_call | solution.py:188
  2.4 9.2 %all-to-all-start = ((bf16[32,24,256]{2,1,0:T(8,128)(2,1)}), bf16[32,24,256]{2,1,0:T(8,128)(2,1)S(1)}, u32[]{:S(2)}, u32[]{:S(2)}) async-start(bf16[32,24,256]{2,1,0:T(8,128)(2,1)} %bitcast.7), calls=%async_computation | async-start | bytes 786432 | tf_op jit(solution)/shard_map/all_to_all | solution.py:213
  11.7 1.0 %collective-permute-start = (s32[1,8]{1,0:T(1,128)S(1)}, s32[1,8]{1,0:T(1,128)S(1)}, u32[]{:S(2)}, u32[]{:S(2)}) collective-permute-start(s32[1,8]{1,0:T(1,128)S(1)} %get-tuple-element.21.refs_0_), channel_id=1, source_target_pairs={{0,8},{1,9},{2,10},{3,11},{4,12},{5,13},{6,14},{7,15},{8,0},{9,1},... | collective-permute-start | bytes 104 | tf_op jit(solution)/shard_map/ppermute | solution.py:226
  12.7 1.5 %collective-permute-start.1 = (s32[1,8]{1,0:T(1,128)S(1)}, s32[1,8]{1,0:T(1,128)S(1)}, u32[]{:S(2)}, u32[]{:S(2)}) collective-permute-start(s32[1,8]{1,0:T(1,128)S(1)} %get-tuple-element.21.refs_0_), channel_id=1, source_target_pairs={{0,1},{1,0},{2,3},{3,2},{4,5},{5,4},{6,7},{7,6},{8,9},{9,8},{10,11... | collective-permute-start | bytes 104 | tf_op jit(solution)/shard_map/ppermute | solution.py:226
  14.2 0.2 collective-permute-start.2
  14.4 2.5 %collective-permute-done.1.refs_2_ = s32[1,8]{1,0:T(1,128)S(1)} collective-permute-done((s32[1,8]{1,0:T(1,128)S(1)}, s32[1,8]{1,0:T(1,128)S(1)}, u32[]{:S(2)}, u32[]{:S(2)}) %collective-permute-start.1) | collective-permute-done | bytes 64 | tf_op jit(solution)/shard_map/ppermute | solution.py:226
  16.9 1.5 %collective-permute-done.2.refs_3_ = s32[1,8]{1,0:T(1,128)S(1)} collective-permute-done((s32[1,8]{1,0:T(1,128)S(1)}, s32[1,8]{1,0:T(1,128)S(1)}, u32[]{:S(2)}, u32[]{:S(2)}) %collective-permute-start.2) | collective-permute-done | bytes 64 | tf_op jit(solution)/shard_map/ppermute | solution.py:226
  18.4 3.1 %all-to-all-done = bf16[32,24,256]{2,1,0:T(8,128)(2,1)S(1)} async-done(((bf16[32,24,256]{2,1,0:T(8,128)(2,1)}), bf16[32,24,256]{2,1,0:T(8,128)(2,1)S(1)}, u32[]{:S(2)}, u32[]{:S(2)}) %all-to-all-start) | async-done | bytes 393248 | tf_op jit(solution)/shard_map/all_to_all | solution.py:213
  21.6 0.5 %give.1 = (bf16[384,128]{1,0:T(8,128)(2,1)S(1)}, bf16[96,768]{1,0:T(8,128)(2,1)S(1)}, f32[8,768]{1,0:T(8,128)S(1)}) custom-call(s32[1,8]{1,0:T(1,128)S(1)} %get-tuple-element.21.refs_0_, s32[1,8]{1,0:T(1,128)S(1)} %collective-permute-done.refs_1_, s32[1,8]{1,0:T(1,128)S(1)} %collective-permute-done.1.refs_2_, s32[1,8]{1,0:T(1,128)S(1)} %collective-permute-done.2.refs_3_, ...), custom_call_target="tpu_custom_call" | custom-call | flops 250000000 | bytes 1000000 | tf_op jit(solution)/shard_map/give/pallas_call | solution.py:188
  22.1 2.1 %collective-permute-start.3 = (bf16[384,128]{1,0:T(8,128)(2,1)S(1)}, bf16[384,128]{1,0:T(8,128)(2,1)S(1)}, u32[]{:S(2)}, u32[]{:S(2)}) collective-permute-start(bf16[384,128]{1,0:T(8,128)(2,1)S(1)} %get-tuple-element.25), channel_id=1, source_target_pairs={{0,8},{1,9},{2,10},{3,11},{4,12},{5,13},{6,14},{7,15},{8,0},{9,1},... | collective-permute-start | bytes 294920 | tf_op jit(solution)/shard_map/ppermute | solution.py:226
  24.2 0.3 keep.1.own_ref
  24.5 0.6 %collective-permute-done.3.far_ref = bf16[384,128]{1,0:T(8,128)(2,1)S(1)} collective-permute-done((bf16[384,128]{1,0:T(8,128)(2,1)S(1)}, bf16[384,128]{1,0:T(8,128)(2,1)S(1)}, u32[]{:S(2)}, u32[]{:S(2)}) %collective-permute-start.3) | collective-permute-done | bytes 98336 | tf_op jit(solution)/shard_map/ppermute | solution.py:226
  25.2 3.1 %collective-permute-start.4 = (bf16[384,128]{1,0:T(8,128)(2,1)S(1)}, bf16[384,128]{1,0:T(8,128)(2,1)S(1)}, u32[]{:S(2)}, u32[]{:S(2)}) collective-permute-start(bf16[384,128]{1,0:T(8,128)(2,1)S(1)} %get-tuple-element.27), channel_id=1, source_target_pairs={{0,6},{1,7},{2,4},{3,5},{4,2},{5,3},{6,0},{7,1},{8,10},{9,11},{10,... | collective-permute-start | bytes 294920 | tf_op jit(solution)/shard_map/ppermute | solution.py:226
  28.2 0.3 columns.1.refs_0_
  28.5 2.7 %collective-permute-done.4.far_ref = bf16[384,128]{1,0:T(8,128)(2,1)S(1)} collective-permute-done((bf16[384,128]{1,0:T(8,128)(2,1)S(1)}, bf16[384,128]{1,0:T(8,128)(2,1)S(1)}, u32[]{:S(2)}, u32[]{:S(2)}) %collective-permute-start.4) | collective-permute-done | bytes 98336 | tf_op jit(solution)/shard_map/ppermute | solution.py:226
  31.2 3.7 %collective-permute-start.5 = (bf16[384,128]{1,0:T(8,128)(2,1)S(1)}, bf16[384,128]{1,0:T(8,128)(2,1)S(1)}, u32[]{:S(2)}, u32[]{:S(2)}) collective-permute-start(bf16[384,128]{1,0:T(8,128)(2,1)S(1)} %get-tuple-element.29), channel_id=1, source_target_pairs={{0,2},{1,3},{2,0},{3,1},{4,6},{5,7},{6,4},{7,5},{8,14},{9,15},{10,... | collective-permute-start | bytes 294920 | tf_op jit(solution)/shard_map/ppermute | solution.py:226
  34.9 0.1 flip.1.persons_ref
  35.1 2.4 %collective-permute-done.5.far_ref = bf16[384,128]{1,0:T(8,128)(2,1)S(1)} collective-permute-done((bf16[384,128]{1,0:T(8,128)(2,1)S(1)}, bf16[384,128]{1,0:T(8,128)(2,1)S(1)}, u32[]{:S(2)}, u32[]{:S(2)}) %collective-permute-start.5) | collective-permute-done | bytes 98336 | tf_op jit(solution)/shard_map/ppermute | solution.py:226
  37.5 3.4 %collective-permute-start.6 = (bf16[384,128]{1,0:T(8,128)(2,1)S(1)}, bf16[384,128]{1,0:T(8,128)(2,1)S(1)}, u32[]{:S(2)}, u32[]{:S(2)}) collective-permute-start(bf16[384,128]{1,0:T(8,128)(2,1)S(1)} %last_add.1.refs_2_), channel_id=1, source_target_pairs={{0,8},{1,9},{2,10},{3,11},{4,12},{5,13},{6,14},{7,15},{8,0},{9,1},... | collective-permute-start | bytes 294920 | tf_op jit(solution)/shard_map/ppermute | solution.py:226
  40.8 0.8 %own.1 = (f32[768,128]{1,0:T(8,128)S(1)}, bf16[768,512]{1,0:T(8,128)(2,1)S(1)}) custom-call(bf16[768,128]{1,0:T(8,128)(2,1)S(1)} %columns.1.refs_0_, bf16[768,256]{1,0:T(8,128)(2,1)S(1)} %bitcast.15, bf16[384,128]{1,0:T(8,128)(2,1)S(1)} %last_add.1.refs_2_), custom_call_target="tpu_custom_call" | custom-call | flops 300000000 | bytes 1200000 | tf_op jit(solution)/shard_map/own/pallas_call | solution.py:188
  41.6 0.1 collective-permute-done.6.refs_1_
  41.8 0.4 other.1
  42.2 11.3 %all_to_all.10 = bf16[32,24,128]{2,1,0:T(8,128)(2,1)S(1)} all-to-all(bf16[32,24,128]{2,1,0:T(8,128)(2,1)S(1)} %bitcast.12), channel_id=1, replica_groups={{0,1,16,17,32,33,48,49,64,65,80,81,96,97,112,113,128,129,144,145,160,16..., dimensions={0} | all-to-all | bytes 393216 | tf_op jit(solution)/shard_map/all_to_all | solution.py:213
  53.5 0.8 %finish.1 = bf16[128,128]{1,0:T(8,128)(2,1)} custom-call(bf16[128,768]{1,0:T(8,128)(2,1)S(1)} %flip.1.persons_ref, bf16[768,128]{1,0:T(8,128)(2,1)S(1)} %bitcast.11), custom_call_target="tpu_custom_call" | custom-call | tf_op jit(solution)/shard_map/finish/pallas_call | solution.py:312
  (4 shorter events, 0.1 us)
Async XLA Ops:
  2.4 19.1 %all-to-all-start = ((bf16[32,24,256]{2,1,0:T(8,128)(2,1)}), bf16[32,24,256]{2,1,0:T(8,128)(2,1)S(1)}, u32[]{:S(2)}, u32[]{:S(2)}) async-start(bf16[32,24,256]{2,1,0:T(8,128)(2,1)} %bitcast.7), calls=%async_computation | async-start | bytes 786432 | tf_op jit(solution)/shard_map/all_to_all | solution.py:213
  11.7 2.8 %collective-permute-start = (s32[1,8]{1,0:T(1,128)S(1)}, s32[1,8]{1,0:T(1,128)S(1)}, u32[]{:S(2)}, u32[]{:S(2)}) collective-permute-start(s32[1,8]{1,0:T(1,128)S(1)} %get-tuple-element.21.refs_0_), channel_id=1, source_target_pairs={{0,8},{1,9},{2,10},{3,11},{4,12},{5,13},{6,14},{7,15},{8,0},{9,1},... | collective-permute-start | bytes 104 | tf_op jit(solution)/shard_map/ppermute | solution.py:226
  12.7 4.2 %collective-permute-start.1 = (s32[1,8]{1,0:T(1,128)S(1)}, s32[1,8]{1,0:T(1,128)S(1)}, u32[]{:S(2)}, u32[]{:S(2)}) collective-permute-start(s32[1,8]{1,0:T(1,128)S(1)} %get-tuple-element.21.refs_0_), channel_id=1, source_target_pairs={{0,1},{1,0},{2,3},{3,2},{4,5},{5,4},{6,7},{7,6},{8,9},{9,8},{10,11... | collective-permute-start | bytes 104 | tf_op jit(solution)/shard_map/ppermute | solution.py:226
  14.2 4.2 %collective-permute-start.2 = (s32[1,8]{1,0:T(1,128)S(1)}, s32[1,8]{1,0:T(1,128)S(1)}, u32[]{:S(2)}, u32[]{:S(2)}) collective-permute-start(s32[1,8]{1,0:T(1,128)S(1)} %get-tuple-element.21.refs_0_), channel_id=1, source_target_pairs={{0,9},{1,8},{2,11},{3,10},{4,13},{5,12},{6,15},{7,14},{8,1},{9,0},... | collective-permute-start | bytes 104 | tf_op jit(solution)/shard_map/ppermute | solution.py:226
  22.1 3.0 %collective-permute-start.3 = (bf16[384,128]{1,0:T(8,128)(2,1)S(1)}, bf16[384,128]{1,0:T(8,128)(2,1)S(1)}, u32[]{:S(2)}, u32[]{:S(2)}) collective-permute-start(bf16[384,128]{1,0:T(8,128)(2,1)S(1)} %get-tuple-element.25), channel_id=1, source_target_pairs={{0,8},{1,9},{2,10},{3,11},{4,12},{5,13},{6,14},{7,15},{8,0},{9,1},... | collective-permute-start | bytes 294920 | tf_op jit(solution)/shard_map/ppermute | solution.py:226
  25.2 6.0 %collective-permute-start.4 = (bf16[384,128]{1,0:T(8,128)(2,1)S(1)}, bf16[384,128]{1,0:T(8,128)(2,1)S(1)}, u32[]{:S(2)}, u32[]{:S(2)}) collective-permute-start(bf16[384,128]{1,0:T(8,128)(2,1)S(1)} %get-tuple-element.27), channel_id=1, source_target_pairs={{0,6},{1,7},{2,4},{3,5},{4,2},{5,3},{6,0},{7,1},{8,10},{9,11},{10,... | collective-permute-start | bytes 294920 | tf_op jit(solution)/shard_map/ppermute | solution.py:226
  31.2 6.2 %collective-permute-start.5 = (bf16[384,128]{1,0:T(8,128)(2,1)S(1)}, bf16[384,128]{1,0:T(8,128)(2,1)S(1)}, u32[]{:S(2)}, u32[]{:S(2)}) collective-permute-start(bf16[384,128]{1,0:T(8,128)(2,1)S(1)} %get-tuple-element.29), channel_id=1, source_target_pairs={{0,2},{1,3},{2,0},{3,1},{4,6},{5,7},{6,4},{7,5},{8,14},{9,15},{10,... | collective-permute-start | bytes 294920 | tf_op jit(solution)/shard_map/ppermute | solution.py:226
  37.5 4.3 %collective-permute-start.6 = (bf16[384,128]{1,0:T(8,128)(2,1)S(1)}, bf16[384,128]{1,0:T(8,128)(2,1)S(1)}, u32[]{:S(2)}, u32[]{:S(2)}) collective-permute-start(bf16[384,128]{1,0:T(8,128)(2,1)S(1)} %last_add.1.refs_2_), channel_id=1, source_target_pairs={{0,8},{1,9},{2,10},{3,11},{4,12},{5,13},{6,14},{7,15},{8,0},{9,1},... | collective-permute-start | bytes 294920 | tf_op jit(solution)/shard_map/ppermute | solution.py:226

commit v12 on v11

--- a/solution.py
+++ b/solution.py
@@ -231,7 +231,7 @@
 
 
 def site_step(step, pop, site):
-    if (step + pop) % 2 == 1:
+    if (step + pop + site) % 2 == 1:
         return pop, site ^ 2
     return pop, (8 - site if site % 2 else 6 - site) % 8
 

time: 54.6 us -> 54.3 us (level)
  blocking collectives: 11.3 us -> 12.5 us
  starting transfers between devices: 24.2 us -> 23.1 us
    all_to_all x1, blocking collectives: 11.3 us -> 12.5 us  [exchange(): lax.all_to_all(blocks, ('pop', 'site'), 0, 0, tiled=True, axis_index_grou...]
    ppermute x7, starting transfers between devices: 15 us -> 13.9 us  [swap(): return lax.ppermute(array, ('pop', 'site'), pairs)]
where the time goes in v12:
time: 54.3 us; the launch traced here: 54 us
  starting transfers between devices  23.1 us (43%)
  waiting for transfers between devices  12.6 us (23%)
  blocking collectives  12.5 us (23%)
  Pallas kernels  5.75 us (11%)
    ppermute x7, starting transfers between devices, swap(): return lax.ppermute(array, ('pop', 'site'), pairs)  13.9 us
    all_to_all x1, blocking collectives, exchange(): lax.all_to_all(blocks, ('pop', 'site'), 0, 0, tiled=True, axis_index_grou...  12.5 us
    ppermute x7, waiting for transfers between devices, swap(): return lax.ppermute(array, ('pop', 'site'), pairs)  9.45 us
    all_to_all x1, starting transfers between devices, exchange(): lax.all_to_all(blocks, ('pop', 'site'), 0, 0, tiled=True, axis_index_grou...  9.22 us
    pallas_call x10, Pallas kernels, call(): pl.pallas_call(kernel, out_shape=tuple((pltpu.VMEM(shape, kind) for shape...  4.93 us
    all_to_all x1, waiting for transfers between devices, exchange(): lax.all_to_all(blocks, ('pop', 'site'), 0, 0, tiled=True, axis_index_grou...  3.12 us
  transfers between devices with their start and end apart: 8, of which 7 were waited for; matrix products, arithmetic and copies ran while one was open for 0% of the time, Pallas kernels for 3%

profile of v12, /device:TPU:1, one launch (start us, length us, event | category | flops | bytes accessed | tf_op | source)
XLA Modules:
  0.0 54.0 jit_solution(3048427132643294205)
XLA Ops:
  0.0 2.4 %pack.1 = (bf16[768,256]{1,0:T(8,128)(2,1)}, bf16[768,128]{1,0:T(8,128)(2,1)S(1)}, s32[1,8]{1,0:T(1,128)S(1)}) custom-call(bf16[96,128]{1,0:T(8,128)(2,1)} %bitcast.16, bf16[128,128]{1,0:T(8,128)(2,1)} %refs_1_.1, s32[1,512]{1,0:T(1,128)} %bitcast.17, s32[1,512]{1,0:T(1,128)} %bitcast.18, s32[1,512]{1,0:T(1,128)} %bitcast.19, s32[1,512]{1,0:T(1,128)} %bitcast.20, ...), custom_call_target="tpu_custom_call" | custom-call | flops 250000000 | bytes 1000000 | tf_op jit(solution)/shard_map/pack/pallas_call | solution.py:188
  2.4 9.2 %all-to-all-start = ((bf16[32,24,256]{2,1,0:T(8,128)(2,1)}), bf16[32,24,256]{2,1,0:T(8,128)(2,1)S(1)}, u32[]{:S(2)}, u32[]{:S(2)}) async-start(bf16[32,24,256]{2,1,0:T(8,128)(2,1)} %bitcast.7), calls=%async_computation | async-start | bytes 786432 | tf_op jit(solution)/shard_map/all_to_all | solution.py:213
  11.7 1.0 %collective-permute-start = (s32[1,8]{1,0:T(1,128)S(1)}, s32[1,8]{1,0:T(1,128)S(1)}, u32[]{:S(2)}, u32[]{:S(2)}) collective-permute-start(s32[1,8]{1,0:T(1,128)S(1)} %get-tuple-element.21.refs_0_), channel_id=1, source_target_pairs={{0,8},{1,9},{2,10},{3,11},{4,12},{5,13},{6,14},{7,15},{8,0},{9,1},... | collective-permute-start | bytes 104 | tf_op jit(solution)/shard_map/ppermute | solution.py:226
  12.7 1.5 %collective-permute-start.1 = (s32[1,8]{1,0:T(1,128)S(1)}, s32[1,8]{1,0:T(1,128)S(1)}, u32[]{:S(2)}, u32[]{:S(2)}) collective-permute-start(s32[1,8]{1,0:T(1,128)S(1)} %get-tuple-element.21.refs_0_), channel_id=1, source_target_pairs={{0,1},{1,0},{2,3},{3,2},{4,5},{5,4},{6,7},{7,6},{8,9},{9,8},{10,11... | collective-permute-start | bytes 104 | tf_op jit(solution)/shard_map/ppermute | solution.py:226
  14.2 0.2 collective-permute-start.2
  14.4 2.5 %collective-permute-done.1.refs_2_ = s32[1,8]{1,0:T(1,128)S(1)} collective-permute-done((s32[1,8]{1,0:T(1,128)S(1)}, s32[1,8]{1,0:T(1,128)S(1)}, u32[]{:S(2)}, u32[]{:S(2)}) %collective-permute-start.1) | collective-permute-done | bytes 64 | tf_op jit(solution)/shard_map/ppermute | solution.py:226
  16.9 1.5 %collective-permute-done.2.refs_3_ = s32[1,8]{1,0:T(1,128)S(1)} collective-permute-done((s32[1,8]{1,0:T(1,128)S(1)}, s32[1,8]{1,0:T(1,128)S(1)}, u32[]{:S(2)}, u32[]{:S(2)}) %collective-permute-start.2) | collective-permute-done | bytes 64 | tf_op jit(solution)/shard_map/ppermute | solution.py:226
  18.4 3.1 %all-to-all-done = bf16[32,24,256]{2,1,0:T(8,128)(2,1)S(1)} async-done(((bf16[32,24,256]{2,1,0:T(8,128)(2,1)}), bf16[32,24,256]{2,1,0:T(8,128)(2,1)S(1)}, u32[]{:S(2)}, u32[]{:S(2)}) %all-to-all-start) | async-done | bytes 393248 | tf_op jit(solution)/shard_map/all_to_all | solution.py:213
  21.6 0.5 %give.1 = (bf16[384,128]{1,0:T(8,128)(2,1)S(1)}, bf16[96,768]{1,0:T(8,128)(2,1)S(1)}, f32[8,768]{1,0:T(8,128)S(1)}) custom-call(s32[1,8]{1,0:T(1,128)S(1)} %get-tuple-element.21.refs_0_, s32[1,8]{1,0:T(1,128)S(1)} %collective-permute-done.refs_1_, s32[1,8]{1,0:T(1,128)S(1)} %collective-permute-done.1.refs_2_, s32[1,8]{1,0:T(1,128)S(1)} %collective-permute-done.2.refs_3_, ...), custom_call_target="tpu_custom_call" | custom-call | flops 250000000 | bytes 1000000 | tf_op jit(solution)/shard_map/give/pallas_call | solution.py:188
  22.1 2.1 %collective-permute-start.3 = (bf16[384,128]{1,0:T(8,128)(2,1)S(1)}, bf16[384,128]{1,0:T(8,128)(2,1)S(1)}, u32[]{:S(2)}, u32[]{:S(2)}) collective-permute-start(bf16[384,128]{1,0:T(8,128)(2,1)S(1)} %get-tuple-element.25), channel_id=1, source_target_pairs={{0,8},{1,9},{2,10},{3,11},{4,12},{5,13},{6,14},{7,15},{8,0},{9,1},... | collective-permute-start | bytes 294920 | tf_op jit(solution)/shard_map/ppermute | solution.py:226
  24.2 0.3 keep.1.own_ref
  24.5 0.6 %collective-permute-done.3.far_ref = bf16[384,128]{1,0:T(8,128)(2,1)S(1)} collective-permute-done((bf16[384,128]{1,0:T(8,128)(2,1)S(1)}, bf16[384,128]{1,0:T(8,128)(2,1)S(1)}, u32[]{:S(2)}, u32[]{:S(2)}) %collective-permute-start.3) | collective-permute-done | bytes 98336 | tf_op jit(solution)/shard_map/ppermute | solution.py:226
  25.2 3.1 %collective-permute-start.4 = (bf16[384,128]{1,0:T(8,128)(2,1)S(1)}, bf16[384,128]{1,0:T(8,128)(2,1)S(1)}, u32[]{:S(2)}, u32[]{:S(2)}) collective-permute-start(bf16[384,128]{1,0:T(8,128)(2,1)S(1)} %get-tuple-element.27), channel_id=1, source_target_pairs={{0,6},{1,3},{2,4},{3,1},{4,2},{5,7},{6,0},{7,5},{8,10},{9,15},{10,... | collective-permute-start | bytes 294920 | tf_op jit(solution)/shard_map/ppermute | solution.py:226
  28.2 0.3 columns.1.refs_0_
  28.5 2.8 %collective-permute-done.4.far_ref = bf16[384,128]{1,0:T(8,128)(2,1)S(1)} collective-permute-done((bf16[384,128]{1,0:T(8,128)(2,1)S(1)}, bf16[384,128]{1,0:T(8,128)(2,1)S(1)}, u32[]{:S(2)}, u32[]{:S(2)}) %collective-permute-start.4) | collective-permute-done | bytes 98336 | tf_op jit(solution)/shard_map/ppermute | solution.py:226
  31.3 3.6 %collective-permute-start.5 = (bf16[384,128]{1,0:T(8,128)(2,1)S(1)}, bf16[384,128]{1,0:T(8,128)(2,1)S(1)}, u32[]{:S(2)}, u32[]{:S(2)}) collective-permute-start(bf16[384,128]{1,0:T(8,128)(2,1)S(1)} %get-tuple-element.29), channel_id=1, source_target_pairs={{0,2},{1,7},{2,0},{3,5},{4,6},{5,3},{6,4},{7,1},{8,14},{9,11},{10,... | collective-permute-start | bytes 294920 | tf_op jit(solution)/shard_map/ppermute | solution.py:226
  35.0 0.1 flip.1.persons_ref
  35.1 1.9 %collective-permute-done.5.far_ref = bf16[384,128]{1,0:T(8,128)(2,1)S(1)} collective-permute-done((bf16[384,128]{1,0:T(8,128)(2,1)S(1)}, bf16[384,128]{1,0:T(8,128)(2,1)S(1)}, u32[]{:S(2)}, u32[]{:S(2)}) %collective-permute-start.5) | collective-permute-done | bytes 98336 | tf_op jit(solution)/shard_map/ppermute | solution.py:226
  37.0 2.3 %collective-permute-start.6 = (bf16[384,128]{1,0:T(8,128)(2,1)S(1)}, bf16[384,128]{1,0:T(8,128)(2,1)S(1)}, u32[]{:S(2)}, u32[]{:S(2)}) collective-permute-start(bf16[384,128]{1,0:T(8,128)(2,1)S(1)} %last_add.1.refs_2_), channel_id=1, source_target_pairs={{0,8},{1,9},{2,10},{3,11},{4,12},{5,13},{6,14},{7,15},{8,0},{9,1},... | collective-permute-start | bytes 294920 | tf_op jit(solution)/shard_map/ppermute | solution.py:226
  39.4 0.8 %own.1 = (f32[768,128]{1,0:T(8,128)S(1)}, bf16[768,512]{1,0:T(8,128)(2,1)S(1)}) custom-call(bf16[768,128]{1,0:T(8,128)(2,1)S(1)} %columns.1.refs_0_, bf16[768,256]{1,0:T(8,128)(2,1)S(1)} %bitcast.15, bf16[384,128]{1,0:T(8,128)(2,1)S(1)} %last_add.1.refs_2_), custom_call_target="tpu_custom_call" | custom-call | flops 300000000 | bytes 1200000 | tf_op jit(solution)/shard_map/own/pallas_call | solution.py:188
  40.2 0.1 collective-permute-done.6.refs_1_
  40.3 0.4 other.1
  40.7 12.5 %all_to_all.10 = bf16[32,24,128]{2,1,0:T(8,128)(2,1)S(1)} all-to-all(bf16[32,24,128]{2,1,0:T(8,128)(2,1)S(1)} %bitcast.12), channel_id=1, replica_groups={{0,1,16,17,32,33,48,49,64,65,80,81,96,97,112,113,128,129,144,145,160,16..., dimensions={0} | all-to-all | bytes 393216 | tf_op jit(solution)/shard_map/all_to_all | solution.py:213
  53.2 0.8 %finish.1 = bf16[128,128]{1,0:T(8,128)(2,1)} custom-call(bf16[128,768]{1,0:T(8,128)(2,1)S(1)} %flip.1.persons_ref, bf16[768,128]{1,0:T(8,128)(2,1)S(1)} %bitcast.11), custom_call_target="tpu_custom_call" | custom-call | tf_op jit(solution)/shard_map/finish/pallas_call | solution.py:312
  (4 shorter events, 0.1 us)
Async XLA Ops:
  2.4 19.1 %all-to-all-start = ((bf16[32,24,256]{2,1,0:T(8,128)(2,1)}), bf16[32,24,256]{2,1,0:T(8,128)(2,1)S(1)}, u32[]{:S(2)}, u32[]{:S(2)}) async-start(bf16[32,24,256]{2,1,0:T(8,128)(2,1)} %bitcast.7), calls=%async_computation | async-start | bytes 786432 | tf_op jit(solution)/shard_map/all_to_all | solution.py:213
  11.7 2.8 %collective-permute-start = (s32[1,8]{1,0:T(1,128)S(1)}, s32[1,8]{1,0:T(1,128)S(1)}, u32[]{:S(2)}, u32[]{:S(2)}) collective-permute-start(s32[1,8]{1,0:T(1,128)S(1)} %get-tuple-element.21.refs_0_), channel_id=1, source_target_pairs={{0,8},{1,9},{2,10},{3,11},{4,12},{5,13},{6,14},{7,15},{8,0},{9,1},... | collective-permute-start | bytes 104 | tf_op jit(solution)/shard_map/ppermute | solution.py:226
  12.7 4.2 %collective-permute-start.1 = (s32[1,8]{1,0:T(1,128)S(1)}, s32[1,8]{1,0:T(1,128)S(1)}, u32[]{:S(2)}, u32[]{:S(2)}) collective-permute-start(s32[1,8]{1,0:T(1,128)S(1)} %get-tuple-element.21.refs_0_), channel_id=1, source_target_pairs={{0,1},{1,0},{2,3},{3,2},{4,5},{5,4},{6,7},{7,6},{8,9},{9,8},{10,11... | collective-permute-start | bytes 104 | tf_op jit(solution)/shard_map/ppermute | solution.py:226
  14.2 4.2 %collective-permute-start.2 = (s32[1,8]{1,0:T(1,128)S(1)}, s32[1,8]{1,0:T(1,128)S(1)}, u32[]{:S(2)}, u32[]{:S(2)}) collective-permute-start(s32[1,8]{1,0:T(1,128)S(1)} %get-tuple-element.21.refs_0_), channel_id=1, source_target_pairs={{0,9},{1,8},{2,11},{3,10},{4,13},{5,12},{6,15},{7,14},{8,1},{9,0},... | collective-permute-start | bytes 104 | tf_op jit(solution)/shard_map/ppermute | solution.py:226
  22.1 3.0 %collective-permute-start.3 = (bf16[384,128]{1,0:T(8,128)(2,1)S(1)}, bf16[384,128]{1,0:T(8,128)(2,1)S(1)}, u32[]{:S(2)}, u32[]{:S(2)}) collective-permute-start(bf16[384,128]{1,0:T(8,128)(2,1)S(1)} %get-tuple-element.25), channel_id=1, source_target_pairs={{0,8},{1,9},{2,10},{3,11},{4,12},{5,13},{6,14},{7,15},{8,0},{9,1},... | collective-permute-start | bytes 294920 | tf_op jit(solution)/shard_map/ppermute | solution.py:226
  25.2 6.1 %collective-permute-start.4 = (bf16[384,128]{1,0:T(8,128)(2,1)S(1)}, bf16[384,128]{1,0:T(8,128)(2,1)S(1)}, u32[]{:S(2)}, u32[]{:S(2)}) collective-permute-start(bf16[384,128]{1,0:T(8,128)(2,1)S(1)} %get-tuple-element.27), channel_id=1, source_target_pairs={{0,6},{1,3},{2,4},{3,1},{4,2},{5,7},{6,0},{7,5},{8,10},{9,15},{10,... | collective-permute-start | bytes 294920 | tf_op jit(solution)/shard_map/ppermute | solution.py:226
  31.3 5.7 %collective-permute-start.5 = (bf16[384,128]{1,0:T(8,128)(2,1)S(1)}, bf16[384,128]{1,0:T(8,128)(2,1)S(1)}, u32[]{:S(2)}, u32[]{:S(2)}) collective-permute-start(bf16[384,128]{1,0:T(8,128)(2,1)S(1)} %get-tuple-element.29), channel_id=1, source_target_pairs={{0,2},{1,7},{2,0},{3,5},{4,6},{5,3},{6,4},{7,1},{8,14},{9,11},{10,... | collective-permute-start | bytes 294920 | tf_op jit(solution)/shard_map/ppermute | solution.py:226
  37.0 3.3 %collective-permute-start.6 = (bf16[384,128]{1,0:T(8,128)(2,1)S(1)}, bf16[384,128]{1,0:T(8,128)(2,1)S(1)}, u32[]{:S(2)}, u32[]{:S(2)}) collective-permute-start(bf16[384,128]{1,0:T(8,128)(2,1)S(1)} %last_add.1.refs_2_), channel_id=1, source_target_pairs={{0,8},{1,9},{2,10},{3,11},{4,12},{5,13},{6,14},{7,15},{8,0},{9,1},... | collective-permute-start | bytes 294920 | tf_op jit(solution)/shard_map/ppermute | solution.py:226
